TPU v7x, 512 devices: a whole 4x8x8 slice. The times are simulated.
512 devices in a mesh: dp: 32 (over x_lo, y, core), tensor: 16 (over x_hi, z).
Axes of the slice: x: 4 (x_hi: 2, x_lo: 2; x = x_hi * 2 + x_lo), y: 8, z: 8, core: 2. Of those that a mesh axis runs over, the one named last changes fastest.
Arguments:
- tokens: bfloat16 [8192, 4096], P(('dp', 'tensor')), may hold values from -110 to 110
- norm_gain: bfloat16 [4096], replicated, may hold values from 0.099609375 to 1.8984375
- query_weight: bfloat16 [4096, 4096], P('dp', 'tensor'), may hold values from -1 to 1
- kv_weight: bfloat16 [4096, 1024], P('dp', 'tensor'), may hold values from -1 to 1
- out_weight: bfloat16 [4096, 4096], P('tensor', 'dp'), may hold values from -0.09375 to 0.09375
- grad_out: bfloat16 [8192, 4096], P(('dp', 'tensor')), may hold values from -6 to 6
- doc_lengths: int32 [32, 4], P('dp'), may hold values from 1 to 128, 256 in all within a row
Outputs:
- input_grad: bfloat16 [8192, 4096], P(('dp', 'tensor'))
- query_weight_grad: float32 [4096, 4096], P('dp', 'tensor')
- kv_weight_grad: float32 [4096, 1024], P('dp', 'tensor')
Inputs may be any that keep to these rules, and one draw needn't show every extreme that they name: `doc_lengths`: each row sums to 256.
All inputs are finite; a program needn't handle non-finite values.
Results may differ from a plain program's by a relative error of at most 0.025.
Values may be sent and summed in bfloat16 or wider, within the bound.
A program may use at most 64 MiB of HBM per device.

v0:
```python
import math

import jax
import jax.numpy as jnp
from jax import lax
from jax.sharding import PartitionSpec as P

KVH = 4
HD = 128


epsilon = 1e-05


def partner_2(value, axis, bit):
    mask = 2**bit
    pairs = [(source, source ^ mask) for source in range(lax.axis_size(axis))]
    return lax.ppermute(value, axis, pairs)


def document_mask(lengths, length_total):
    ends = jnp.cumsum(lengths)
    positions = jnp.arange(length_total, dtype=jnp.int32)
    labels = jnp.sum((ends[None, :] <= positions[:, None]).astype(jnp.int32), axis=1)
    return (labels[:, None] == labels[None, :]) & (positions[None, :] <= positions[:, None])


def local(tokens, norm_gain, query_weight, kv_weight, out_weight, grad_out, doc_lengths):
    tensor_size = lax.axis_size("tensor")
    data_size = lax.axis_size("dp")
    tensor_index = lax.axis_index("tensor")
    sharers = tensor_size // KVH
    levels = sharers.bit_length() - 1
    contract_last = (((1,), (1,)), ((), ()))
    values32 = tokens.astype(jnp.float32)
    root_mean = jnp.sqrt(jnp.mean(values32 * values32, axis=-1) + epsilon)
    unit = values32 / root_mean[:, None]
    gain32 = norm_gain.astype(jnp.float32)
    normed_local = (unit * gain32).astype(jnp.bfloat16)
    normed = lax.all_gather(normed_local, "tensor", axis=0, tiled=True)
    seq_length = normed.shape[0]
    query_full = lax.all_gather(query_weight, "dp", axis=0, tiled=True)
    queries = jnp.dot(normed, query_full, preferred_element_type=jnp.float32).astype(jnp.bfloat16)
    kv_local = lax.all_gather(kv_weight, "dp", axis=0, tiled=True)
    head_weight = kv_local
    for bit_index in range(levels):
        partner = partner_2(head_weight, "tensor", bit_index)
        joined_upper_half = tensor_index >> bit_index & 1 == 1
        head_weight = jnp.concatenate(
            [
                jnp.where(joined_upper_half, partner, head_weight),
                jnp.where(joined_upper_half, head_weight, partner),
            ],
            axis=1,
        )
    keyvals = jnp.dot(normed, head_weight, preferred_element_type=jnp.float32).astype(jnp.bfloat16)
    key_rows = keyvals[:, :HD]
    value_rows = keyvals[:, HD:]
    grad_full = lax.all_gather(grad_out, "tensor", axis=0, tiled=True)
    out_grad = lax.dot_general(
        grad_full,
        lax.all_gather(out_weight, "dp", axis=1, tiled=True),
        contract_last,
        preferred_element_type=jnp.float32,
    ).astype(jnp.bfloat16)
    local_heads = queries.shape[1] // HD
    query_heads = queries.reshape(seq_length, local_heads, HD)
    out_heads = out_grad.reshape(seq_length, local_heads, HD)
    allowed = document_mask(doc_lengths[0], seq_length)
    scores = jnp.einsum(
        "qhd,td->hqt", query_heads, key_rows, preferred_element_type=jnp.float32
    ) / math.sqrt(HD)
    scores = jnp.where(allowed[None, :, :], scores, -1e30)
    peak = jnp.max(scores, axis=-1, keepdims=True)
    expo = jnp.exp(scores - peak)
    probs = expo / jnp.sum(expo, axis=-1, keepdims=True)
    probs_low = probs.astype(jnp.bfloat16)
    prob_grad = jnp.einsum("qhd,td->hqt", out_heads, value_rows, preferred_element_type=jnp.float32)
    inner = jnp.sum(probs * prob_grad, axis=-1, keepdims=True)
    score_grad = (probs * (prob_grad - inner) / math.sqrt(HD)).astype(jnp.bfloat16)
    query_grad = jnp.einsum("hqt,td->qhd", score_grad, key_rows, preferred_element_type=jnp.float32)
    query_grad = query_grad.astype(jnp.bfloat16).reshape(seq_length, local_heads * HD)
    key_part = jnp.einsum(
        "hqt,qhd->td", score_grad, query_heads, preferred_element_type=jnp.float32
    )
    value_part = jnp.einsum("hqt,qhd->td", probs_low, out_heads, preferred_element_type=jnp.float32)
    kv_partial = jnp.concatenate([key_part, value_part], axis=1)
    for bit_index in reversed(range(levels)):
        half_cols = kv_partial.shape[1] // 2
        upper_half = tensor_index >> bit_index & 1 == 1
        lower_cols = kv_partial[:, :half_cols]
        higher_cols = kv_partial[:, half_cols:]
        kept = jnp.where(upper_half, higher_cols, lower_cols)
        handed = jnp.where(upper_half, lower_cols, higher_cols)
        kv_partial = kept + partner_2(handed.astype(jnp.bfloat16), "tensor", bit_index).astype(
            handed.dtype
        )
    kv_grad = kv_partial.astype(jnp.bfloat16)
    from_query = lax.dot_general(
        query_grad, query_full, contract_last, preferred_element_type=jnp.float32
    )
    from_kv = lax.dot_general(kv_grad, kv_local, contract_last, preferred_element_type=jnp.float32)
    normed_grad = lax.psum_scatter(
        (from_query + from_kv).astype(jnp.bfloat16), "tensor", scatter_dimension=0, tiled=True
    ).astype(jnp.float32)
    scaled = normed_grad * gain32
    correction = unit * jnp.mean(scaled * unit, axis=-1, keepdims=True)
    input_grad = (grad_out.astype(jnp.float32) + (scaled - correction) / root_mean[:, None]).astype(
        jnp.bfloat16
    )
    combined = jnp.concatenate([query_grad, kv_grad], axis=1)
    weight_grads = (
        lax.psum_scatter(
            lax.dot_general(
                normed, combined, (((0,), (0,)), ((), ())), preferred_element_type=jnp.float32
            ).astype(jnp.bfloat16),
            "dp",
            scatter_dimension=0,
            tiled=True,
        ).astype(jnp.float32)
        / data_size
    )
    query_width = query_weight.shape[1]
    return (input_grad, weight_grads[:, :query_width], weight_grads[:, query_width:])


def solution(mesh):
    placed = (
        P(("dp", "tensor"), None),
        P(),
        P("dp", "tensor"),
        P("dp", "tensor"),
        P("tensor", "dp"),
        P(("dp", "tensor"), None),
        P("dp", None),
    )
    return jax.shard_map(
        local,
        mesh=mesh,
        in_specs=placed,
        out_specs=(P(("dp", "tensor"), None), P("dp", "tensor"), P("dp", "tensor")),
        check_vma=False,
    )
```

profile of v0, /device:TPU:1, one launch (start us, length us, event | category | flops | bytes accessed | tf_op | source)
XLA Modules:
  0.0 716.6 jit_solution(1927866429500999006)
XLA Ops:
  9.0 1.7 multiply_convert_fusion
  12.2 38.8 %all_gather.16 = bf16[4096,64]{0,1:T(8,128)(2,1)S(1)} all-gather(bf16[128,64]{0,1:T(8,128)(2,1)} %param.10), channel_id=1, replica_groups=mesh['dp'=32,'tensor'=16] {'dp'}, dimensions={0}, use_global_device_ids=true | all-gather | bytes 540672 | tf_op jit(solution)/shard_map/all_gather | solution.py:44
  51.0 2.9 collective-permute-start
  54.0 13.4 %collective-permute-done = bf16[4096,64]{0,1:T(8,128)(2,1)S(1)} collective-permute-done((bf16[4096,64]{0,1:T(8,128)(2,1)S(1)}, bf16[4096,64]{0,1:T(8,128)(2,1)S(1)}, u32[]{:S(2)}, u32[]{:S(2)}) %collective-permute-start) | collective-permute-done | bytes 524320 | tf_op jit(solution)/shard_map/ppermute | solution.py:18
  68.7 4.8 collective-permute-start.1
  73.9 55.1 %collective-permute-done.1 = bf16[4096,128]{0,1:T(8,128)(2,1)S(1)} collective-permute-done((bf16[4096,128]{0,1:T(8,128)(2,1)}, bf16[4096,128]{0,1:T(8,128)(2,1)S(1)}, u32[]{:S(2)}, u32[]{:S(2)}) %collective-permute-start.1) | collective-permute-done | bytes 1048608 | tf_op jit(solution)/shard_map/ppermute | solution.py:18
  129.0 1.8 broadcast_select_fusion.1
  130.9 2.9 fusion.15
  133.8 82.1 %all-gather.9.cloned.1.call-done = bf16[256,4096]{1,0:T(8,128)(2,1)} async-done(((bf16[16,4096]{1,0:T(8,128)(2,1)}), bf16[256,4096]{1,0:T(8,128)(2,1)}) %all-gather.9.cloned.1.call-update) | async-done | bytes 2097168 | tf_op jit(solution)/shard_map/all_gather | solution.py:59
  215.9 70.7 %all-gather.11.cloned.1.call-done = bf16[256,4096]{1,0:T(8,128)(2,1)} async-done(((bf16[256,128]{1,0:T(8,128)(2,1)}), bf16[256,4096]{1,0:T(8,128)(2,1)}) %all-gather.11.cloned.1.call-update) | async-done | bytes 2097168 | tf_op jit(solution)/shard_map/all_gather | solution.py:62
  286.6 3.0 convolution_convert_fusion.2
  289.8 64.7 %all-gather.7.cloned.1.call-done = bf16[4096,256]{1,0:T(8,128)(2,1)} async-done(((bf16[128,256]{1,0:T(8,128)(2,1)}), bf16[4096,256]{1,0:T(8,128)(2,1)}) %all-gather.7.cloned.1.call-update) | async-done | bytes 2097168 | tf_op jit(solution)/shard_map/all_gather | solution.py:42
  354.5 2.5 convolution_convert_fusion.3
  357.0 1.2 fusion.39
  359.9 4.5 collective-permute-start.2
  364.4 1.5 convolution_convert_fusion.1
  367.6 4.3 collective-permute-start.3
  373.2 2.1 fusion.2
  375.4 2.4 convolution_convert_fusion
  377.8 2.8 copy.38
  380.6 202.0 %reduce-scatter.5.cloned.1.call-done = bf16[16,4096]{1,0:T(8,128)(2,1)} async-done(((bf16[256,4096]{1,0:T(8,128)(2,1)}), bf16[16,4096]{1,0:T(8,128)(2,1)}) %reduce-scatter.5.cloned.1.call-update) | async-done | bytes 131088 | tf_op jit(solution)/shard_map/reduce_scatter | solution.py:103
  582.6 1.1 multiply_reduce_fusion.1
  583.7 1.7 add_convert_fusion
  585.4 121.9 %reduce-scatter.7.cloned.1.call-done = bf16[128,320]{1,0:T(8,128)(2,1)} async-done(((bf16[4096,320]{1,0:T(8,128)(2,1)}), bf16[128,320]{1,0:T(8,128)(2,1)}) %reduce-scatter.7.cloned.1.call-update) | async-done | bytes 81936
  (56 shorter events, 12.4 us)
Async XLA Ops:
  7.2 123.7 %all-gather.5.cloned.1.call-start = ((), (), s32[]{:S(2)}) async-start(), calls=%async_computation.2 | async-start | bytes 2228224 | tf_op jit(solution)/shard_map/all_gather | solution.py:40
  8.3 0.7 copy-start.5
  10.7 205.2 %all-gather.9.cloned.1.call-start = ((), (), s32[]{:S(2)}) async-start(), calls=%async_computation.4 | async-start | bytes 2228224 | tf_op jit(solution)/shard_map/all_gather | solution.py:59
  11.4 275.2 %all-gather.11.cloned.1.call-start = ((), (), s32[]{:S(2)}) async-start(), calls=%async_computation.5 | async-start | bytes 2162688 | tf_op jit(solution)/shard_map/all_gather | solution.py:62
  12.2 342.3 %all-gather.7.cloned.1.call-start = ((), (), s32[]{:S(2)}) async-start(), calls=%async_computation.3 | async-start | bytes 2162688 | tf_op jit(solution)/shard_map/all_gather | solution.py:42
  51.0 16.5 %collective-permute-start = (bf16[4096,64]{0,1:T(8,128)(2,1)S(1)}, bf16[4096,64]{0,1:T(8,128)(2,1)S(1)}, u32[]{:S(2)}, u32[]{:S(2)}) collective-permute-start(bf16[4096,64]{0,1:T(8,128)(2,1)S(1)} %all_gather.16), channel_id=1, source_target_pairs={{0,1},{1,0},{2,3},{3,2},{4,5},{5,4},{6,7},{7,6},{8,9},{9,8},{10,11... | collective-permute-start | bytes 1572872 | tf_op jit(solution)/shard_map/ppermute | solution.py:18
  54.0 528.6 %reduce-scatter.5.cloned.1.call-start = ((), (), s32[]{:S(2)}) async-start(), calls=%async_computation.6 | async-start | bytes 2228224 | tf_op jit(solution)/shard_map/reduce_scatter | solution.py:103
  54.0 19.5 %copy-start.7 = (s32[1,4]{1,0:T(1,128)S(1)}, s32[1,4]{1,0:T(1,128)}, u32[]{:S(2)}) copy-start(s32[1,4]{1,0:T(1,128)} %param.13) | copy-start | bytes 52
  68.7 60.4 %collective-permute-start.1 = (bf16[4096,128]{0,1:T(8,128)(2,1)}, bf16[4096,128]{0,1:T(8,128)(2,1)S(1)}, u32[]{:S(2)}, u32[]{:S(2)}) collective-permute-start(bf16[4096,128]{0,1:T(8,128)(2,1)} %pad_maximum_fusion), channel_id=1, source_target_pairs={{0,2},{1,3},{2,0},{3,1},{4,6},{5,7},{6,4},{7,5},{8,10},{9,11},{10,... | collective-permute-start | bytes 3145736 | tf_op jit(solution)/shard_map/ppermute | solution.py:18
  133.8 155.8 %copy-start.4 = (bf16[256,256]{1,0:T(8,128)(2,1)}, bf16[256,256]{1,0:T(8,128)(2,1)S(1)}, u32[]{:S(2)}) copy-start(bf16[256,256]{1,0:T(8,128)(2,1)S(1)} %fusion.15) | copy-start | bytes 393220
  133.8 220.7 %copy-start.1 = (bf16[256,4096]{1,0:T(8,128)(2,1)S(1)}, bf16[256,4096]{1,0:T(8,128)(2,1)}, u32[]{:S(2)}) copy-start(bf16[256,4096]{1,0:T(8,128)(2,1)} %all-gather.5.cloned.1.call-done) | copy-start | bytes 6291460
  358.2 0.8 copy-start.8
  358.2 0.8 copy-start.9
  359.9 12.0 %copy-start = (bf16[4096,256]{1,0:T(8,128)(2,1)S(1)}, bf16[4096,256]{1,0:T(8,128)(2,1)}, u32[]{:S(2)}) copy-start(bf16[4096,256]{1,0:T(8,128)(2,1)} %all-gather.7.cloned.1.call-done) | copy-start | bytes 6291460
  359.9 6.8 collective-permute-start.2
  367.6 5.6 collective-permute-start.3
  375.3 332.0 %reduce-scatter.7.cloned.1.call-start = ((), (), s32[]{:S(2)}) async-start(), calls=%async_computation.7 | async-start | bytes 3244032
  380.6 202.0 %copy-start.2 = (bf16[16,4096]{1,0:T(8,128)(2,1)S(1)}, bf16[16,4096]{1,0:T(8,128)(2,1)}, u32[]{:S(2)}) copy-start(bf16[16,4096]{1,0:T(8,128)(2,1)} %param.7) | copy-start | bytes 393220
  380.6 202.0 %copy-start.6 = (f32[16]{0:T(128)S(1)}, f32[16]{0:T(128)}, u32[]{:S(2)}) copy-start(f32[16]{0:T(128)} %copy-done.5) | copy-start | bytes 196
  380.6 203.1 %copy-start.3 = (bf16[16,4096]{1,0:T(8,128)(2,1)S(1)}, bf16[16,4096]{1,0:T(8,128)(2,1)}, u32[]{:S(2)}) copy-start(bf16[16,4096]{1,0:T(8,128)(2,1)} %param.12) | copy-start | bytes 393220
Sparse Core Ops, SparseCore 0:
  11.7 108.7 all-gather.4
  123.7 92.1 all-gather.8
  218.0 68.5 all-gather.10
  288.6 65.8 all-gather.6
  375.4 207.0 reduce-scatter.4
  585.3 122.0 reduce-scatter.6
where the time goes:
time: 719 us; the launch traced here: 717 us
  waiting for transfers between devices  613 us (85%)
  blocking collectives  38.8 us (5%)
  matrix products  17.7 us (2%)
  starting transfers between devices  16.7 us (2%)
  between operations  14.3 us (2%)
  other arithmetic  10.6 us (1%)
    reduce_scatter x1, waiting for transfers between devices, local(): lax.psum_scatter((from_query + from_kv).astype(jnp.bfloat16), 'tensor', s...  202 us
    unnamed x7, waiting for transfers between devices  123 us
    all_gather x1, waiting for transfers between devices, local(): grad_full = lax.all_gather(grad_out, 'tensor', axis=0, tiled=True)  82.1 us
    all_gather x1, waiting for transfers between devices, local(): lax.all_gather(out_weight, 'dp', axis=1, tiled=True)  70.7 us
    ppermute x4, waiting for transfers between devices, partner_2(): return lax.ppermute(value, axis, pairs)  69.9 us
    all_gather x1, waiting for transfers between devices, local(): query_full = lax.all_gather(query_weight, 'dp', axis=0, tiled=True)  64.7 us
    all_gather x1, blocking collectives, local(): kv_local = lax.all_gather(kv_weight, 'dp', axis=0, tiled=True)  38.8 us
    ppermute x4, starting transfers between devices, partner_2(): return lax.ppermute(value, axis, pairs)  16.5 us
  transfers between devices with their start and end apart: 10, of which 9 were waited for; matrix products, arithmetic and copies ran while one was open for 3% of the time, Pallas kernels for 0%

commit v1 on v0

--- a/solution.py
+++ b/solution.py
@@ -1,12 +1,16 @@
+import functools
 import math
 
 import jax
 import jax.numpy as jnp
 from jax import lax
+from jax.experimental import pallas as pl
+from jax.experimental.pallas import tpu as pltpu
 from jax.sharding import PartitionSpec as P
 
 KVH = 4
 HD = 128
+MESH_ID = pl.DeviceIdType.MESH
 
 
 epsilon = 1e-05
@@ -23,6 +27,106 @@
     positions = jnp.arange(length_total, dtype=jnp.int32)
     labels = jnp.sum((ends[None, :] <= positions[:, None]).astype(jnp.int32), axis=1)
     return (labels[:, None] == labels[None, :]) & (positions[None, :] <= positions[:, None])
+
+
+def _enter(axis, n):
+    me = lax.axis_index(axis)
+    barrier = pltpu.get_barrier_semaphore()
+    for j in range(1, n):
+        pl.semaphore_signal(
+            barrier, inc=1, device_id={axis: lax.rem(me + j, n)}, device_id_type=MESH_ID
+        )
+    pl.semaphore_wait(barrier, n - 1)
+    return me
+
+
+def _gather_body(axis, n, count, *refs):
+    ins = refs[:count]
+    outs = refs[count : 2 * count]
+    send_sem, recv_sem, local_sem = refs[2 * count :]
+    me = _enter(axis, n)
+    local = []
+    for i in range(count):
+        copy = pltpu.make_async_copy(ins[i], outs[i].at[me], local_sem.at[i])
+        copy.start()
+        local.append(copy)
+    remote = []
+    for j in range(1, n):
+        peer = lax.rem(me + j, n)
+        for i in range(count):
+            copy = pltpu.make_async_remote_copy(
+                src_ref=ins[i],
+                dst_ref=outs[i].at[me],
+                send_sem=send_sem.at[i, j],
+                recv_sem=recv_sem.at[i, j],
+                device_id={axis: peer},
+                device_id_type=MESH_ID,
+            )
+            copy.start()
+            remote.append(copy)
+    for copy in remote:
+        copy.wait()
+    for copy in local:
+        copy.wait()
+
+
+def push_gather(pieces, axis, n, cid):
+    count = len(pieces)
+    nbytes = sum(p.size * p.dtype.itemsize for p in pieces)
+    return pl.pallas_call(
+        functools.partial(_gather_body, axis, n, count),
+        out_shape=[jax.ShapeDtypeStruct((n,) + p.shape, p.dtype) for p in pieces],
+        in_specs=[pl.BlockSpec(memory_space=pl.ANY)] * count,
+        out_specs=[pl.BlockSpec(memory_space=pl.ANY)] * count,
+        scratch_shapes=[
+            pltpu.SemaphoreType.DMA((count, n)),
+            pltpu.SemaphoreType.DMA((count, n)),
+            pltpu.SemaphoreType.DMA((count,)),
+        ],
+        compiler_params=pltpu.CompilerParams(collective_id=cid, has_side_effects=True),
+        cost_estimate=pl.CostEstimate(
+            flops=0, transcendentals=0, bytes_accessed=2 * n * nbytes
+        ),
+    )(*pieces)
+
+
+def _scatter_body(axis, n, x_ref, o_ref, send_sem, recv_sem, local_sem):
+    me = _enter(axis, n)
+    local = pltpu.make_async_copy(x_ref.at[me], o_ref.at[me], local_sem)
+    local.start()
+    remote = []
+    for j in range(1, n):
+        peer = lax.rem(me + j, n)
+        copy = pltpu.make_async_remote_copy(
+            src_ref=x_ref.at[peer],
+            dst_ref=o_ref.at[me],
+            send_sem=send_sem.at[j],
+            recv_sem=recv_sem.at[j],
+            device_id={axis: peer},
+            device_id_type=MESH_ID,
+        )
+        copy.start()
+        remote.append(copy)
+    for copy in remote:
+        copy.wait()
+    local.wait()
+
+
+def push_scatter(x, axis, n, cid):
+    nbytes = x.size * x.dtype.itemsize
+    return pl.pallas_call(
+        functools.partial(_scatter_body, axis, n),
+        out_shape=jax.ShapeDtypeStruct(x.shape, x.dtype),
+        in_specs=[pl.BlockSpec(memory_space=pl.ANY)],
+        out_specs=pl.BlockSpec(memory_space=pl.ANY),
+        scratch_shapes=[
+            pltpu.SemaphoreType.DMA((n,)),
+            pltpu.SemaphoreType.DMA((n,)),
+            pltpu.SemaphoreType.DMA(()),
+        ],
+        compiler_params=pltpu.CompilerParams(collective_id=cid, has_side_effects=True),
+        cost_estimate=pl.CostEstimate(flops=0, transcendentals=0, bytes_accessed=2 * nbytes),
+    )(x)
 
 
 def local(tokens, norm_gain, query_weight, kv_weight, out_weight, grad_out, doc_lengths):
@@ -32,37 +136,40 @@
     sharers = tensor_size // KVH
     levels = sharers.bit_length() - 1
     contract_last = (((1,), (1,)), ((), ()))
+    query_width = query_weight.shape[1]
+    kv_width = kv_weight.shape[1]
     values32 = tokens.astype(jnp.float32)
     root_mean = jnp.sqrt(jnp.mean(values32 * values32, axis=-1) + epsilon)
     unit = values32 / root_mean[:, None]
     gain32 = norm_gain.astype(jnp.float32)
     normed_local = (unit * gain32).astype(jnp.bfloat16)
-    normed = lax.all_gather(normed_local, "tensor", axis=0, tiled=True)
+    rows = tokens.shape[0]
+    normed_parts, grad_parts = push_gather([normed_local, grad_out], "tensor", tensor_size, 0)
+    normed = normed_parts.reshape(tensor_size * rows, -1)
+    grad_full = grad_parts.reshape(tensor_size * rows, -1)
     seq_length = normed.shape[0]
-    query_full = lax.all_gather(query_weight, "dp", axis=0, tiled=True)
+    weights_local = jnp.concatenate([query_weight, kv_weight, out_weight.T], axis=1)
+    weights_full = lax.all_gather(weights_local, "dp", axis=0, tiled=True)
+    query_full = weights_full[:, :query_width]
+    kv_local = weights_full[:, query_width : query_width + kv_width]
+    out_full_t = weights_full[:, query_width + kv_width :]
     queries = jnp.dot(normed, query_full, preferred_element_type=jnp.float32).astype(jnp.bfloat16)
-    kv_local = lax.all_gather(kv_weight, "dp", axis=0, tiled=True)
-    head_weight = kv_local
+    keyvals = jnp.dot(normed, kv_local, preferred_element_type=jnp.float32).astype(jnp.bfloat16)
     for bit_index in range(levels):
-        partner = partner_2(head_weight, "tensor", bit_index)
+        partner = partner_2(keyvals, "tensor", bit_index)
         joined_upper_half = tensor_index >> bit_index & 1 == 1
-        head_weight = jnp.concatenate(
+        keyvals = jnp.concatenate(
             [
-                jnp.where(joined_upper_half, partner, head_weight),
-                jnp.where(joined_upper_half, head_weight, partner),
+                jnp.where(joined_upper_half, partner, keyvals),
+                jnp.where(joined_upper_half, keyvals, partner),
             ],
             axis=1,
         )
-    keyvals = jnp.dot(normed, head_weight, preferred_element_type=jnp.float32).astype(jnp.bfloat16)
     key_rows = keyvals[:, :HD]
     value_rows = keyvals[:, HD:]
-    grad_full = lax.all_gather(grad_out, "tensor", axis=0, tiled=True)
-    out_grad = lax.dot_general(
-        grad_full,
-        lax.all_gather(out_weight, "dp", axis=1, tiled=True),
-        contract_last,
-        preferred_element_type=jnp.float32,
-    ).astype(jnp.bfloat16)
+    out_grad = jnp.dot(grad_full, out_full_t, preferred_element_type=jnp.float32).astype(
+        jnp.bfloat16
+    )
     local_heads = queries.shape[1] // HD
     query_heads = queries.reshape(seq_length, local_heads, HD)
     out_heads = out_grad.reshape(seq_length, local_heads, HD)
@@ -100,9 +207,9 @@
         query_grad, query_full, contract_last, preferred_element_type=jnp.float32
     )
     from_kv = lax.dot_general(kv_grad, kv_local, contract_last, preferred_element_type=jnp.float32)
-    normed_grad = lax.psum_scatter(
-        (from_query + from_kv).astype(jnp.bfloat16), "tensor", scatter_dimension=0, tiled=True
-    ).astype(jnp.float32)
+    partial = (from_query + from_kv).astype(jnp.bfloat16).reshape(tensor_size, rows, -1)
+    arrived = push_scatter(partial, "tensor", tensor_size, 1)
+    normed_grad = jnp.sum(arrived.astype(jnp.float32), axis=0)
     scaled = normed_grad * gain32
     correction = unit * jnp.mean(scaled * unit, axis=-1, keepdims=True)
     input_grad = (grad_out.astype(jnp.float32) + (scaled - correction) / root_mean[:, None]).astype(
@@ -120,7 +227,6 @@
         ).astype(jnp.float32)
         / data_size
     )
-    query_width = query_weight.shape[1]
     return (input_grad, weight_grads[:, :query_width], weight_grads[:, query_width:])
 
 

time: 719 us -> 294 us (0.41)
  waiting for transfers between devices: 613 us -> 69 us
  Pallas kernels: 0 us -> 164 us
  blocking collectives: 38.8 us -> 0 us
    all_gather x4 -> x1, waiting for transfers between devices: 217 us -> 1.81 us  [local(): weights_full = lax.all_gather(weights_local, 'dp', axis=0, tiled=True)]
    reduce_scatter x1 -> x0, waiting for transfers between devices: 202 us -> none  [local(): lax.psum_scatter((from_query + from_kv).astype(jnp.bfloat16), 'tensor', s...]
    pallas_call x0 -> x2, Pallas kernels: none -> 164 us  [the longest x1 110 us: push_gather(): pl.pallas_call(functools.partial(_gather_body, axis, n, count), out_shape...]
    ppermute x4, waiting for transfers between devices: 69.9 us -> 3.85 us  [partner_2(): return lax.ppermute(value, axis, pairs)]
    unnamed x7 -> x3, waiting for transfers between devices: 123 us -> 63.3 us
    all_gather x1 -> x0, blocking collectives: 38.8 us -> none  [local(): kv_local = lax.all_gather(kv_weight, 'dp', axis=0, tiled=True)]
  transfers between devices with their start and end apart: 10 -> 6, of which waited for: 9 -> 5; matrix products, arithmetic and copies ran while one was open for 3% -> 6% of each run, Pallas kernels for 0% -> 56%
where the time goes in v1:
time: 294 us; the launch traced here: 292 us
  Pallas kernels  164 us (56%)
  waiting for transfers between devices  69 us (23%)
  matrix products  16.7 us (6%)
  between operations  14.3 us (5%)
  starting transfers between devices  12.8 us (4%)
  other arithmetic  9.07 us (3%)
  local copies, waits for them, and re-layouts  6.16 us (2%)
    pallas_call x1, Pallas kernels, push_gather(): pl.pallas_call(functools.partial(_gather_body, axis, n, count), out_shape...  110 us
    unnamed x3, waiting for transfers between devices  63.3 us
    pallas_call x1, Pallas kernels, push_scatter(): pl.pallas_call(functools.partial(_scatter_body, axis, n), out_shape=jax.S...  53.2 us
    ppermute x4, starting transfers between devices, partner_2(): return lax.ppermute(value, axis, pairs)  12.7 us
  transfers between devices with their start and end apart: 6, of which 5 were waited for; matrix products, arithmetic and copies ran while one was open for 6% of the time, Pallas kernels for 56%

profile of v1, /device:TPU:1, one launch (start us, length us, event | category | flops | bytes accessed | tf_op | source)
XLA Modules:
  0.0 291.6 jit_solution(4798796242399276753)
XLA Ops:
  7.2 0.9 copy.28
  8.2 1.5 pad_maximum_fusion
  9.8 0.8 reduce-window.8
  11.3 1.0 fusion.29
  12.3 1.7 multiply_convert_fusion.refs_0_
  14.0 110.4 %shard_map.94 = (bf16[16,16,4096]{2,1,0:T(8,128)(2,1)}, bf16[16,16,4096]{2,1,0:T(8,128)(2,1)}) custom-call(bf16[16,4096]{1,0:T(8,128)(2,1)} %multiply_convert_fusion.refs_0_, bf16[16,4096]{1,0:T(8,128)(2,1)} %refs_1_.1), custom_call_target="tpu_custom_call" | custom-call | bytes 8388608 | tf_op jit(solution)/shard_map/pallas_call | solution.py:76
  124.6 1.8 all-gather.2.cloned.1.call-done
  126.4 2.4 convolution_convert_fusion.2
  128.9 2.1 collective-permute-start
  130.9 2.3 fusion.17
  133.7 3.8 %collective-permute-start.1 = (bf16[256,128]{0,1:T(8,128)(2,1)S(1)}, bf16[256,128]{0,1:T(8,128)(2,1)S(1)}, u32[]{:S(2)}, u32[]{:S(2)}) collective-permute-start(bf16[256,128]{0,1:T(8,128)(2,1)S(1)} %pad_maximum_fusion.1), channel_id=1, source_target_pairs={{0,2},{1,3},{2,0},{3,1},{4,6},{5,7},{6,4},{7,5},{8,10},{9,11},{10,... | collective-permute-start | bytes 196616 | tf_op jit(solution)/shard_map/ppermute | solution.py:22
  137.5 2.5 fusion.20
  141.3 3.4 %collective-permute-start.2 = (bf16[256,128]{0,1:T(8,128)(2,1)S(1)}, bf16[256,128]{0,1:T(8,128)(2,1)S(1)}, u32[]{:S(2)}, u32[]{:S(2)}) collective-permute-start(bf16[256,128]{0,1:T(8,128)(2,1)S(1)} %get-tuple-element.20), channel_id=1, source_target_pairs={{0,2},{1,3},{2,0},{3,1},{4,6},{5,7},{6,4},{7,5},{8,10},{9,11},{10,... | collective-permute-start | bytes 196616 | tf_op jit(solution)/shard_map/ppermute | solution.py:22
  144.7 2.5 collective-permute-done.2
  147.2 3.5 %collective-permute-start.3 = (bf16[256,64]{0,1:T(8,128)(2,1)S(1)}, bf16[256,64]{0,1:T(8,128)(2,1)S(1)}, u32[]{:S(2)}, u32[]{:S(2)}) collective-permute-start(bf16[256,64]{0,1:T(8,128)(2,1)S(1)} %select_convert_fusion.1), channel_id=1, source_target_pairs={{0,1},{1,0},{2,3},{3,2},{4,5},{5,4},{6,7},{7,6},{8,9},{9,8},{10,11... | collective-permute-start | bytes 98312 | tf_op jit(solution)/shard_map/ppermute | solution.py:22
  151.0 1.0 collective-permute-done.3
  152.0 2.4 convolution_convert_fusion
  154.4 2.8 copy.46
  157.3 2.3 fusion.5
  159.6 3.2 %fusion.2 = bf16[256,4096]{1,0:T(8,128)(2,1)} fusion(f32[256,4096]{1,0:T(8,128)S(1)} %fusion.5, bf16[256,64]{0,1:T(8,128)(2,1)S(1)} %add_convert_fusion.1, bf16[4096,576]{0,1:T(8,128)(2,1)} %all-gather.2.cloned.1.call-done), kind=kOutput, calls=%fused_computation.4 | convolution fusion | flops 136314880 | bytes 6848512 | tf_op jit(solution)/shard_map/dot_general | solution.py:209
  162.7 53.2 %shard_map.95 = bf16[16,16,4096]{2,1,0:T(8,128)(2,1)} custom-call(bf16[16,16,4096]{2,1,0:T(8,128)(2,1)} %bitcast.53), custom_call_target="tpu_custom_call" | custom-call | bytes 4194304 | tf_op jit(solution)/shard_map/pallas_call | solution.py:117
  216.0 2.0 convert_reduce_fusion
  219.0 63.3 %reduce-scatter.4.cloned.1.call-done = bf16[128,320]{1,0:T(8,128)(2,1)} async-done(((bf16[4096,320]{1,0:T(8,128)(2,1)}), bf16[128,320]{1,0:T(8,128)(2,1)}) %reduce-scatter.4.cloned.1.call-update) | async-done | bytes 81936
  282.3 1.0 copy.47
  (36 shorter events, 5.4 us)
Async XLA Ops:
  7.2 119.3 %all-gather.2.cloned.1.call-start = ((), (), s32[]{:S(2)}) async-start(), calls=%async_computation.1 | async-start | bytes 4866048 | tf_op jit(solution)/shard_map/all_gather | solution.py:152
  9.7 272.6 %reduce-scatter.4.cloned.1.call-start = ((), (), s32[]{:S(2)}) async-start(), calls=%async_computation.2 | async-start | bytes 3244032
  124.4 6.5 %copy-start = (bf16[16,16,4096]{2,1,0:T(8,128)(2,1)S(1)}, bf16[16,16,4096]{2,1,0:T(8,128)(2,1)}, u32[]{:S(2)}) copy-start(bf16[16,16,4096]{2,1,0:T(8,128)(2,1)} %get-tuple-element.5) | copy-start | bytes 6291460
  128.9 8.6 %copy-start.3 = (bf16[16,16,4096]{2,1,0:T(8,128)(2,1)S(1)}, bf16[16,16,4096]{2,1,0:T(8,128)(2,1)}, u32[]{:S(2)}) copy-start(bf16[16,16,4096]{2,1,0:T(8,128)(2,1)} %get-tuple-element.6) | copy-start | bytes 6291460
  128.9 4.8 %collective-permute-start = (bf16[256,64]{0,1:T(8,128)(2,1)S(1)}, bf16[256,64]{0,1:T(8,128)(2,1)S(1)}, u32[]{:S(2)}, u32[]{:S(2)}) collective-permute-start(bf16[256,64]{0,1:T(8,128)(2,1)S(1)} %convolution_convert_fusion.2), channel_id=1, source_target_pairs={{0,1},{1,0},{2,3},{3,2},{4,5},{5,4},{6,7},{7,6},{8,9},{9,8},{10,11... | collective-permute-start | bytes 98312 | tf_op jit(solution)/shard_map/ppermute | solution.py:22
  133.7 6.4 %collective-permute-start.1 = (bf16[256,128]{0,1:T(8,128)(2,1)S(1)}, bf16[256,128]{0,1:T(8,128)(2,1)S(1)}, u32[]{:S(2)}, u32[]{:S(2)}) collective-permute-start(bf16[256,128]{0,1:T(8,128)(2,1)S(1)} %pad_maximum_fusion.1), channel_id=1, source_target_pairs={{0,2},{1,3},{2,0},{3,1},{4,6},{5,7},{6,4},{7,5},{8,10},{9,11},{10,... | collective-permute-start | bytes 196616 | tf_op jit(solution)/shard_map/ppermute | solution.py:22
  141.3 5.9 %collective-permute-start.2 = (bf16[256,128]{0,1:T(8,128)(2,1)S(1)}, bf16[256,128]{0,1:T(8,128)(2,1)S(1)}, u32[]{:S(2)}, u32[]{:S(2)}) collective-permute-start(bf16[256,128]{0,1:T(8,128)(2,1)S(1)} %get-tuple-element.20), channel_id=1, source_target_pairs={{0,2},{1,3},{2,0},{3,1},{4,6},{5,7},{6,4},{7,5},{8,10},{9,11},{10,... | collective-permute-start | bytes 196616 | tf_op jit(solution)/shard_map/ppermute | solution.py:22
  147.2 4.7 %collective-permute-start.3 = (bf16[256,64]{0,1:T(8,128)(2,1)S(1)}, bf16[256,64]{0,1:T(8,128)(2,1)S(1)}, u32[]{:S(2)}, u32[]{:S(2)}) collective-permute-start(bf16[256,64]{0,1:T(8,128)(2,1)S(1)} %select_convert_fusion.1), channel_id=1, source_target_pairs={{0,1},{1,0},{2,3},{3,2},{4,5},{5,4},{6,7},{7,6},{8,9},{9,8},{10,11... | collective-permute-start | bytes 98312 | tf_op jit(solution)/shard_map/ppermute | solution.py:22
  216.0 2.0 copy-start.1
  216.0 2.2 copy-start.2
Sparse Core Ops, SparseCore 0:
  10.1 116.3 all-gather.1
  157.4 124.9 reduce-scatter.3

commit v2 on v0

--- a/solution.py
+++ b/solution.py
@@ -1,12 +1,16 @@
+import functools
 import math
 
 import jax
 import jax.numpy as jnp
 from jax import lax
+from jax.experimental import pallas as pl
+from jax.experimental.pallas import tpu as pltpu
 from jax.sharding import PartitionSpec as P
 
 KVH = 4
 HD = 128
+MESH_ID = pl.DeviceIdType.MESH
 
 
 epsilon = 1e-05
@@ -23,6 +27,78 @@
     positions = jnp.arange(length_total, dtype=jnp.int32)
     labels = jnp.sum((ends[None, :] <= positions[:, None]).astype(jnp.int32), axis=1)
     return (labels[:, None] == labels[None, :]) & (positions[None, :] <= positions[:, None])
+
+
+def _push_body(plan, *refs):
+    count = len(plan)
+    ins = refs[:count]
+    outs = refs[count : 2 * count]
+    send_sems = refs[2 * count : 3 * count]
+    recv_sems = refs[3 * count : 4 * count]
+    local_sem = refs[4 * count]
+    barrier = pltpu.get_barrier_semaphore()
+    mine = []
+    expected = 0
+    for axis, n, _ in plan:
+        me = lax.axis_index(axis)
+        mine.append(me)
+        for j in range(1, n):
+            pl.semaphore_signal(
+                barrier, inc=1, device_id={axis: lax.rem(me + j, n)}, device_id_type=MESH_ID
+            )
+        expected += n - 1
+    pl.semaphore_wait(barrier, expected)
+    local = []
+    for g, (axis, n, scatter) in enumerate(plan):
+        me = mine[g]
+        src = ins[g].at[me] if scatter else ins[g]
+        copy = pltpu.make_async_copy(src, outs[g].at[me], local_sem.at[g])
+        copy.start()
+        local.append(copy)
+    remote = []
+    for j in range(1, max(n for _, n, _ in plan)):
+        for g, (axis, n, scatter) in enumerate(plan):
+            if j >= n:
+                continue
+            me = mine[g]
+            peer = lax.rem(me + j, n)
+            copy = pltpu.make_async_remote_copy(
+                src_ref=ins[g].at[peer] if scatter else ins[g],
+                dst_ref=outs[g].at[me],
+                send_sem=send_sems[g].at[j],
+                recv_sem=recv_sems[g].at[j],
+                device_id={axis: peer},
+                device_id_type=MESH_ID,
+            )
+            copy.start()
+            remote.append(copy)
+    for copy in remote:
+        copy.wait()
+    for copy in local:
+        copy.wait()
+
+
+def push_exchange(groups, cid):
+    plan = tuple((axis, n, scatter) for axis, n, _, scatter in groups)
+    arrays = [array for _, _, array, _ in groups]
+    out_shape = []
+    moved = 0
+    for _, n, array, scatter in groups:
+        shape = array.shape if scatter else (n,) + array.shape
+        out_shape.append(jax.ShapeDtypeStruct(shape, array.dtype))
+        moved += 2 * math.prod(shape) * array.dtype.itemsize
+    count = len(groups)
+    return pl.pallas_call(
+        functools.partial(_push_body, plan),
+        out_shape=out_shape,
+        in_specs=[pl.BlockSpec(memory_space=pl.ANY)] * count,
+        out_specs=[pl.BlockSpec(memory_space=pl.ANY)] * count,
+        scratch_shapes=[pltpu.SemaphoreType.DMA((n,)) for _, n, _, _ in groups]
+        + [pltpu.SemaphoreType.DMA((n,)) for _, n, _, _ in groups]
+        + [pltpu.SemaphoreType.DMA((count,))],
+        compiler_params=pltpu.CompilerParams(collective_id=cid, has_side_effects=True),
+        cost_estimate=pl.CostEstimate(flops=0, transcendentals=0, bytes_accessed=moved),
+    )(*arrays)
 
 
 def local(tokens, norm_gain, query_weight, kv_weight, out_weight, grad_out, doc_lengths):
@@ -32,37 +108,42 @@
     sharers = tensor_size // KVH
     levels = sharers.bit_length() - 1
     contract_last = (((1,), (1,)), ((), ()))
+    query_width = query_weight.shape[1]
+    kv_width = kv_weight.shape[1]
     values32 = tokens.astype(jnp.float32)
     root_mean = jnp.sqrt(jnp.mean(values32 * values32, axis=-1) + epsilon)
     unit = values32 / root_mean[:, None]
     gain32 = norm_gain.astype(jnp.float32)
     normed_local = (unit * gain32).astype(jnp.bfloat16)
-    normed = lax.all_gather(normed_local, "tensor", axis=0, tiled=True)
+    rows = tokens.shape[0]
+    normed_parts, grad_parts = push_exchange(
+        [("tensor", tensor_size, normed_local, False), ("tensor", tensor_size, grad_out, False)], 0
+    )
+    normed = normed_parts.reshape(tensor_size * rows, -1)
+    grad_full = grad_parts.reshape(tensor_size * rows, -1)
     seq_length = normed.shape[0]
-    query_full = lax.all_gather(query_weight, "dp", axis=0, tiled=True)
+    weights_local = jnp.concatenate([query_weight, kv_weight, out_weight.T], axis=1)
+    weights_full = lax.all_gather(weights_local, "dp", axis=0, tiled=True)
+    query_full = weights_full[:, :query_width]
+    kv_local = weights_full[:, query_width : query_width + kv_width]
+    out_full_t = weights_full[:, query_width + kv_width :]
     queries = jnp.dot(normed, query_full, preferred_element_type=jnp.float32).astype(jnp.bfloat16)
-    kv_local = lax.all_gather(kv_weight, "dp", axis=0, tiled=True)
-    head_weight = kv_local
+    keyvals = jnp.dot(normed, kv_local, preferred_element_type=jnp.float32).astype(jnp.bfloat16)
     for bit_index in range(levels):
-        partner = partner_2(head_weight, "tensor", bit_index)
+        partner = partner_2(keyvals, "tensor", bit_index)
         joined_upper_half = tensor_index >> bit_index & 1 == 1
-        head_weight = jnp.concatenate(
+        keyvals = jnp.concatenate(
             [
-                jnp.where(joined_upper_half, partner, head_weight),
-                jnp.where(joined_upper_half, head_weight, partner),
+                jnp.where(joined_upper_half, partner, keyvals),
+                jnp.where(joined_upper_half, keyvals, partner),
             ],
             axis=1,
         )
-    keyvals = jnp.dot(normed, head_weight, preferred_element_type=jnp.float32).astype(jnp.bfloat16)
     key_rows = keyvals[:, :HD]
     value_rows = keyvals[:, HD:]
-    grad_full = lax.all_gather(grad_out, "tensor", axis=0, tiled=True)
-    out_grad = lax.dot_general(
-        grad_full,
-        lax.all_gather(out_weight, "dp", axis=1, tiled=True),
-        contract_last,
-        preferred_element_type=jnp.float32,
-    ).astype(jnp.bfloat16)
+    out_grad = jnp.dot(grad_full, out_full_t, preferred_element_type=jnp.float32).astype(
+        jnp.bfloat16
+    )
     local_heads = queries.shape[1] // HD
     query_heads = queries.reshape(seq_length, local_heads, HD)
     out_heads = out_grad.reshape(seq_length, local_heads, HD)
@@ -100,27 +181,22 @@
         query_grad, query_full, contract_last, preferred_element_type=jnp.float32
     )
     from_kv = lax.dot_general(kv_grad, kv_local, contract_last, preferred_element_type=jnp.float32)
-    normed_grad = lax.psum_scatter(
-        (from_query + from_kv).astype(jnp.bfloat16), "tensor", scatter_dimension=0, tiled=True
-    ).astype(jnp.float32)
+    partial = (from_query + from_kv).astype(jnp.bfloat16).reshape(tensor_size, rows, -1)
+    combined = jnp.concatenate([query_grad, kv_grad], axis=1)
+    weight_partial = lax.dot_general(
+        normed, combined, (((0,), (0,)), ((), ())), preferred_element_type=jnp.float32
+    ).astype(jnp.bfloat16)
+    weight_partial = weight_partial.reshape(data_size, -1, weight_partial.shape[1])
+    arrived, weight_arrived = push_exchange(
+        [("tensor", tensor_size, partial, True), ("dp", data_size, weight_partial, True)], 1
+    )
+    normed_grad = jnp.sum(arrived.astype(jnp.float32), axis=0)
     scaled = normed_grad * gain32
     correction = unit * jnp.mean(scaled * unit, axis=-1, keepdims=True)
     input_grad = (grad_out.astype(jnp.float32) + (scaled - correction) / root_mean[:, None]).astype(
         jnp.bfloat16
     )
-    combined = jnp.concatenate([query_grad, kv_grad], axis=1)
-    weight_grads = (
-        lax.psum_scatter(
-            lax.dot_general(
-                normed, combined, (((0,), (0,)), ((), ())), preferred_element_type=jnp.float32
-            ).astype(jnp.bfloat16),
-            "dp",
-            scatter_dimension=0,
-            tiled=True,
-        ).astype(jnp.float32)
-        / data_size
-    )
-    query_width = query_weight.shape[1]
+    weight_grads = jnp.sum(weight_arrived.astype(jnp.float32), axis=0) / data_size
     return (input_grad, weight_grads[:, :query_width], weight_grads[:, query_width:])
 
 

time: 719 us -> 276 us (0.38)
  waiting for transfers between devices: 613 us -> 4.58 us
  Pallas kernels: 0 us -> 205 us
  blocking collectives: 38.8 us -> 0 us
    all_gather x4 -> x1, waiting for transfers between devices: 217 us -> 2.01 us  [local(): weights_full = lax.all_gather(weights_local, 'dp', axis=0, tiled=True)]
    pallas_call x0 -> x2, Pallas kernels: none -> 205 us  [push_exchange(): pl.pallas_call(functools.partial(_push_body, plan), out_shape=out_shape,...]
    reduce_scatter x1 -> x0, waiting for transfers between devices: 202 us -> none  [local(): lax.psum_scatter((from_query + from_kv).astype(jnp.bfloat16), 'tensor', s...]
    unnamed x7 -> x1, waiting for transfers between devices: 123 us -> 0.02 us
    ppermute x4, waiting for transfers between devices: 69.9 us -> 2.55 us  [partner_2(): return lax.ppermute(value, axis, pairs)]
    all_gather x1 -> x0, blocking collectives: 38.8 us -> none  [local(): kv_local = lax.all_gather(kv_weight, 'dp', axis=0, tiled=True)]
  transfers between devices with their start and end apart: 10 -> 5, of which waited for: 9 -> 3; matrix products, arithmetic and copies ran while one was open for 3% -> 5% of each run, Pallas kernels for 0% -> 41%
where the time goes in v2:
time: 276 us; the launch traced here: 270 us
  Pallas kernels  205 us (74%)
  matrix products  18.6 us (7%)
  between operations  14.3 us (5%)
  starting transfers between devices  12.7 us (5%)
  other arithmetic  9.95 us (4%)
  local copies, waits for them, and re-layouts  5.17 us (2%)
  waiting for transfers between devices  4.58 us (2%)
    pallas_call x2, Pallas kernels, push_exchange(): pl.pallas_call(functools.partial(_push_body, plan), out_shape=out_shape,...  205 us
    ppermute x4, starting transfers between devices, partner_2(): return lax.ppermute(value, axis, pairs)  12.6 us
  transfers between devices with their start and end apart: 5, of which 3 were waited for; matrix products, arithmetic and copies ran while one was open for 5% of the time, Pallas kernels for 41%

profile of v2, /device:TPU:1, one launch (start us, length us, event | category | flops | bytes accessed | tf_op | source)
XLA Modules:
  0.0 270.5 jit_solution(14289053919609702830)
XLA Ops:
  7.2 0.9 copy.30
  8.2 1.5 pad_maximum_fusion
  9.7 0.7 convert_element_type.68
  10.4 0.8 reduce-window.8
  11.2 1.0 fusion.29
  12.3 1.7 multiply_convert_fusion.refs_0_
  14.0 110.4 %shard_map.94 = (bf16[16,16,4096]{2,1,0:T(8,128)(2,1)}, bf16[16,16,4096]{2,1,0:T(8,128)(2,1)}) custom-call(bf16[16,4096]{1,0:T(8,128)(2,1)} %multiply_convert_fusion.refs_0_, bf16[16,4096]{1,0:T(8,128)(2,1)} %refs_1_.1), custom_call_target="tpu_custom_call" | custom-call | bytes 8388608 | tf_op jit(solution)/shard_map/pallas_call | solution.py:91
  124.6 2.0 all-gather.2.cloned.1.call-done
  126.6 2.4 convolution_convert_fusion.2
  129.0 2.1 collective-permute-start
  131.1 2.3 fusion.17
  133.8 3.7 %collective-permute-start.1 = (bf16[256,128]{0,1:T(8,128)(2,1)S(1)}, bf16[256,128]{0,1:T(8,128)(2,1)S(1)}, u32[]{:S(2)}, u32[]{:S(2)}) collective-permute-start(bf16[256,128]{0,1:T(8,128)(2,1)S(1)} %pad_maximum_fusion.1), channel_id=1, source_target_pairs={{0,2},{1,3},{2,0},{3,1},{4,6},{5,7},{6,4},{7,5},{8,10},{9,11},{10,... | collective-permute-start | bytes 196616 | tf_op jit(solution)/shard_map/ppermute | solution.py:22
  137.6 2.5 fusion.20
  141.3 3.4 %collective-permute-start.2 = (bf16[256,128]{0,1:T(8,128)(2,1)S(1)}, bf16[256,128]{0,1:T(8,128)(2,1)S(1)}, u32[]{:S(2)}, u32[]{:S(2)}) collective-permute-start(bf16[256,128]{0,1:T(8,128)(2,1)S(1)} %get-tuple-element.24), channel_id=1, source_target_pairs={{0,2},{1,3},{2,0},{3,1},{4,6},{5,7},{6,4},{7,5},{8,10},{9,11},{10,... | collective-permute-start | bytes 196616 | tf_op jit(solution)/shard_map/ppermute | solution.py:22
  145.1 2.2 collective-permute-done.2
  147.3 3.4 %collective-permute-start.3 = (bf16[256,64]{0,1:T(8,128)(2,1)S(1)}, bf16[256,64]{0,1:T(8,128)(2,1)S(1)}, u32[]{:S(2)}, u32[]{:S(2)}) collective-permute-start(bf16[256,64]{0,1:T(8,128)(2,1)S(1)} %select_convert_fusion.1), channel_id=1, source_target_pairs={{0,1},{1,0},{2,3},{3,2},{4,5},{5,4},{6,7},{7,6},{8,9},{9,8},{10,11... | collective-permute-start | bytes 98312 | tf_op jit(solution)/shard_map/ppermute | solution.py:22
  150.7 4.5 %fusion.5 = f32[256,4096]{1,0:T(8,128)} fusion(bf16[256,256]{0,1:T(8,128)(2,1)S(1)} %bitcast.58, bf16[4096,576]{0,1:T(8,128)(2,1)} %all-gather.2.cloned.1.call-done), kind=kOutput, calls=%fused_computation.9 | convolution fusion | flops 536870912 | bytes 6422528 | tf_op jit(solution)/shard_map/dot_general | solution.py:180
  155.3 0.9 convolution_convert_fusion
  156.1 2.8 %copy.38 = bf16[4096,320]{1,0:T(8,128)(2,1)} copy(bf16[4096,320]{0,1:T(8,128)(2,1)S(1)} %convolution_convert_fusion) | data formatting | bytes 5242880 | tf_op jit(solution)/shard_map/convert_element_type | solution.py:188
  159.0 4.5 %fusion.2 = bf16[256,4096]{1,0:T(8,128)(2,1)} fusion(f32[256,4096]{1,0:T(8,128)} %fusion.5, bf16[256,64]{0,1:T(8,128)(2,1)S(1)} %add_convert_fusion.1, bf16[4096,576]{0,1:T(8,128)(2,1)} %all-gather.2.cloned.1.call-done), kind=kOutput, calls=%fused_computation.5 | convolution fusion | flops 136314880 | bytes 6848512 | tf_op jit(solution)/shard_map/dot_general | solution.py:183
  163.4 94.8 %shard_map.95 = (bf16[16,16,4096]{2,1,0:T(8,128)(2,1)}, bf16[32,128,320]{2,1,0:T(8,128)(2,1)}) custom-call(bf16[16,16,4096]{2,1,0:T(8,128)(2,1)} %bitcast.54, bf16[32,128,320]{2,1,0:T(8,128)(2,1)} %bitcast.53), custom_call_target="tpu_custom_call" | custom-call | bytes 9437184 | tf_op jit(solution)/shard_map/pallas_call | solution.py:91
  258.3 2.6 convert_reduce_fusion
  262.1 0.8 add_convert_fusion
  262.9 0.7 copy.39
  (37 shorter events, 3.4 us)
Async XLA Ops:
  7.2 119.4 %all-gather.2.cloned.1.call-start = ((), (), s32[]{:S(2)}) async-start(), calls=%async_computation | async-start | bytes 4866048 | tf_op jit(solution)/shard_map/all_gather | solution.py:126
  124.4 6.7 %copy-start = (bf16[16,16,4096]{2,1,0:T(8,128)(2,1)S(1)}, bf16[16,16,4096]{2,1,0:T(8,128)(2,1)}, u32[]{:S(2)}) copy-start(bf16[16,16,4096]{2,1,0:T(8,128)(2,1)} %get-tuple-element.7) | copy-start | bytes 6291460
  129.0 8.5 %copy-start.5 = (bf16[16,16,4096]{2,1,0:T(8,128)(2,1)S(1)}, bf16[16,16,4096]{2,1,0:T(8,128)(2,1)}, u32[]{:S(2)}) copy-start(bf16[16,16,4096]{2,1,0:T(8,128)(2,1)} %get-tuple-element.8) | copy-start | bytes 6291460
  129.0 4.8 %collective-permute-start = (bf16[256,64]{0,1:T(8,128)(2,1)S(1)}, bf16[256,64]{0,1:T(8,128)(2,1)S(1)}, u32[]{:S(2)}, u32[]{:S(2)}) collective-permute-start(bf16[256,64]{0,1:T(8,128)(2,1)S(1)} %convolution_convert_fusion.2), channel_id=1, source_target_pairs={{0,1},{1,0},{2,3},{3,2},{4,5},{5,4},{6,7},{7,6},{8,9},{9,8},{10,11... | collective-permute-start | bytes 98312 | tf_op jit(solution)/shard_map/ppermute | solution.py:22
  133.8 6.3 %collective-permute-start.1 = (bf16[256,128]{0,1:T(8,128)(2,1)S(1)}, bf16[256,128]{0,1:T(8,128)(2,1)S(1)}, u32[]{:S(2)}, u32[]{:S(2)}) collective-permute-start(bf16[256,128]{0,1:T(8,128)(2,1)S(1)} %pad_maximum_fusion.1), channel_id=1, source_target_pairs={{0,2},{1,3},{2,0},{3,1},{4,6},{5,7},{6,4},{7,5},{8,10},{9,11},{10,... | collective-permute-start | bytes 196616 | tf_op jit(solution)/shard_map/ppermute | solution.py:22
  141.3 5.9 %collective-permute-start.2 = (bf16[256,128]{0,1:T(8,128)(2,1)S(1)}, bf16[256,128]{0,1:T(8,128)(2,1)S(1)}, u32[]{:S(2)}, u32[]{:S(2)}) collective-permute-start(bf16[256,128]{0,1:T(8,128)(2,1)S(1)} %get-tuple-element.24), channel_id=1, source_target_pairs={{0,2},{1,3},{2,0},{3,1},{4,6},{5,7},{6,4},{7,5},{8,10},{9,11},{10,... | collective-permute-start | bytes 196616 | tf_op jit(solution)/shard_map/ppermute | solution.py:22
  147.3 8.0 %collective-permute-start.3 = (bf16[256,64]{0,1:T(8,128)(2,1)S(1)}, bf16[256,64]{0,1:T(8,128)(2,1)S(1)}, u32[]{:S(2)}, u32[]{:S(2)}) collective-permute-start(bf16[256,64]{0,1:T(8,128)(2,1)S(1)} %select_convert_fusion.1), channel_id=1, source_target_pairs={{0,1},{1,0},{2,3},{3,2},{4,5},{5,4},{6,7},{7,6},{8,9},{9,8},{10,11... | collective-permute-start | bytes 98312 | tf_op jit(solution)/shard_map/ppermute | solution.py:22
  150.7 4.5 %copy-start.1 = (bf16[16,16,4096]{2,1,0:T(8,128)(2,1)S(1)}, bf16[16,16,4096]{2,1,0:T(8,128)(2,1)}, u32[]{:S(2)}) copy-start(bf16[16,16,4096]{2,1,0:T(8,128)(2,1)} %get-tuple-element.7) | copy-start | bytes 6291460
  258.3 3.3 %copy-start.2 = (bf16[16,16,4096]{2,1,0:T(8,128)(2,1)S(1)}, bf16[16,16,4096]{2,1,0:T(8,128)(2,1)}, u32[]{:S(2)}) copy-start(bf16[16,16,4096]{2,1,0:T(8,128)(2,1)} %get-tuple-element.9) | copy-start | bytes 6291460
  258.3 3.6 %copy-start.3 = (bf16[16,4096]{1,0:T(8,128)(2,1)S(1)}, bf16[16,4096]{1,0:T(8,128)(2,1)}, u32[]{:S(2)}) copy-start(bf16[16,4096]{1,0:T(8,128)(2,1)} %param.7) | copy-start | bytes 393220
  258.3 3.8 %copy-start.4 = (bf16[16,4096]{1,0:T(8,128)(2,1)S(1)}, bf16[16,4096]{1,0:T(8,128)(2,1)}, u32[]{:S(2)}) copy-start(bf16[16,4096]{1,0:T(8,128)(2,1)} %refs_1_.1) | copy-start | bytes 393220
Sparse Core Ops, SparseCore 0:
  10.1 116.4 all-gather.1

commit v3 on v2

--- a/solution.py
+++ b/solution.py
@@ -11,6 +11,7 @@
 KVH = 4
 HD = 128
 MESH_ID = pl.DeviceIdType.MESH
+RING = 8
 
 
 epsilon = 1e-05
@@ -101,6 +102,112 @@
     )(*arrays)
 
 
+def _gather_start_body(ring, pieces_ref, weights_ref, tens_out, dp_out, ring_send, ring_recv,
+                       cross_sem, dp_send, dp_recv, local_sem):
+    n_t = lax.axis_size("tensor")
+    n_d = lax.axis_size("dp")
+    t = lax.axis_index("tensor")
+    r = lax.axis_index("dp")
+    z = lax.rem(t, ring)
+    base = t - z
+    other = lax.rem(t + ring, n_t) - z
+    cross = lax.rem(t + ring, n_t)
+    right = base + lax.rem(z + 1, ring)
+    left = base + lax.rem(z + ring - 1, ring)
+    pair = r + 1 - 2 * lax.rem(r, 2)
+    peers = n_d // 2
+    barrier = pltpu.get_barrier_semaphore()
+    for device in ({"tensor": cross}, {"tensor": right}, {"tensor": left}, {"dp": pair}):
+        pl.semaphore_signal(barrier, inc=1, device_id=device, device_id_type=MESH_ID)
+    for k in range(1, peers):
+        pl.semaphore_signal(
+            barrier, inc=1, device_id={"dp": lax.rem(r + 2 * k, n_d)}, device_id_type=MESH_ID
+        )
+    pl.semaphore_wait(barrier, 4 + peers - 1)
+
+    def remote(src, dst, send, recv, device):
+        copy = pltpu.make_async_remote_copy(
+            src_ref=src, dst_ref=dst, send_sem=send, recv_sem=recv,
+            device_id=device, device_id_type=MESH_ID,
+        )
+        copy.start()
+        return copy
+
+    waits = []
+    for k in range(1, peers):
+        waits.append(remote(weights_ref, dp_out.at[r], dp_send.at[0, k], dp_recv.at[0, k],
+                            {"dp": lax.rem(r + 2 * k, n_d)}))
+    waits.append(remote(weights_ref, dp_out.at[r], dp_send.at[0, 0], dp_recv.at[0, 0],
+                        {"dp": pair}))
+    crossed = remote(pieces_ref, tens_out.at[t], cross_sem.at[0], cross_sem.at[1],
+                     {"tensor": cross})
+    own_t = pltpu.make_async_copy(pieces_ref, tens_out.at[t], local_sem.at[0])
+    own_t.start()
+    own_d = pltpu.make_async_copy(weights_ref, dp_out.at[r], local_sem.at[1])
+    own_d.start()
+    crossed.wait()
+    steps = (ring // 2, ring - 1 - ring // 2)
+    moving = [None, None]
+    for s in range(max(steps)):
+        for d, (target, sign) in enumerate(((right, -1), (left, 1))):
+            if s >= steps[d]:
+                continue
+            if s > 0:
+                for copy in moving[d]:
+                    copy.wait_recv()
+            origin = lax.rem(z + sign * s + ring, ring)
+            sent = []
+            for h, start in enumerate((base, other)):
+                slot = start + origin
+                src = pieces_ref if (s == 0 and h == 0) else tens_out.at[slot]
+                sent.append(remote(src, tens_out.at[slot], ring_send.at[d, s, h],
+                                   ring_recv.at[d, s, h], {"tensor": target}))
+            waits.extend(sent)
+            moving[d] = sent
+    for d in range(2):
+        for copy in moving[d]:
+            copy.wait_recv()
+    for k in range(1, peers):
+        slot = lax.rem(r + n_d - 2 * k, n_d)
+        arrival = pltpu.make_async_copy(dp_out.at[slot], dp_out.at[slot], dp_recv.at[0, k])
+        arrival.wait()
+        waits.append(remote(dp_out.at[slot], dp_out.at[slot], dp_send.at[1, k],
+                            dp_recv.at[1, k], {"dp": pair}))
+    for copy in waits:
+        copy.wait_send()
+    pltpu.make_async_copy(dp_out.at[r], dp_out.at[r], dp_recv.at[0, 0]).wait()
+    for k in range(1, peers):
+        slot = lax.rem(pair + n_d - 2 * k, n_d)
+        pltpu.make_async_copy(dp_out.at[slot], dp_out.at[slot], dp_recv.at[1, k]).wait()
+    own_t.wait()
+    own_d.wait()
+
+
+def gather_start(pieces, weights, ring):
+    n_t = lax.axis_size("tensor")
+    n_d = lax.axis_size("dp")
+    moved = 2 * (n_t * pieces.size * pieces.dtype.itemsize + n_d * weights.size * weights.dtype.itemsize)
+    return pl.pallas_call(
+        functools.partial(_gather_start_body, ring),
+        out_shape=[
+            jax.ShapeDtypeStruct((n_t,) + pieces.shape, pieces.dtype),
+            jax.ShapeDtypeStruct((n_d,) + weights.shape, weights.dtype),
+        ],
+        in_specs=[pl.BlockSpec(memory_space=pl.ANY)] * 2,
+        out_specs=[pl.BlockSpec(memory_space=pl.ANY)] * 2,
+        scratch_shapes=[
+            pltpu.SemaphoreType.DMA((2, ring // 2, 2)),
+            pltpu.SemaphoreType.DMA((2, ring // 2, 2)),
+            pltpu.SemaphoreType.DMA((2,)),
+            pltpu.SemaphoreType.DMA((2, n_d // 2)),
+            pltpu.SemaphoreType.DMA((2, n_d // 2)),
+            pltpu.SemaphoreType.DMA((2,)),
+        ],
+        compiler_params=pltpu.CompilerParams(collective_id=0, has_side_effects=True),
+        cost_estimate=pl.CostEstimate(flops=0, transcendentals=0, bytes_accessed=moved),
+    )(pieces, weights)
+
+
 def local(tokens, norm_gain, query_weight, kv_weight, out_weight, grad_out, doc_lengths):
     tensor_size = lax.axis_size("tensor")
     data_size = lax.axis_size("dp")
@@ -116,14 +223,13 @@
     gain32 = norm_gain.astype(jnp.float32)
     normed_local = (unit * gain32).astype(jnp.bfloat16)
     rows = tokens.shape[0]
-    normed_parts, grad_parts = push_exchange(
-        [("tensor", tensor_size, normed_local, False), ("tensor", tensor_size, grad_out, False)], 0
-    )
-    normed = normed_parts.reshape(tensor_size * rows, -1)
-    grad_full = grad_parts.reshape(tensor_size * rows, -1)
+    pieces = jnp.stack([normed_local, grad_out])
+    weights_local = jnp.concatenate([query_weight, kv_weight, out_weight.T], axis=1)
+    tens_parts, weight_parts = gather_start(pieces, weights_local, RING)
+    normed = tens_parts[:, 0].reshape(tensor_size * rows, -1)
+    grad_full = tens_parts[:, 1].reshape(tensor_size * rows, -1)
     seq_length = normed.shape[0]
-    weights_local = jnp.concatenate([query_weight, kv_weight, out_weight.T], axis=1)
-    weights_full = lax.all_gather(weights_local, "dp", axis=0, tiled=True)
+    weights_full = weight_parts.reshape(-1, weights_local.shape[1])
     query_full = weights_full[:, :query_width]
     kv_local = weights_full[:, query_width : query_width + kv_width]
     out_full_t = weights_full[:, query_width + kv_width :]

time: 276 us -> 259 us (0.938); the launches traced: 270 us -> 258 us
  between operations: 14.3 us -> 0.88 us
  local copies, waits for them, and re-layouts: 5.17 us -> 9.68 us
  Pallas kernels: 205 us -> 201 us
    pallas_call x2 -> x1, Pallas kernels: 205 us -> 92.8 us  [push_exchange(): pl.pallas_call(functools.partial(_push_body, plan), out_shape=out_shape,...]
    pallas_call x0 -> x1, Pallas kernels: none -> 109 us  [gather_start(): pl.pallas_call(functools.partial(_gather_start_body, ring), out_shape=[ja...]
    ppermute x4, waiting for transfers between devices: 2.55 us -> 6.84 us  [partner_2(): return lax.ppermute(value, axis, pairs)]
  transfers between devices with their start and end apart: 5 -> 4, of which waited for: 3 -> 3; matrix products, arithmetic and copies ran while one was open for 5% -> 3% of each run, Pallas kernels for 41% -> 0%
where the time goes in v3:
time: 259 us; the launch traced here: 258 us
  Pallas kernels  201 us (78%)
  matrix products  17.6 us (7%)
  starting transfers between devices  10.9 us (4%)
  other arithmetic  10.4 us (4%)
  local copies, waits for them, and re-layouts  9.68 us (4%)
  waiting for transfers between devices  6.84 us (3%)
    pallas_call x1, Pallas kernels, gather_start(): pl.pallas_call(functools.partial(_gather_start_body, ring), out_shape=[ja...  109 us
    pallas_call x1, Pallas kernels, push_exchange(): pl.pallas_call(functools.partial(_push_body, plan), out_shape=out_shape,...  92.8 us
    ppermute x4, starting transfers between devices, partner_2(): return lax.ppermute(value, axis, pairs)  10.9 us
    ppermute x4, waiting for transfers between devices, partner_2(): return lax.ppermute(value, axis, pairs)  6.84 us
  transfers between devices with their start and end apart: 4, of which 3 were waited for; matrix products, arithmetic and copies ran while one was open for 3% of the time, Pallas kernels for 0%

profile of v3, /device:TPU:1, one launch (start us, length us, event | category | flops | bytes accessed | tf_op | source)
XLA Modules:
  0.0 257.7 jit_solution(3863863823744519013)
XLA Ops:
  1.3 1.0 fusion.29
  4.2 1.0 fusion.37
  5.2 1.6 pad_maximum_fusion.pieces_ref
  6.8 1.6 pad_maximum_fusion.1.weights_ref
  8.4 108.6 %shard_map.94 = (bf16[16,2,16,4096]{3,2,1,0:T(8,128)(2,1)}, bf16[32,128,576]{2,1,0:T(8,128)(2,1)}) custom-call(bf16[2,16,4096]{2,1,0:T(8,128)(2,1)} %pad_maximum_fusion.pieces_ref, bf16[128,576]{1,0:T(8,128)(2,1)} %pad_maximum_fusion.1.weights_ref), custom_call_target="tpu_custom_call" | custom-call | bytes 17825792 | tf_op jit(solution)/shard_map/pallas_call | solution.py:190
  117.1 2.7 %fusion.55 = (bf16[16,1,16,4096]{3,2,1,0:T(8,128)(2,1)S(1)}, bf16[16,1,16,4096]{3,2,1,0:T(8,128)(2,1)S(1)}) fusion(bf16[16,2,16,4096]{3,2,1,0:T(8,128)(2,1)} %get-tuple-element.7), kind=kLoop, calls=%fused_computation.78 | loop fusion | bytes 8388608 | tf_op jit(solution)/shard_map/slice | solution.py:229
  121.6 3.1 %collective-permute-start = (bf16[256,64]{0,1:T(8,128)(2,1)S(1)}, bf16[256,64]{0,1:T(8,128)(2,1)S(1)}, u32[]{:S(2)}, u32[]{:S(2)}) collective-permute-start(bf16[256,64]{0,1:T(8,128)(2,1)S(1)} %convolution_convert_fusion.2), channel_id=1, source_target_pairs={{0,1},{1,0},{2,3},{3,2},{4,5},{5,4},{6,7},{7,6},{8,9},{9,8},{10,11... | collective-permute-start | bytes 98312 | tf_op jit(solution)/shard_map/ppermute | solution.py:23
  124.7 1.0 fusion.17
  125.7 1.9 fusion.20
  127.9 4.0 %collective-permute-start.1 = (bf16[256,128]{0,1:T(8,128)(2,1)S(1)}, bf16[256,128]{0,1:T(8,128)(2,1)S(1)}, u32[]{:S(2)}, u32[]{:S(2)}) collective-permute-start(bf16[256,128]{0,1:T(8,128)(2,1)S(1)} %pad_maximum_fusion.2), channel_id=1, source_target_pairs={{0,2},{1,3},{2,0},{3,1},{4,6},{5,7},{6,4},{7,5},{8,10},{9,11},{10,... | collective-permute-start | bytes 196616 | tf_op jit(solution)/shard_map/ppermute | solution.py:23
  132.0 4.0 %collective-permute-done.1 = bf16[256,128]{0,1:T(8,128)(2,1)S(1)} collective-permute-done((bf16[256,128]{0,1:T(8,128)(2,1)S(1)}, bf16[256,128]{0,1:T(8,128)(2,1)S(1)}, u32[]{:S(2)}, u32[]{:S(2)}) %collective-permute-start.1) | collective-permute-done | bytes 65568 | tf_op jit(solution)/shard_map/ppermute | solution.py:23
  136.0 1.1 fusion.56
  137.2 1.3 convolution_bitcast_fusion.2
  138.7 1.5 select_convert_fusion
  140.2 1.9 collective-permute-start.2
  142.2 1.5 convolution_convert_fusion.1
  143.7 2.5 collective-permute-done.2
  146.2 1.9 collective-permute-start.3
  148.1 2.4 fusion.5
  150.9 2.4 convolution_convert_fusion
  153.3 3.5 %fusion.2 = bf16[256,4096]{1,0:T(8,128)(2,1)} fusion(f32[256,4096]{1,0:T(8,128)S(1)} %fusion.5, bf16[256,64]{0,1:T(8,128)(2,1)S(1)} %add_convert_fusion.1, bf16[4096,576]{1,0:T(8,128)(2,1)} %bitcast.63), kind=kOutput, calls=%fused_computation.5 | convolution fusion | flops 136314880 | bytes 7372800 | tf_op jit(solution)/shard_map/dot_general | solution.py:289
  156.8 2.8 %copy.41 = bf16[4096,320]{1,0:T(8,128)(2,1)} copy(bf16[4096,320]{0,1:T(8,128)(2,1)S(1)} %copy-done) | data formatting | bytes 5242880 | tf_op jit(solution)/shard_map/convert_element_type | solution.py:294
  159.6 92.8 %shard_map.95 = (bf16[16,16,4096]{2,1,0:T(8,128)(2,1)}, bf16[32,128,320]{2,1,0:T(8,128)(2,1)}) custom-call(bf16[16,16,4096]{2,1,0:T(8,128)(2,1)} %bitcast.61, bf16[32,128,320]{2,1,0:T(8,128)(2,1)} %bitcast.60), custom_call_target="tpu_custom_call" | custom-call | bytes 9437184 | tf_op jit(solution)/shard_map/pallas_call | solution.py:92
  252.4 2.6 convert_reduce_fusion
  (37 shorter events, 8.1 us)
Async XLA Ops:
  117.1 3.8 %copy-start.1 = (bf16[32,128,576]{2,1,0:T(8,128)(2,1)S(1)}, bf16[32,128,576]{2,1,0:T(8,128)(2,1)}, u32[]{:S(2)}) copy-start(bf16[32,128,576]{2,1,0:T(8,128)(2,1)} %get-tuple-element.8) | copy-start | bytes 14155780
  121.6 6.3 %collective-permute-start = (bf16[256,64]{0,1:T(8,128)(2,1)S(1)}, bf16[256,64]{0,1:T(8,128)(2,1)S(1)}, u32[]{:S(2)}, u32[]{:S(2)}) collective-permute-start(bf16[256,64]{0,1:T(8,128)(2,1)S(1)} %convolution_convert_fusion.2), channel_id=1, source_target_pairs={{0,1},{1,0},{2,3},{3,2},{4,5},{5,4},{6,7},{7,6},{8,9},{9,8},{10,11... | collective-permute-start | bytes 98312 | tf_op jit(solution)/shard_map/ppermute | solution.py:23
  125.7 1.9 copy-start.5
  127.9 8.1 %collective-permute-start.1 = (bf16[256,128]{0,1:T(8,128)(2,1)S(1)}, bf16[256,128]{0,1:T(8,128)(2,1)S(1)}, u32[]{:S(2)}, u32[]{:S(2)}) collective-permute-start(bf16[256,128]{0,1:T(8,128)(2,1)S(1)} %pad_maximum_fusion.2), channel_id=1, source_target_pairs={{0,2},{1,3},{2,0},{3,1},{4,6},{5,7},{6,4},{7,5},{8,10},{9,11},{10,... | collective-permute-start | bytes 196616 | tf_op jit(solution)/shard_map/ppermute | solution.py:23
  140.2 5.9 %collective-permute-start.2 = (bf16[256,128]{0,1:T(8,128)(2,1)S(1)}, bf16[256,128]{0,1:T(8,128)(2,1)S(1)}, u32[]{:S(2)}, u32[]{:S(2)}) collective-permute-start(bf16[256,128]{0,1:T(8,128)(2,1)S(1)} %get-tuple-element.26), channel_id=1, source_target_pairs={{0,2},{1,3},{2,0},{3,1},{4,6},{5,7},{6,4},{7,5},{8,10},{9,11},{10,... | collective-permute-start | bytes 196616 | tf_op jit(solution)/shard_map/ppermute | solution.py:23
  146.2 4.7 %collective-permute-start.3 = (bf16[256,64]{0,1:T(8,128)(2,1)S(1)}, bf16[256,64]{0,1:T(8,128)(2,1)S(1)}, u32[]{:S(2)}, u32[]{:S(2)}) collective-permute-start(bf16[256,64]{0,1:T(8,128)(2,1)S(1)} %select_convert_fusion.1), channel_id=1, source_target_pairs={{0,1},{1,0},{2,3},{3,2},{4,5},{5,4},{6,7},{7,6},{8,9},{9,8},{10,11... | collective-permute-start | bytes 98312 | tf_op jit(solution)/shard_map/ppermute | solution.py:23
  153.3 3.5 %copy-start = (bf16[4096,320]{0,1:T(8,128)(2,1)S(1)}, bf16[4096,320]{0,1:T(8,128)(2,1)}, u32[]{:S(2)}) copy-start(bf16[4096,320]{0,1:T(8,128)(2,1)} %convolution_convert_fusion) | copy-start | bytes 7864324
  252.4 3.3 %copy-start.2 = (bf16[16,16,4096]{2,1,0:T(8,128)(2,1)S(1)}, bf16[16,16,4096]{2,1,0:T(8,128)(2,1)}, u32[]{:S(2)}) copy-start(bf16[16,16,4096]{2,1,0:T(8,128)(2,1)} %get-tuple-element.9) | copy-start | bytes 6291460
  252.4 3.6 %copy-start.3 = (bf16[16,4096]{1,0:T(8,128)(2,1)S(1)}, bf16[16,4096]{1,0:T(8,128)(2,1)}, u32[]{:S(2)}) copy-start(bf16[16,4096]{1,0:T(8,128)(2,1)} %param.7) | copy-start | bytes 393220
  252.4 3.8 %copy-start.4 = (bf16[16,4096]{1,0:T(8,128)(2,1)S(1)}, bf16[16,4096]{1,0:T(8,128)(2,1)}, u32[]{:S(2)}) copy-start(bf16[16,4096]{1,0:T(8,128)(2,1)} %param.12) | copy-start | bytes 393220

commit v4 on v3

--- a/solution.py
+++ b/solution.py
@@ -15,12 +15,6 @@
 
 
 epsilon = 1e-05
-
-
-def partner_2(value, axis, bit):
-    mask = 2**bit
-    pairs = [(source, source ^ mask) for source in range(lax.axis_size(axis))]
-    return lax.ppermute(value, axis, pairs)
 
 
 def document_mask(lengths, length_total):
@@ -40,25 +34,32 @@
     barrier = pltpu.get_barrier_semaphore()
     mine = []
     expected = 0
-    for axis, n, _ in plan:
-        me = lax.axis_index(axis)
+    places = []
+    for axis, n, _, stride in plan:
+        index = lax.axis_index(axis)
+        me = lax.rem(index // stride, n)
+        offset = index - me * stride
         mine.append(me)
+        places.append(functools.partial(lambda o, st, p: o + p * st, offset, stride))
         for j in range(1, n):
             pl.semaphore_signal(
-                barrier, inc=1, device_id={axis: lax.rem(me + j, n)}, device_id_type=MESH_ID
+                barrier,
+                inc=1,
+                device_id={axis: places[-1](lax.rem(me + j, n))},
+                device_id_type=MESH_ID,
             )
         expected += n - 1
     pl.semaphore_wait(barrier, expected)
     local = []
-    for g, (axis, n, scatter) in enumerate(plan):
+    for g, (axis, n, scatter, _) in enumerate(plan):
         me = mine[g]
         src = ins[g].at[me] if scatter else ins[g]
         copy = pltpu.make_async_copy(src, outs[g].at[me], local_sem.at[g])
         copy.start()
         local.append(copy)
     remote = []
-    for j in range(1, max(n for _, n, _ in plan)):
-        for g, (axis, n, scatter) in enumerate(plan):
+    for j in range(1, max(n for _, n, _, _ in plan)):
+        for g, (axis, n, scatter, _) in enumerate(plan):
             if j >= n:
                 continue
             me = mine[g]
@@ -68,7 +69,7 @@
                 dst_ref=outs[g].at[me],
                 send_sem=send_sems[g].at[j],
                 recv_sem=recv_sems[g].at[j],
-                device_id={axis: peer},
+                device_id={axis: places[g](peer)},
                 device_id_type=MESH_ID,
             )
             copy.start()
@@ -80,11 +81,12 @@
 
 
 def push_exchange(groups, cid):
-    plan = tuple((axis, n, scatter) for axis, n, _, scatter in groups)
-    arrays = [array for _, _, array, _ in groups]
+    groups = [g if len(g) == 5 else g + (1,) for g in groups]
+    plan = tuple((axis, n, scatter, stride) for axis, n, _, scatter, stride in groups)
+    arrays = [array for _, _, array, _, _ in groups]
     out_shape = []
     moved = 0
-    for _, n, array, scatter in groups:
+    for _, n, array, scatter, _ in groups:
         shape = array.shape if scatter else (n,) + array.shape
         out_shape.append(jax.ShapeDtypeStruct(shape, array.dtype))
         moved += 2 * math.prod(shape) * array.dtype.itemsize
@@ -94,15 +96,15 @@
         out_shape=out_shape,
         in_specs=[pl.BlockSpec(memory_space=pl.ANY)] * count,
         out_specs=[pl.BlockSpec(memory_space=pl.ANY)] * count,
-        scratch_shapes=[pltpu.SemaphoreType.DMA((n,)) for _, n, _, _ in groups]
-        + [pltpu.SemaphoreType.DMA((n,)) for _, n, _, _ in groups]
+        scratch_shapes=[pltpu.SemaphoreType.DMA((n,)) for _, n, _, _, _ in groups]
+        + [pltpu.SemaphoreType.DMA((n,)) for _, n, _, _, _ in groups]
         + [pltpu.SemaphoreType.DMA((count,))],
         compiler_params=pltpu.CompilerParams(collective_id=cid, has_side_effects=True),
         cost_estimate=pl.CostEstimate(flops=0, transcendentals=0, bytes_accessed=moved),
     )(*arrays)
 
 
-def _gather_start_body(ring, pieces_ref, weights_ref, tens_out, dp_out, ring_send, ring_recv,
+def _gather_start_body(ring, chunks, pieces_ref, weights_ref, tens_out, dp_out, ring_send, ring_recv,
                        cross_sem, dp_send, dp_recv, local_sem):
     n_t = lax.axis_size("tensor")
     n_d = lax.axis_size("dp")
@@ -160,8 +162,12 @@
             for h, start in enumerate((base, other)):
                 slot = start + origin
                 src = pieces_ref if (s == 0 and h == 0) else tens_out.at[slot]
-                sent.append(remote(src, tens_out.at[slot], ring_send.at[d, s, h],
-                                   ring_recv.at[d, s, h], {"tensor": target}))
+                step = src.shape[0] // chunks
+                for c in range(chunks):
+                    part = pl.ds(c * step, step)
+                    sent.append(remote(src.at[part], tens_out.at[slot].at[part],
+                                       ring_send.at[d, s, h * chunks + c],
+                                       ring_recv.at[d, s, h * chunks + c], {"tensor": target}))
             waits.extend(sent)
             moving[d] = sent
     for d in range(2):
@@ -183,12 +189,12 @@
     own_d.wait()
 
 
-def gather_start(pieces, weights, ring):
+def gather_start(pieces, weights, ring, chunks=1):
     n_t = lax.axis_size("tensor")
     n_d = lax.axis_size("dp")
     moved = 2 * (n_t * pieces.size * pieces.dtype.itemsize + n_d * weights.size * weights.dtype.itemsize)
     return pl.pallas_call(
-        functools.partial(_gather_start_body, ring),
+        functools.partial(_gather_start_body, ring, chunks),
         out_shape=[
             jax.ShapeDtypeStruct((n_t,) + pieces.shape, pieces.dtype),
             jax.ShapeDtypeStruct((n_d,) + weights.shape, weights.dtype),
@@ -196,8 +202,8 @@
         in_specs=[pl.BlockSpec(memory_space=pl.ANY)] * 2,
         out_specs=[pl.BlockSpec(memory_space=pl.ANY)] * 2,
         scratch_shapes=[
-            pltpu.SemaphoreType.DMA((2, ring // 2, 2)),
-            pltpu.SemaphoreType.DMA((2, ring // 2, 2)),
+            pltpu.SemaphoreType.DMA((2, ring // 2, 2 * chunks)),
+            pltpu.SemaphoreType.DMA((2, ring // 2, 2 * chunks)),
             pltpu.SemaphoreType.DMA((2,)),
             pltpu.SemaphoreType.DMA((2, n_d // 2)),
             pltpu.SemaphoreType.DMA((2, n_d // 2)),
@@ -211,9 +217,7 @@
 def local(tokens, norm_gain, query_weight, kv_weight, out_weight, grad_out, doc_lengths):
     tensor_size = lax.axis_size("tensor")
     data_size = lax.axis_size("dp")
-    tensor_index = lax.axis_index("tensor")
     sharers = tensor_size // KVH
-    levels = sharers.bit_length() - 1
     contract_last = (((1,), (1,)), ((), ()))
     query_width = query_weight.shape[1]
     kv_width = kv_weight.shape[1]
@@ -224,7 +228,8 @@
     normed_local = (unit * gain32).astype(jnp.bfloat16)
     rows = tokens.shape[0]
     pieces = jnp.stack([normed_local, grad_out])
-    weights_local = jnp.concatenate([query_weight, kv_weight, out_weight.T], axis=1)
+    weights_local = jnp.concatenate([query_weight, kv_weight], axis=1)
+    out_full_t = lax.all_gather(out_weight.T, "dp", axis=0, tiled=True)
     tens_parts, weight_parts = gather_start(pieces, weights_local, RING)
     normed = tens_parts[:, 0].reshape(tensor_size * rows, -1)
     grad_full = tens_parts[:, 1].reshape(tensor_size * rows, -1)
@@ -232,19 +237,10 @@
     weights_full = weight_parts.reshape(-1, weights_local.shape[1])
     query_full = weights_full[:, :query_width]
     kv_local = weights_full[:, query_width : query_width + kv_width]
-    out_full_t = weights_full[:, query_width + kv_width :]
     queries = jnp.dot(normed, query_full, preferred_element_type=jnp.float32).astype(jnp.bfloat16)
     keyvals = jnp.dot(normed, kv_local, preferred_element_type=jnp.float32).astype(jnp.bfloat16)
-    for bit_index in range(levels):
-        partner = partner_2(keyvals, "tensor", bit_index)
-        joined_upper_half = tensor_index >> bit_index & 1 == 1
-        keyvals = jnp.concatenate(
-            [
-                jnp.where(joined_upper_half, partner, keyvals),
-                jnp.where(joined_upper_half, keyvals, partner),
-            ],
-            axis=1,
-        )
+    (shared,) = push_exchange([("tensor", sharers, keyvals, False)], 2)
+    keyvals = jnp.moveaxis(shared, 0, 1).reshape(seq_length, sharers * kv_width)
     key_rows = keyvals[:, :HD]
     value_rows = keyvals[:, HD:]
     out_grad = jnp.dot(grad_full, out_full_t, preferred_element_type=jnp.float32).astype(
@@ -272,17 +268,9 @@
     )
     value_part = jnp.einsum("hqt,qhd->td", probs_low, out_heads, preferred_element_type=jnp.float32)
     kv_partial = jnp.concatenate([key_part, value_part], axis=1)
-    for bit_index in reversed(range(levels)):
-        half_cols = kv_partial.shape[1] // 2
-        upper_half = tensor_index >> bit_index & 1 == 1
-        lower_cols = kv_partial[:, :half_cols]
-        higher_cols = kv_partial[:, half_cols:]
-        kept = jnp.where(upper_half, higher_cols, lower_cols)
-        handed = jnp.where(upper_half, lower_cols, higher_cols)
-        kv_partial = kept + partner_2(handed.astype(jnp.bfloat16), "tensor", bit_index).astype(
-            handed.dtype
-        )
-    kv_grad = kv_partial.astype(jnp.bfloat16)
+    blocks = jnp.moveaxis(kv_partial.reshape(seq_length, sharers, kv_width), 1, 0)
+    (kv_arrived,) = push_exchange([("tensor", sharers, blocks.astype(jnp.bfloat16), True)], 3)
+    kv_grad = jnp.sum(kv_arrived.astype(jnp.float32), axis=0).astype(jnp.bfloat16)
     from_query = lax.dot_general(
         query_grad, query_full, contract_last, preferred_element_type=jnp.float32
     )

time: 259 us -> 274 us (1.058)
  between operations: 0.88 us -> 14.2 us
  starting transfers between devices: 10.9 us -> 0.04 us
  Pallas kernels: 201 us -> 209 us
  waiting for transfers between devices: 6.84 us -> 0.68 us
  matrix products: 17.6 us -> 23.6 us
  local copies, waits for them, and re-layouts: 9.68 us -> 13.4 us
    pallas_call x1 -> x3, Pallas kernels: 92.8 us -> 110 us  [push_exchange(): pl.pallas_call(functools.partial(_push_body, plan), out_shape=out_shape,...]
    ppermute x4 -> x0, starting transfers between devices: 10.9 us -> none  [partner_2(): return lax.ppermute(value, axis, pairs)]
    pallas_call x1, Pallas kernels: 109 us -> 98.8 us  [gather_start(): pl.pallas_call(functools.partial(_gather_start_body, ring, chunks), out_s...]
    ppermute x4 -> x0, waiting for transfers between devices: 6.84 us -> none  [partner_2(): return lax.ppermute(value, axis, pairs)]
  transfers between devices with their start and end apart: 4 -> 1, of which waited for: 3 -> 0; matrix products, arithmetic and copies ran while one was open for 3% -> 7% of each run, Pallas kernels for 0% -> 40%
where the time goes in v4:
time: 274 us; the launch traced here: 272 us
  Pallas kernels  209 us (76%)
  matrix products  23.6 us (9%)
  between operations  14.2 us (5%)
  local copies, waits for them, and re-layouts  13.4 us (5%)
  other arithmetic  11.2 us (4%)
    pallas_call x3, Pallas kernels, push_exchange(): pl.pallas_call(functools.partial(_push_body, plan), out_shape=out_shape,...  110 us
    pallas_call x1, Pallas kernels, gather_start(): pl.pallas_call(functools.partial(_gather_start_body, ring, chunks), out_s...  98.8 us
  transfers between devices with their start and end apart: 1, of which 0 were waited for; matrix products, arithmetic and copies ran while one was open for 7% of the time, Pallas kernels for 40%

profile of v4, /device:TPU:1, one launch (start us, length us, event | category | flops | bytes accessed | tf_op | source)
XLA Modules:
  0.0 272.3 jit_solution(5911817717593412625)
XLA Ops:
  8.6 0.8 copy.64
  9.4 1.5 pad_maximum_fusion.2.weights_ref
  10.9 1.0 fusion.26
  12.0 1.0 fusion.34
  13.0 1.6 pad_maximum_fusion.pieces_ref
  14.6 98.8 %shard_map.94 = (bf16[16,2,16,4096]{3,2,1,0:T(8,128)(2,1)}, bf16[32,128,320]{2,1,0:T(8,128)(2,1)}) custom-call(bf16[2,16,4096]{2,1,0:T(8,128)(2,1)} %pad_maximum_fusion.pieces_ref, bf16[128,320]{1,0:T(8,128)(2,1)} %pad_maximum_fusion.2.weights_ref), custom_call_target="tpu_custom_call" | custom-call | bytes 13631488 | tf_op jit(solution)/shard_map/pallas_call | solution.py:196
  113.5 3.9 %fusion.43 = (bf16[16,1,16,4096]{3,2,1,0:T(8,128)(2,1)S(1)}, bf16[16,1,16,4096]{3,2,1,0:T(8,128)(2,1)}) fusion(bf16[16,2,16,4096]{3,2,1,0:T(8,128)(2,1)} %get-tuple-element.7), kind=kLoop, calls=%fused_computation.68 | loop fusion | bytes 8388608 | tf_op jit(solution)/shard_map/slice | solution.py:234
  117.4 2.0 convolution_convert_fusion.3
  120.2 8.8 %shard_map.95 = bf16[4,256,64]{2,1,0:T(8,128)(2,1)} custom-call(bf16[256,64]{1,0:T(8,128)(2,1)} %copy.65.refs_0_), custom_call_target="tpu_custom_call" | custom-call | bytes 262144 | tf_op jit(solution)/shard_map/pallas_call | solution.py:94
  129.0 1.1 copy.66
  130.5 2.5 fusion.14
  133.0 1.1 fusion.44
  134.1 3.0 %convolution_convert_fusion.2 = bf16[256,256]{0,1:T(8,128)(2,1)S(1)} fusion(bf16[256,4096]{1,0:T(8,128)(2,1)} %bitcast.86, bf16[4096,256]{0,1:T(8,128)(2,1)} %all-gather.2.cloned.1.call-done), kind=kOutput, calls=%fused_computation.22 | convolution fusion | flops 536936448 | bytes 4325376 | tf_op jit(solution)/shard_map/dot_general | solution.py:246
  137.9 1.5 fusion.17
  139.4 1.5 convolution_convert_fusion.1
  141.0 0.8 copy.75
  141.8 7.9 %shard_map.96 = bf16[4,256,64]{2,1,0:T(8,128)(2,1)} custom-call(bf16[4,256,64]{2,1,0:T(8,128)(2,1)} %bitcast.88), custom_call_target="tpu_custom_call" | custom-call | bytes 262144 | tf_op jit(solution)/shard_map/pallas_call | solution.py:94
  149.7 1.0 reduce_sum.79
  150.8 3.9 %fusion.23 = f32[256,4096]{1,0:T(8,128)} fusion(bf16[256,64]{1,0:T(8,128)(2,1)S(1)} %reduce_sum.79, bf16[4096,320]{1,0:T(8,128)(2,1)} %bitcast.84), kind=kOutput, calls=%fused_computation.31 | convolution fusion | flops 134217728 | bytes 5275648 | tf_op jit(solution)/shard_map/dot_general | solution.py:277
  154.7 5.0 %fusion.2 = bf16[256,4096]{1,0:T(8,128)(2,1)} fusion(f32[256,4096]{1,0:T(8,128)} %fusion.23, bf16[256,256]{0,1:T(8,128)(2,1)S(1)} %bitcast.89, bf16[4096,320]{1,0:T(8,128)(2,1)} %bitcast.85), kind=kOutput, calls=%fused_computation.5 | convolution fusion | flops 538968064 | bytes 8519680 | tf_op jit(solution)/shard_map/dot_general | solution.py:274
  159.7 2.4 convolution_convert_fusion
  162.1 4.5 %copy.77 = bf16[4096,320]{1,0:T(8,128)(2,1)} copy(bf16[4096,320]{0,1:T(8,128)(2,1)} %convolution_convert_fusion) | data formatting | bytes 5242880 | tf_op jit(solution)/shard_map/convert_element_type | solution.py:282
  166.6 93.5 %shard_map.97 = (bf16[16,16,4096]{2,1,0:T(8,128)(2,1)}, bf16[32,128,320]{2,1,0:T(8,128)(2,1)}) custom-call(bf16[16,16,4096]{2,1,0:T(8,128)(2,1)} %bitcast.81, bf16[32,128,320]{2,1,0:T(8,128)(2,1)} %bitcast.80), custom_call_target="tpu_custom_call" | custom-call | bytes 9437184 | tf_op jit(solution)/shard_map/pallas_call | solution.py:94
  260.2 2.6 convert_reduce_fusion
  (29 shorter events, 6.2 us)
Async XLA Ops:
  7.2 127.0 %all-gather.2.cloned.1.call-start = ((), (), s32[]{:S(2)}) async-start(), calls=%async_computation | async-start | bytes 2162688 | tf_op jit(solution)/shard_map/all_gather | solution.py:232
  117.4 12.7 %copy-start.3 = (s32[1,4]{1,0:T(1,128)S(1)}, s32[1,4]{1,0:T(1,128)}, u32[]{:S(2)}) copy-start(s32[1,4]{1,0:T(1,128)} %param.13) | copy-start | bytes 52
  260.2 3.3 %copy-start = (bf16[16,16,4096]{2,1,0:T(8,128)(2,1)S(1)}, bf16[16,16,4096]{2,1,0:T(8,128)(2,1)}, u32[]{:S(2)}) copy-start(bf16[16,16,4096]{2,1,0:T(8,128)(2,1)} %get-tuple-element.9) | copy-start | bytes 6291460
  262.7 1.0 copy-start.1
  262.7 1.3 copy-start.2
Sparse Core Ops, SparseCore 0:
  10.1 90.1 all-gather.1

commit v5 on v3

--- a/solution.py
+++ b/solution.py
@@ -40,25 +40,32 @@
     barrier = pltpu.get_barrier_semaphore()
     mine = []
     expected = 0
-    for axis, n, _ in plan:
-        me = lax.axis_index(axis)
+    places = []
+    for axis, n, _, stride in plan:
+        index = lax.axis_index(axis)
+        me = lax.rem(index // stride, n)
+        offset = index - me * stride
         mine.append(me)
+        places.append(functools.partial(lambda o, st, p: o + p * st, offset, stride))
         for j in range(1, n):
             pl.semaphore_signal(
-                barrier, inc=1, device_id={axis: lax.rem(me + j, n)}, device_id_type=MESH_ID
+                barrier,
+                inc=1,
+                device_id={axis: places[-1](lax.rem(me + j, n))},
+                device_id_type=MESH_ID,
             )
         expected += n - 1
     pl.semaphore_wait(barrier, expected)
     local = []
-    for g, (axis, n, scatter) in enumerate(plan):
+    for g, (axis, n, scatter, _) in enumerate(plan):
         me = mine[g]
         src = ins[g].at[me] if scatter else ins[g]
         copy = pltpu.make_async_copy(src, outs[g].at[me], local_sem.at[g])
         copy.start()
         local.append(copy)
     remote = []
-    for j in range(1, max(n for _, n, _ in plan)):
-        for g, (axis, n, scatter) in enumerate(plan):
+    for j in range(1, max(n for _, n, _, _ in plan)):
+        for g, (axis, n, scatter, _) in enumerate(plan):
             if j >= n:
                 continue
             me = mine[g]
@@ -68,7 +75,7 @@
                 dst_ref=outs[g].at[me],
                 send_sem=send_sems[g].at[j],
                 recv_sem=recv_sems[g].at[j],
-                device_id={axis: peer},
+                device_id={axis: places[g](peer)},
                 device_id_type=MESH_ID,
             )
             copy.start()
@@ -80,11 +87,12 @@
 
 
 def push_exchange(groups, cid):
-    plan = tuple((axis, n, scatter) for axis, n, _, scatter in groups)
-    arrays = [array for _, _, array, _ in groups]
+    groups = [g if len(g) == 5 else g + (1,) for g in groups]
+    plan = tuple((axis, n, scatter, stride) for axis, n, _, scatter, stride in groups)
+    arrays = [array for _, _, array, _, _ in groups]
     out_shape = []
     moved = 0
-    for _, n, array, scatter in groups:
+    for _, n, array, scatter, _ in groups:
         shape = array.shape if scatter else (n,) + array.shape
         out_shape.append(jax.ShapeDtypeStruct(shape, array.dtype))
         moved += 2 * math.prod(shape) * array.dtype.itemsize
@@ -94,8 +102,8 @@
         out_shape=out_shape,
         in_specs=[pl.BlockSpec(memory_space=pl.ANY)] * count,
         out_specs=[pl.BlockSpec(memory_space=pl.ANY)] * count,
-        scratch_shapes=[pltpu.SemaphoreType.DMA((n,)) for _, n, _, _ in groups]
-        + [pltpu.SemaphoreType.DMA((n,)) for _, n, _, _ in groups]
+        scratch_shapes=[pltpu.SemaphoreType.DMA((n,)) for _, n, _, _, _ in groups]
+        + [pltpu.SemaphoreType.DMA((n,)) for _, n, _, _, _ in groups]
         + [pltpu.SemaphoreType.DMA((count,))],
         compiler_params=pltpu.CompilerParams(collective_id=cid, has_side_effects=True),
         cost_estimate=pl.CostEstimate(flops=0, transcendentals=0, bytes_accessed=moved),
@@ -292,9 +300,18 @@
     weight_partial = lax.dot_general(
         normed, combined, (((0,), (0,)), ((), ())), preferred_element_type=jnp.float32
     ).astype(jnp.bfloat16)
-    weight_partial = weight_partial.reshape(data_size, -1, weight_partial.shape[1])
+    weight_partial = weight_partial.reshape(data_size // 2, 2, -1, weight_partial.shape[1])
+    parity = lax.rem(lax.axis_index("dp"), 2)
+    kept = jnp.where(parity == 0, weight_partial[:, 0], weight_partial[:, 1])
+    handed = jnp.where(parity == 0, weight_partial[:, 1], weight_partial[:, 0])
+    swapped = lax.ppermute(handed, "dp", [(i, i ^ 1) for i in range(data_size)])
+    paired = (kept.astype(jnp.float32) + swapped.astype(jnp.float32)).astype(jnp.bfloat16)
     arrived, weight_arrived = push_exchange(
-        [("tensor", tensor_size, partial, True), ("dp", data_size, weight_partial, True)], 1
+        [
+            ("tensor", tensor_size, partial, True),
+            ("dp", data_size // 2, paired, True, 2),
+        ],
+        1,
     )
     normed_grad = jnp.sum(arrived.astype(jnp.float32), axis=0)
     scaled = normed_grad * gain32

time: 259 us -> 262 us (1.012)
  Pallas kernels: 201 us -> 170 us
  local copies, waits for them, and re-layouts: 9.68 us -> 32.3 us
  starting transfers between devices: 10.9 us -> 16.2 us
  other arithmetic: 10.4 us -> 14.3 us
    pallas_call x1, Pallas kernels: 92.8 us -> 61.8 us  [push_exchange(): pl.pallas_call(functools.partial(_push_body, plan), out_shape=out_shape,...]
    unnamed x15 -> x17, local copies, waits for them, and re-layouts: 3.48 us -> 14.3 us
    ppermute x0 -> x1, starting transfers between devices: none -> 5.33 us  [local(): swapped = lax.ppermute(handed, 'dp', [(i, i ^ 1) for i in range(data_size)])]
    slice x0 -> x1, local copies, waits for them, and re-layouts: none -> 5.22 us  [local(): kept = jnp.where(parity == 0, weight_partial[:, 0], weight_partial[:, 1])]
    reshape x0 -> x1, local copies, waits for them, and re-layouts: none -> 4.24 us  [local(): weight_partial.reshape(data_size // 2, 2, -1, weight_partial.shape[1])]
    convert_element_type x0 -> x1, other arithmetic: none -> 3.29 us  [local(): (kept.astype(jnp.float32) + swapped.astype(jnp.float32)).astype(jnp.bfloa...]
    convert_element_type x1 -> x0, local copies, waits for them, and re-layouts: 2.78 us -> none  [local(): weight_partial = lax.dot_general(normed, combined, (((0,), (0,)), ((), ()...]
  transfers between devices with their start and end apart: 4 -> 5, of which waited for: 3 -> 3; matrix products, arithmetic and copies ran while one was open for 3% -> 4% of each run, Pallas kernels for 0% -> 0%
where the time goes in v5:
time: 262 us; the launch traced here: 259 us
  Pallas kernels  170 us (65%)
  local copies, waits for them, and re-layouts  32.3 us (12%)
  starting transfers between devices  16.2 us (6%)
  matrix products  15.6 us (6%)
  other arithmetic  14.3 us (5%)
  waiting for transfers between devices  9.19 us (4%)
    pallas_call x1, Pallas kernels, gather_start(): pl.pallas_call(functools.partial(_gather_start_body, ring), out_shape=[ja...  109 us
    pallas_call x1, Pallas kernels, push_exchange(): pl.pallas_call(functools.partial(_push_body, plan), out_shape=out_shape,...  61.8 us
    unnamed x17, local copies, waits for them, and re-layouts  14.3 us
    ppermute x4, starting transfers between devices, partner_2(): return lax.ppermute(value, axis, pairs)  10.9 us
    ppermute x4, waiting for transfers between devices, partner_2(): return lax.ppermute(value, axis, pairs)  9.19 us
    ppermute x1, starting transfers between devices, local(): swapped = lax.ppermute(handed, 'dp', [(i, i ^ 1) for i in range(data_size)])  5.33 us
  transfers between devices with their start and end apart: 5, of which 3 were waited for; matrix products, arithmetic and copies ran while one was open for 4% of the time, Pallas kernels for 0%

profile of v5, /device:TPU:1, one launch (start us, length us, event | category | flops | bytes accessed | tf_op | source)
XLA Modules:
  0.0 259.0 jit_solution(18103832609283783473)
XLA Ops:
  5.2 1.6 pad_maximum_fusion.pieces_ref
  6.8 1.6 pad_maximum_fusion.1.weights_ref
  8.4 108.6 %shard_map.94 = (bf16[16,2,16,4096]{3,2,1,0:T(8,128)(2,1)}, bf16[32,128,576]{2,1,0:T(8,128)(2,1)}) custom-call(bf16[2,16,4096]{2,1,0:T(8,128)(2,1)} %pad_maximum_fusion.pieces_ref, bf16[128,576]{1,0:T(8,128)(2,1)} %pad_maximum_fusion.1.weights_ref), custom_call_target="tpu_custom_call" | custom-call | bytes 17825792 | tf_op jit(solution)/shard_map/pallas_call | solution.py:198
  117.1 2.7 %fusion.56 = (bf16[16,1,16,4096]{3,2,1,0:T(8,128)(2,1)S(1)}, bf16[16,1,16,4096]{3,2,1,0:T(8,128)(2,1)S(1)}) fusion(bf16[16,2,16,4096]{3,2,1,0:T(8,128)(2,1)} %get-tuple-element.7), kind=kLoop, calls=%fused_computation.81 | loop fusion | bytes 8388608 | tf_op jit(solution)/shard_map/slice | solution.py:237
  121.6 3.1 %collective-permute-start = (bf16[256,64]{0,1:T(8,128)(2,1)S(1)}, bf16[256,64]{0,1:T(8,128)(2,1)S(1)}, u32[]{:S(2)}, u32[]{:S(2)}) collective-permute-start(bf16[256,64]{0,1:T(8,128)(2,1)S(1)} %convolution_convert_fusion.2), channel_id=1, source_target_pairs={{0,1},{1,0},{2,3},{3,2},{4,5},{5,4},{6,7},{7,6},{8,9},{9,8},{10,11... | collective-permute-start | bytes 98312 | tf_op jit(solution)/shard_map/ppermute | solution.py:23
  125.7 1.9 fusion.21
  127.9 4.0 %collective-permute-start.1 = (bf16[256,128]{0,1:T(8,128)(2,1)S(1)}, bf16[256,128]{0,1:T(8,128)(2,1)S(1)}, u32[]{:S(2)}, u32[]{:S(2)}) collective-permute-start(bf16[256,128]{0,1:T(8,128)(2,1)S(1)} %pad_maximum_fusion.2), channel_id=1, source_target_pairs={{0,2},{1,3},{2,0},{3,1},{4,6},{5,7},{6,4},{7,5},{8,10},{9,11},{10,... | collective-permute-start | bytes 196616 | tf_op jit(solution)/shard_map/ppermute | solution.py:23
  132.0 4.0 %collective-permute-done.1 = bf16[256,128]{0,1:T(8,128)(2,1)S(1)} collective-permute-done((bf16[256,128]{0,1:T(8,128)(2,1)S(1)}, bf16[256,128]{0,1:T(8,128)(2,1)S(1)}, u32[]{:S(2)}, u32[]{:S(2)}) %collective-permute-start.1) | collective-permute-done | bytes 65568 | tf_op jit(solution)/shard_map/ppermute | solution.py:23
  139.2 1.9 collective-permute-start.2
  141.2 4.0 %collective-permute-done.2 = bf16[256,128]{0,1:T(8,128)(2,1)S(1)} collective-permute-done((bf16[256,128]{0,1:T(8,128)(2,1)S(1)}, bf16[256,128]{0,1:T(8,128)(2,1)S(1)}, u32[]{:S(2)}, u32[]{:S(2)}) %collective-permute-start.2) | collective-permute-done | bytes 65568 | tf_op jit(solution)/shard_map/ppermute | solution.py:23
  145.2 1.9 collective-permute-start.3
  149.9 2.4 convolution_convert_fusion
  152.2 4.2 %reshape.114 = bf16[16,2,128,320]{2,1,0,3:T(2,128)(2,1)S(1)} reshape(bf16[4096,320]{0,1:T(8,128)(2,1)} %convolution_convert_fusion) | data formatting | bytes 5242880 | tf_op jit(solution)/shard_map/reshape | solution.py:303
  156.5 5.2 %fusion.57 = (bf16[16,1,128,320]{2,1,0,3:T(2,128)(2,1)}, bf16[16,1,128,320]{2,1,0,3:T(2,128)(2,1)}) fusion(bf16[16,2,128,320]{2,1,0,3:T(2,128)(2,1)S(1)} %reshape.114), kind=kLoop, calls=%fused_computation.82 | loop fusion | bytes 5242880 | tf_op jit(solution)/shard_map/slice | solution.py:305
  161.7 5.0 %copy.69 = bf16[16,1,128,320]{3,2,0,1:T(8,128)(2,1)S(1)} copy(bf16[16,1,128,320]{2,1,0,3:T(2,128)(2,1)} %get-tuple-element.25) | data formatting | bytes 2621440
  166.7 5.0 %copy.70 = bf16[16,1,128,320]{3,2,0,1:T(8,128)(2,1)S(1)} copy(bf16[16,1,128,320]{2,1,0,3:T(2,128)(2,1)} %get-tuple-element.26) | data formatting | bytes 2621440
  173.1 2.6 copy.57
  175.7 5.3 %collective-permute-start.4 = (bf16[16,128,320]{1,2,0:T(8,128)(2,1)}, bf16[16,128,320]{1,2,0:T(8,128)(2,1)}, u32[]{:S(2)}, u32[]{:S(2)}) collective-permute-start(bf16[16,128,320]{1,2,0:T(8,128)(2,1)} %copy.57), channel_id=1, source_target_pairs={{0,16},{16,0},{32,48},{48,32},{64,80},{80,64},{96,112},{112,96},{1... | collective-permute-start | bytes 3932168 | tf_op jit(solution)/shard_map/ppermute | solution.py:307
  181.0 2.4 fusion.6
  183.4 3.3 %fusion.2 = bf16[256,4096]{1,0:T(8,128)(2,1)} fusion(f32[256,4096]{1,0:T(8,128)S(1)} %fusion.6, bf16[256,64]{0,1:T(8,128)(2,1)S(1)} %add_convert_fusion.1, bf16[4096,576]{1,0:T(8,128)(2,1)} %bitcast.68), kind=kOutput, calls=%fused_computation.4 | convolution fusion | flops 136314880 | bytes 7372800 | tf_op jit(solution)/shard_map/dot_general | solution.py:297
  186.7 2.5 copy.58
  189.3 3.3 %fusion.3.refs_1_ = bf16[16,128,320]{2,1,0:T(8,128)(2,1)} fusion(bf16[16,128,320]{2,1,0:T(8,128)(2,1)} %copy.58, bf16[16,1,128,320]{3,2,0,1:T(8,128)(2,1)S(1)} %copy.69, bf16[16,1,128,320]{3,2,0,1:T(8,128)(2,1)S(1)} %copy.70, pred[]{:T(512)S(6)} %eq.34), kind=kLoop, calls=%fused_computation.7 | loop fusion | flops 3276800 | bytes 5242881 | tf_op jit(solution)/shard_map/convert_element_type | solution.py:308
  192.6 61.8 %shard_map.95 = (bf16[16,16,4096]{2,1,0:T(8,128)(2,1)}, bf16[16,128,320]{2,1,0:T(8,128)(2,1)}) custom-call(bf16[16,16,4096]{2,1,0:T(8,128)(2,1)} %bitcast.66, bf16[16,128,320]{2,1,0:T(8,128)(2,1)} %fusion.3.refs_1_), custom_call_target="tpu_custom_call" | custom-call | bytes 6815744 | tf_op jit(solution)/shard_map/pallas_call | solution.py:100
  254.4 1.8 convert_reduce_fusion.1
  (46 shorter events, 17.8 us)
Async XLA Ops:
  117.1 3.8 %copy-start = (bf16[32,128,576]{2,1,0:T(8,128)(2,1)S(1)}, bf16[32,128,576]{2,1,0:T(8,128)(2,1)}, u32[]{:S(2)}) copy-start(bf16[32,128,576]{2,1,0:T(8,128)(2,1)} %get-tuple-element.8) | copy-start | bytes 14155780
  121.6 6.3 %collective-permute-start = (bf16[256,64]{0,1:T(8,128)(2,1)S(1)}, bf16[256,64]{0,1:T(8,128)(2,1)S(1)}, u32[]{:S(2)}, u32[]{:S(2)}) collective-permute-start(bf16[256,64]{0,1:T(8,128)(2,1)S(1)} %convolution_convert_fusion.2), channel_id=1, source_target_pairs={{0,1},{1,0},{2,3},{3,2},{4,5},{5,4},{6,7},{7,6},{8,9},{9,8},{10,11... | collective-permute-start | bytes 98312 | tf_op jit(solution)/shard_map/ppermute | solution.py:23
  125.7 1.9 copy-start.4
  127.9 8.1 %collective-permute-start.1 = (bf16[256,128]{0,1:T(8,128)(2,1)S(1)}, bf16[256,128]{0,1:T(8,128)(2,1)S(1)}, u32[]{:S(2)}, u32[]{:S(2)}) collective-permute-start(bf16[256,128]{0,1:T(8,128)(2,1)S(1)} %pad_maximum_fusion.2), channel_id=1, source_target_pairs={{0,2},{1,3},{2,0},{3,1},{4,6},{5,7},{6,4},{7,5},{8,10},{9,11},{10,... | collective-permute-start | bytes 196616 | tf_op jit(solution)/shard_map/ppermute | solution.py:23
  136.4 0.8 copy-start.5
  139.2 5.9 %collective-permute-start.2 = (bf16[256,128]{0,1:T(8,128)(2,1)S(1)}, bf16[256,128]{0,1:T(8,128)(2,1)S(1)}, u32[]{:S(2)}, u32[]{:S(2)}) collective-permute-start(bf16[256,128]{0,1:T(8,128)(2,1)S(1)} %get-tuple-element.31), channel_id=1, source_target_pairs={{0,2},{1,3},{2,0},{3,1},{4,6},{5,7},{6,4},{7,5},{8,10},{9,11},{10,... | collective-permute-start | bytes 196616 | tf_op jit(solution)/shard_map/ppermute | solution.py:23
  145.2 4.7 %collective-permute-start.3 = (bf16[256,64]{0,1:T(8,128)(2,1)S(1)}, bf16[256,64]{0,1:T(8,128)(2,1)S(1)}, u32[]{:S(2)}, u32[]{:S(2)}) collective-permute-start(bf16[256,64]{0,1:T(8,128)(2,1)S(1)} %select_convert_fusion.1), channel_id=1, source_target_pairs={{0,1},{1,0},{2,3},{3,2},{4,5},{5,4},{6,7},{7,6},{8,9},{9,8},{10,11... | collective-permute-start | bytes 98312 | tf_op jit(solution)/shard_map/ppermute | solution.py:23
  175.7 11.0 %collective-permute-start.4 = (bf16[16,128,320]{1,2,0:T(8,128)(2,1)}, bf16[16,128,320]{1,2,0:T(8,128)(2,1)}, u32[]{:S(2)}, u32[]{:S(2)}) collective-permute-start(bf16[16,128,320]{1,2,0:T(8,128)(2,1)} %copy.57), channel_id=1, source_target_pairs={{0,16},{16,0},{32,48},{48,32},{64,80},{80,64},{96,112},{112,96},{1... | collective-permute-start | bytes 3932168 | tf_op jit(solution)/shard_map/ppermute | solution.py:307
  254.4 3.2 %copy-start.1 = (bf16[16,16,4096]{2,1,0:T(8,128)(2,1)S(1)}, bf16[16,16,4096]{2,1,0:T(8,128)(2,1)}, u32[]{:S(2)}) copy-start(bf16[16,16,4096]{2,1,0:T(8,128)(2,1)} %get-tuple-element.9) | copy-start | bytes 6291460
  254.4 3.5 %copy-start.2 = (bf16[16,4096]{1,0:T(8,128)(2,1)S(1)}, bf16[16,4096]{1,0:T(8,128)(2,1)}, u32[]{:S(2)}) copy-start(bf16[16,4096]{1,0:T(8,128)(2,1)} %param.7) | copy-start | bytes 393220
  256.2 2.0 copy-start.3

commit v6 on v5

--- a/solution.py
+++ b/solution.py
@@ -216,6 +216,58 @@
     )(pieces, weights)
 
 
+def _pair_body(x_ref, o_ref, mine, theirs, send_sem, recv_sem, local_sem):
+    r = lax.axis_index("dp")
+    parity = lax.rem(r, 2)
+    pair = r + 1 - 2 * parity
+    slots, _, width = mine.shape
+    barrier = pltpu.get_barrier_semaphore()
+    pl.semaphore_signal(barrier, inc=1, device_id={"dp": pair}, device_id_type=MESH_ID)
+    pl.semaphore_wait(barrier, 1)
+    sent = []
+    kept = []
+    for i in range(slots):
+        give = pl.ds(pl.multiple_of((2 * i + 1 - parity) * width, width), width)
+        keep = pl.ds(pl.multiple_of((2 * i + parity) * width, width), width)
+        copy = pltpu.make_async_remote_copy(
+            src_ref=x_ref.at[:, give], dst_ref=theirs.at[i], send_sem=send_sem.at[i],
+            recv_sem=recv_sem.at[i], device_id={"dp": pair}, device_id_type=MESH_ID,
+        )
+        copy.start()
+        sent.append(copy)
+        own = pltpu.make_async_copy(x_ref.at[:, keep], mine.at[i], local_sem.at[i])
+        own.start()
+        kept.append(own)
+    for copy in sent:
+        copy.wait()
+    for copy in kept:
+        copy.wait()
+    o_ref[...] = (mine[...].astype(jnp.float32) + theirs[...].astype(jnp.float32)).astype(o_ref.dtype)
+
+
+def pair_sum(x, width):
+    rows, cols = x.shape
+    slots = cols // width // 2
+    shape = (slots, rows, width)
+    return pl.pallas_call(
+        _pair_body,
+        out_shape=jax.ShapeDtypeStruct(shape, x.dtype),
+        in_specs=[pl.BlockSpec(memory_space=pl.ANY)],
+        out_specs=pl.BlockSpec(memory_space=pltpu.VMEM),
+        scratch_shapes=[
+            pltpu.VMEM(shape, x.dtype),
+            pltpu.VMEM(shape, x.dtype),
+            pltpu.SemaphoreType.DMA((slots,)),
+            pltpu.SemaphoreType.DMA((slots,)),
+            pltpu.SemaphoreType.DMA((slots,)),
+        ],
+        compiler_params=pltpu.CompilerParams(collective_id=4, has_side_effects=True),
+        cost_estimate=pl.CostEstimate(
+            flops=x.size // 2, transcendentals=0, bytes_accessed=2 * x.size * x.dtype.itemsize
+        ),
+    )(x)
+
+
 def local(tokens, norm_gain, query_weight, kv_weight, out_weight, grad_out, doc_lengths):
     tensor_size = lax.axis_size("tensor")
     data_size = lax.axis_size("dp")
@@ -298,14 +350,10 @@
     partial = (from_query + from_kv).astype(jnp.bfloat16).reshape(tensor_size, rows, -1)
     combined = jnp.concatenate([query_grad, kv_grad], axis=1)
     weight_partial = lax.dot_general(
-        normed, combined, (((0,), (0,)), ((), ())), preferred_element_type=jnp.float32
+        combined, normed, (((0,), (0,)), ((), ())), preferred_element_type=jnp.float32
     ).astype(jnp.bfloat16)
-    weight_partial = weight_partial.reshape(data_size // 2, 2, -1, weight_partial.shape[1])
-    parity = lax.rem(lax.axis_index("dp"), 2)
-    kept = jnp.where(parity == 0, weight_partial[:, 0], weight_partial[:, 1])
-    handed = jnp.where(parity == 0, weight_partial[:, 1], weight_partial[:, 0])
-    swapped = lax.ppermute(handed, "dp", [(i, i ^ 1) for i in range(data_size)])
-    paired = (kept.astype(jnp.float32) + swapped.astype(jnp.float32)).astype(jnp.bfloat16)
+    block = weight_partial.shape[1] // data_size
+    paired = pair_sum(weight_partial, block)
     arrived, weight_arrived = push_exchange(
         [
             ("tensor", tensor_size, partial, True),
@@ -319,7 +367,7 @@
     input_grad = (grad_out.astype(jnp.float32) + (scaled - correction) / root_mean[:, None]).astype(
         jnp.bfloat16
     )
-    weight_grads = jnp.sum(weight_arrived.astype(jnp.float32), axis=0) / data_size
+    weight_grads = (jnp.sum(weight_arrived.astype(jnp.float32), axis=0) / data_size).T
     return (input_grad, weight_grads[:, :query_width], weight_grads[:, query_width:])
 
 

time: 262 us -> 233 us (0.89); the launches traced: 259 us -> 233 us
  local copies, waits for them, and re-layouts: 32.3 us -> 7.72 us
  Pallas kernels: 170 us -> 177 us
  starting transfers between devices: 16.2 us -> 10.9 us
  other arithmetic: 14.3 us -> 11 us
  matrix products: 15.6 us -> 18.9 us
  waiting for transfers between devices: 9.19 us -> 6.41 us
    unnamed x17 -> x13, local copies, waits for them, and re-layouts: 14.3 us -> 4.22 us
    pallas_call x0 -> x1, Pallas kernels: none -> 7.55 us  [pair_sum(): pl.pallas_call(_pair_body, out_shape=jax.ShapeDtypeStruct(shape, x.dtype)...]
    ppermute x1 -> x0, starting transfers between devices: 5.33 us -> none  [local(): swapped = lax.ppermute(handed, 'dp', [(i, i ^ 1) for i in range(data_size)])]
    slice x1 -> x0, local copies, waits for them, and re-layouts: 5.22 us -> none  [local(): kept = jnp.where(parity == 0, weight_partial[:, 0], weight_partial[:, 1])]
    reshape x1 -> x0, local copies, waits for them, and re-layouts: 4.24 us -> none  [local(): weight_partial.reshape(data_size // 2, 2, -1, weight_partial.shape[1])]
    convert_element_type x1 -> x0, other arithmetic: 3.29 us -> none  [local(): (kept.astype(jnp.float32) + swapped.astype(jnp.float32)).astype(jnp.bfloa...]
    ppermute x4, waiting for transfers between devices: 9.19 us -> 6.41 us  [partner_2(): return lax.ppermute(value, axis, pairs)]
  transfers between devices with their start and end apart: 5 -> 4, of which waited for: 3 -> 2; matrix products, arithmetic and copies ran while one was open for 4% -> 4% of each run, Pallas kernels for 0% -> 0%
where the time goes in v6:
time: 233 us
  Pallas kernels  177 us (76%)
  matrix products  18.9 us (8%)
  other arithmetic  11 us (5%)
  starting transfers between devices  10.9 us (5%)
  local copies, waits for them, and re-layouts  7.72 us (3%)
  waiting for transfers between devices  6.41 us (3%)
    pallas_call x1, Pallas kernels, gather_start(): pl.pallas_call(functools.partial(_gather_start_body, ring), out_shape=[ja...  109 us
    pallas_call x1, Pallas kernels, push_exchange(): pl.pallas_call(functools.partial(_push_body, plan), out_shape=out_shape,...  60.8 us
    ppermute x4, starting transfers between devices, partner_2(): return lax.ppermute(value, axis, pairs)  10.9 us
    pallas_call x1, Pallas kernels, pair_sum(): pl.pallas_call(_pair_body, out_shape=jax.ShapeDtypeStruct(shape, x.dtype)...  7.55 us
    ppermute x4, waiting for transfers between devices, partner_2(): return lax.ppermute(value, axis, pairs)  6.41 us
  transfers between devices with their start and end apart: 4, of which 2 were waited for; matrix products, arithmetic and copies ran while one was open for 4% of the time, Pallas kernels for 0%

profile of v6, /device:TPU:1, one launch (start us, length us, event | category | flops | bytes accessed | tf_op | source)
XLA Modules:
  0.0 232.8 jit_solution(5003531965769864598)
XLA Ops:
  1.3 1.0 fusion.29
  2.4 0.9 copy.20
  4.2 1.0 fusion.37
  5.2 1.6 pad_maximum_fusion.pieces_ref
  6.8 1.6 pad_maximum_fusion.1.weights_ref
  8.4 108.6 %shard_map.94 = (bf16[16,2,16,4096]{3,2,1,0:T(8,128)(2,1)}, bf16[32,128,576]{2,1,0:T(8,128)(2,1)}) custom-call(bf16[2,16,4096]{2,1,0:T(8,128)(2,1)} %pad_maximum_fusion.pieces_ref, bf16[128,576]{1,0:T(8,128)(2,1)} %pad_maximum_fusion.1.weights_ref), custom_call_target="tpu_custom_call" | custom-call | bytes 17825792 | tf_op jit(solution)/shard_map/pallas_call | solution.py:198
  117.1 2.9 %fusion.55 = (bf16[16,1,16,4096]{3,2,1,0:T(8,128)(2,1)S(1)}, bf16[16,1,16,4096]{3,2,1,0:T(8,128)(2,1)S(1)}) fusion(bf16[16,2,16,4096]{3,2,1,0:T(8,128)(2,1)} %get-tuple-element.7), kind=kLoop, calls=%fused_computation.78 | loop fusion | bytes 8388608 | tf_op jit(solution)/shard_map/slice | solution.py:289
  121.6 3.1 %collective-permute-start = (bf16[256,64]{0,1:T(8,128)(2,1)S(1)}, bf16[256,64]{0,1:T(8,128)(2,1)S(1)}, u32[]{:S(2)}, u32[]{:S(2)}) collective-permute-start(bf16[256,64]{0,1:T(8,128)(2,1)S(1)} %convolution_convert_fusion.2), channel_id=1, source_target_pairs={{0,1},{1,0},{2,3},{3,2},{4,5},{5,4},{6,7},{7,6},{8,9},{9,8},{10,11... | collective-permute-start | bytes 98312 | tf_op jit(solution)/shard_map/ppermute | solution.py:23
  124.7 1.0 fusion.17
  125.8 1.9 fusion.20
  127.9 4.0 %collective-permute-start.1 = (bf16[256,128]{0,1:T(8,128)(2,1)S(1)}, bf16[256,128]{0,1:T(8,128)(2,1)S(1)}, u32[]{:S(2)}, u32[]{:S(2)}) collective-permute-start(bf16[256,128]{0,1:T(8,128)(2,1)S(1)} %pad_maximum_fusion.2), channel_id=1, source_target_pairs={{0,2},{1,3},{2,0},{3,1},{4,6},{5,7},{6,4},{7,5},{8,10},{9,11},{10,... | collective-permute-start | bytes 196616 | tf_op jit(solution)/shard_map/ppermute | solution.py:23
  132.0 4.0 %collective-permute-done.1 = bf16[256,128]{0,1:T(8,128)(2,1)S(1)} collective-permute-done((bf16[256,128]{0,1:T(8,128)(2,1)S(1)}, bf16[256,128]{0,1:T(8,128)(2,1)S(1)}, u32[]{:S(2)}, u32[]{:S(2)}) %collective-permute-start.1) | collective-permute-done | bytes 65568 | tf_op jit(solution)/shard_map/ppermute | solution.py:23
  137.7 1.6 select_convert_fusion
  139.3 1.9 collective-permute-start.2
  141.2 1.6 convolution_convert_fusion.1
  142.8 2.4 %collective-permute-done.2 = bf16[256,128]{0,1:T(8,128)(2,1)S(1)} collective-permute-done((bf16[256,128]{0,1:T(8,128)(2,1)S(1)}, bf16[256,128]{0,1:T(8,128)(2,1)S(1)}, u32[]{:S(2)}, u32[]{:S(2)}) %collective-permute-start.2) | collective-permute-done | bytes 65568 | tf_op jit(solution)/shard_map/ppermute | solution.py:23
  145.2 1.9 collective-permute-start.3
  147.1 4.4 %fusion.5 = f32[256,4096]{1,0:T(8,128)} fusion(bf16[256,256]{0,1:T(8,128)(2,1)S(1)} %bitcast.69, bf16[4096,576]{1,0:T(8,128)(2,1)} %bitcast.62), kind=kOutput, calls=%fused_computation.9 | convolution fusion | flops 536870912 | bytes 6422528 | tf_op jit(solution)/shard_map/dot_general | solution.py:346
  151.5 2.3 %convolution_convert_fusion.x_ref = bf16[320,4096]{1,0:T(8,128)(2,1)} fusion(bf16[256,4096]{1,0:T(8,128)(2,1)S(1)} %bitcast.60, bf16[256,64]{0,1:T(8,128)(2,1)S(1)} %add_convert_fusion.1, bf16[256,256]{0,1:T(8,128)(2,1)S(1)} %bitcast.70), kind=kOutput, calls=%fused_computation.3 | convolution fusion | flops 672727040 | bytes 4882432 | tf_op jit(solution)/shard_map/dot_general | solution.py:352
  153.9 7.5 %shard_map.95.refs_1_ = bf16[16,320,128]{2,1,0:T(8,128)(2,1)} custom-call(bf16[320,4096]{1,0:T(8,128)(2,1)} %convolution_convert_fusion.x_ref), custom_call_target="tpu_custom_call" | custom-call | flops 655360 | bytes 5242880 | tf_op jit(solution)/shard_map/pallas_call | solution.py:252
  161.4 4.6 %fusion.2 = bf16[256,4096]{1,0:T(8,128)(2,1)} fusion(f32[256,4096]{1,0:T(8,128)} %fusion.5, bf16[256,64]{0,1:T(8,128)(2,1)S(1)} %add_convert_fusion.1, bf16[4096,576]{1,0:T(8,128)(2,1)} %bitcast.63), kind=kOutput, calls=%fused_computation.4 | convolution fusion | flops 136314880 | bytes 7372800 | tf_op jit(solution)/shard_map/dot_general | solution.py:349
  166.0 60.8 %shard_map.96 = (bf16[16,16,4096]{2,1,0:T(8,128)(2,1)}, bf16[16,320,128]{2,1,0:T(8,128)(2,1)}) custom-call(bf16[16,16,4096]{2,1,0:T(8,128)(2,1)} %bitcast.61, bf16[16,320,128]{2,1,0:T(8,128)(2,1)} %shard_map.95.refs_1_), custom_call_target="tpu_custom_call" | custom-call | bytes 6815744 | tf_op jit(solution)/shard_map/pallas_call | solution.py:100
  226.9 1.5 convert_reduce_fusion.1
  229.8 1.9 convert_reduce_fusion
  (35 shorter events, 7.7 us)
Async XLA Ops:
  117.1 3.8 %copy-start = (bf16[32,128,576]{2,1,0:T(8,128)(2,1)S(1)}, bf16[32,128,576]{2,1,0:T(8,128)(2,1)}, u32[]{:S(2)}) copy-start(bf16[32,128,576]{2,1,0:T(8,128)(2,1)} %get-tuple-element.8) | copy-start | bytes 14155780
  121.6 6.3 %collective-permute-start = (bf16[256,64]{0,1:T(8,128)(2,1)S(1)}, bf16[256,64]{0,1:T(8,128)(2,1)S(1)}, u32[]{:S(2)}, u32[]{:S(2)}) collective-permute-start(bf16[256,64]{0,1:T(8,128)(2,1)S(1)} %convolution_convert_fusion.2), channel_id=1, source_target_pairs={{0,1},{1,0},{2,3},{3,2},{4,5},{5,4},{6,7},{7,6},{8,9},{9,8},{10,11... | collective-permute-start | bytes 98312 | tf_op jit(solution)/shard_map/ppermute | solution.py:23
  125.7 1.9 copy-start.3
  127.9 8.1 %collective-permute-start.1 = (bf16[256,128]{0,1:T(8,128)(2,1)S(1)}, bf16[256,128]{0,1:T(8,128)(2,1)S(1)}, u32[]{:S(2)}, u32[]{:S(2)}) collective-permute-start(bf16[256,128]{0,1:T(8,128)(2,1)S(1)} %pad_maximum_fusion.2), channel_id=1, source_target_pairs={{0,2},{1,3},{2,0},{3,1},{4,6},{5,7},{6,4},{7,5},{8,10},{9,11},{10,... | collective-permute-start | bytes 196616 | tf_op jit(solution)/shard_map/ppermute | solution.py:23
  136.4 0.8 copy-start.4
  139.3 5.9 %collective-permute-start.2 = (bf16[256,128]{0,1:T(8,128)(2,1)S(1)}, bf16[256,128]{0,1:T(8,128)(2,1)S(1)}, u32[]{:S(2)}, u32[]{:S(2)}) collective-permute-start(bf16[256,128]{0,1:T(8,128)(2,1)S(1)} %get-tuple-element.23), channel_id=1, source_target_pairs={{0,2},{1,3},{2,0},{3,1},{4,6},{5,7},{6,4},{7,5},{8,10},{9,11},{10,... | collective-permute-start | bytes 196616 | tf_op jit(solution)/shard_map/ppermute | solution.py:23
  145.2 6.3 %collective-permute-start.3 = (bf16[256,64]{0,1:T(8,128)(2,1)S(1)}, bf16[256,64]{0,1:T(8,128)(2,1)S(1)}, u32[]{:S(2)}, u32[]{:S(2)}) collective-permute-start(bf16[256,64]{0,1:T(8,128)(2,1)S(1)} %select_convert_fusion.1), channel_id=1, source_target_pairs={{0,1},{1,0},{2,3},{3,2},{4,5},{5,4},{6,7},{7,6},{8,9},{9,8},{10,11... | collective-permute-start | bytes 98312 | tf_op jit(solution)/shard_map/ppermute | solution.py:23
  226.8 4.9 %copy-start.1 = (bf16[16,4096]{1,0:T(8,128)(2,1)S(1)}, bf16[16,4096]{1,0:T(8,128)(2,1)}, u32[]{:S(2)}) copy-start(bf16[16,4096]{1,0:T(8,128)(2,1)} %param.7) | copy-start | bytes 393220
  228.4 3.6 %copy-start.2 = (bf16[16,4096]{1,0:T(8,128)(2,1)S(1)}, bf16[16,4096]{1,0:T(8,128)(2,1)}, u32[]{:S(2)}) copy-start(bf16[16,4096]{1,0:T(8,128)(2,1)} %param.12) | copy-start | bytes 393220

commit v7 on v6

--- a/solution.py
+++ b/solution.py
@@ -110,28 +110,39 @@
     )(*arrays)
 
 
-def _gather_start_body(ring, pieces_ref, weights_ref, tens_out, dp_out, ring_send, ring_recv,
-                       cross_sem, dp_send, dp_recv, local_sem):
+def _gather_start_body(ring, pieces_ref, weights_ref, tens_out, dp_out, t_send, t_recv, t_cross,
+                       d_send, d_recv, d_cross, pair_send, pair_recv, local_sem):
     n_t = lax.axis_size("tensor")
     n_d = lax.axis_size("dp")
     t = lax.axis_index("tensor")
     r = lax.axis_index("dp")
     z = lax.rem(t, ring)
-    base = t - z
-    other = lax.rem(t + ring, n_t) - z
-    cross = lax.rem(t + ring, n_t)
-    right = base + lax.rem(z + 1, ring)
-    left = base + lax.rem(z + ring - 1, ring)
-    pair = r + 1 - 2 * lax.rem(r, 2)
-    peers = n_d // 2
+    t_base = t - z
+    t_other = lax.rem(t + ring, n_t) - z
+    t_far = lax.rem(t + ring, n_t)
+    d_ring = n_d // 4
+    core = lax.rem(r, 2)
+    y = lax.rem(r // 2, d_ring)
+    x = r // (2 * d_ring)
+    d_base = x * 2 * d_ring + core
+    d_other = (1 - x) * 2 * d_ring + core
+    d_far = d_other + 2 * y
+    pair = r + 1 - 2 * core
+    rings = (
+        ("tensor", tens_out, pieces_ref, z, (t_base, t_other), 1, ring, t_send, t_recv),
+        ("dp", dp_out, weights_ref, y, (d_base, d_other), 2, d_ring, d_send, d_recv),
+    )
+
+    def neighbours(pos, bases, stride, n):
+        return (bases[0] + lax.rem(pos + 1, n) * stride, bases[0] + lax.rem(pos + n - 1, n) * stride)
+
     barrier = pltpu.get_barrier_semaphore()
-    for device in ({"tensor": cross}, {"tensor": right}, {"tensor": left}, {"dp": pair}):
+    targets = [{"tensor": t_far}, {"dp": pair}, {"dp": d_far}]
+    for axis, _, _, pos, bases, stride, n, _, _ in rings:
+        targets.extend({axis: v} for v in neighbours(pos, bases, stride, n))
+    for device in targets:
         pl.semaphore_signal(barrier, inc=1, device_id=device, device_id_type=MESH_ID)
-    for k in range(1, peers):
-        pl.semaphore_signal(
-            barrier, inc=1, device_id={"dp": lax.rem(r + 2 * k, n_d)}, device_id_type=MESH_ID
-        )
-    pl.semaphore_wait(barrier, 4 + peers - 1)
+    pl.semaphore_wait(barrier, len(targets))
 
     def remote(src, dst, send, recv, device):
         copy = pltpu.make_async_remote_copy(
@@ -142,51 +153,61 @@
         return copy
 
     waits = []
-    for k in range(1, peers):
-        waits.append(remote(weights_ref, dp_out.at[r], dp_send.at[0, k], dp_recv.at[0, k],
-                            {"dp": lax.rem(r + 2 * k, n_d)}))
-    waits.append(remote(weights_ref, dp_out.at[r], dp_send.at[0, 0], dp_recv.at[0, 0],
-                        {"dp": pair}))
-    crossed = remote(pieces_ref, tens_out.at[t], cross_sem.at[0], cross_sem.at[1],
-                     {"tensor": cross})
+    forwarded = [0]
+
+    def forward(src, slot):
+        f = forwarded[0]
+        waits.append(remote(src, dp_out.at[slot], pair_send.at[f], pair_recv.at[f], {"dp": pair}))
+        forwarded[0] = f + 1
+
+    forward(weights_ref, r)
+    t_crossed = remote(pieces_ref, tens_out.at[t], t_cross.at[0], t_cross.at[1], {"tensor": t_far})
+    d_crossed = remote(weights_ref, dp_out.at[r], d_cross.at[0], d_cross.at[1], {"dp": d_far})
     own_t = pltpu.make_async_copy(pieces_ref, tens_out.at[t], local_sem.at[0])
     own_t.start()
     own_d = pltpu.make_async_copy(weights_ref, dp_out.at[r], local_sem.at[1])
     own_d.start()
-    crossed.wait()
-    steps = (ring // 2, ring - 1 - ring // 2)
-    moving = [None, None]
-    for s in range(max(steps)):
-        for d, (target, sign) in enumerate(((right, -1), (left, 1))):
-            if s >= steps[d]:
-                continue
-            if s > 0:
-                for copy in moving[d]:
-                    copy.wait_recv()
-            origin = lax.rem(z + sign * s + ring, ring)
-            sent = []
-            for h, start in enumerate((base, other)):
-                slot = start + origin
-                src = pieces_ref if (s == 0 and h == 0) else tens_out.at[slot]
-                sent.append(remote(src, tens_out.at[slot], ring_send.at[d, s, h],
-                                   ring_recv.at[d, s, h], {"tensor": target}))
-            waits.extend(sent)
-            moving[d] = sent
-    for d in range(2):
-        for copy in moving[d]:
-            copy.wait_recv()
-    for k in range(1, peers):
-        slot = lax.rem(r + n_d - 2 * k, n_d)
-        arrival = pltpu.make_async_copy(dp_out.at[slot], dp_out.at[slot], dp_recv.at[0, k])
-        arrival.wait()
-        waits.append(remote(dp_out.at[slot], dp_out.at[slot], dp_send.at[1, k],
-                            dp_recv.at[1, k], {"dp": pair}))
+    t_crossed.wait()
+    d_crossed.wait()
+    forward(dp_out.at[d_far], d_far)
+    moving = {}
+    for s in range(max(ring, d_ring) // 2):
+        for k, (axis, out, own, pos, bases, stride, n, send, recv) in enumerate(rings):
+            right, left = neighbours(pos, bases, stride, n)
+            steps = (n // 2, n - 1 - n // 2)
+            for d, (target, sign) in enumerate(((right, -1), (left, 1))):
+                if s >= steps[d]:
+                    continue
+                origin = lax.rem(pos + sign * s + n, n)
+                if s > 0:
+                    for copy in moving[k, d]:
+                        copy.wait_recv()
+                    if k == 1:
+                        for start in bases:
+                            slot = start + origin * stride
+                            forward(out.at[slot], slot)
+                sent = []
+                for h, start in enumerate(bases):
+                    slot = start + origin * stride
+                    src = own if (s == 0 and h == 0) else out.at[slot]
+                    sent.append(remote(src, out.at[slot], send.at[d, s, h], recv.at[d, s, h],
+                                       {axis: target}))
+                waits.extend(sent)
+                moving[k, d] = sent
+    for k, (axis, out, own, pos, bases, stride, n, send, recv) in enumerate(rings):
+        steps = (n // 2, n - 1 - n // 2)
+        for d, sign in enumerate((-1, 1)):
+            for copy in moving[k, d]:
+                copy.wait_recv()
+            if k == 1:
+                origin = lax.rem(pos + sign * steps[d] + n, n)
+                for start in bases:
+                    slot = start + origin * stride
+                    forward(out.at[slot], slot)
     for copy in waits:
         copy.wait_send()
-    pltpu.make_async_copy(dp_out.at[r], dp_out.at[r], dp_recv.at[0, 0]).wait()
-    for k in range(1, peers):
-        slot = lax.rem(pair + n_d - 2 * k, n_d)
-        pltpu.make_async_copy(dp_out.at[slot], dp_out.at[slot], dp_recv.at[1, k]).wait()
+    for f in range(forwarded[0]):
+        pltpu.make_async_copy(dp_out.at[0], dp_out.at[0], pair_recv.at[f]).wait()
     own_t.wait()
     own_d.wait()
 
@@ -194,6 +215,7 @@
 def gather_start(pieces, weights, ring):
     n_t = lax.axis_size("tensor")
     n_d = lax.axis_size("dp")
+    d_ring = n_d // 4
     moved = 2 * (n_t * pieces.size * pieces.dtype.itemsize + n_d * weights.size * weights.dtype.itemsize)
     return pl.pallas_call(
         functools.partial(_gather_start_body, ring),
@@ -207,8 +229,11 @@
             pltpu.SemaphoreType.DMA((2, ring // 2, 2)),
             pltpu.SemaphoreType.DMA((2, ring // 2, 2)),
             pltpu.SemaphoreType.DMA((2,)),
-            pltpu.SemaphoreType.DMA((2, n_d // 2)),
-            pltpu.SemaphoreType.DMA((2, n_d // 2)),
+            pltpu.SemaphoreType.DMA((2, d_ring // 2, 2)),
+            pltpu.SemaphoreType.DMA((2, d_ring // 2, 2)),
+            pltpu.SemaphoreType.DMA((2,)),
+            pltpu.SemaphoreType.DMA((2 * d_ring,)),
+            pltpu.SemaphoreType.DMA((2 * d_ring,)),
             pltpu.SemaphoreType.DMA((2,)),
         ],
         compiler_params=pltpu.CompilerParams(collective_id=0, has_side_effects=True),

time: 233 us -> 201 us (0.86)
  Pallas kernels: 177 us -> 143 us
  waiting for transfers between devices: 6.41 us -> 9.48 us
    pallas_call x1, Pallas kernels: 109 us -> 74.1 us  [gather_start(): pl.pallas_call(functools.partial(_gather_start_body, ring), out_shape=[ja...]
    ppermute x4, waiting for transfers between devices: 6.41 us -> 9.48 us  [partner_2(): return lax.ppermute(value, axis, pairs)]
  transfers between devices with their start and end apart: 4 -> 4, of which waited for: 2 -> 2; matrix products, arithmetic and copies ran while one was open for 4% -> 5% of each run, Pallas kernels for 0% -> 0%
where the time goes in v7:
time: 201 us; the launch traced here: 200 us
  Pallas kernels  143 us (71%)
  matrix products  18.9 us (9%)
  other arithmetic  11 us (5%)
  waiting for transfers between devices  9.48 us (5%)
  starting transfers between devices  9.17 us (5%)
  local copies, waits for them, and re-layouts  7.72 us (4%)
    pallas_call x1, Pallas kernels, gather_start(): pl.pallas_call(functools.partial(_gather_start_body, ring), out_shape=[ja...  74.1 us
    pallas_call x1, Pallas kernels, push_exchange(): pl.pallas_call(functools.partial(_push_body, plan), out_shape=out_shape,...  62.9 us
    ppermute x4, waiting for transfers between devices, partner_2(): return lax.ppermute(value, axis, pairs)  9.48 us
    ppermute x4, starting transfers between devices, partner_2(): return lax.ppermute(value, axis, pairs)  9.17 us
    pallas_call x1, Pallas kernels, pair_sum(): pl.pallas_call(_pair_body, out_shape=jax.ShapeDtypeStruct(shape, x.dtype)...  6.22 us
    dot_general x1, matrix products, local(): lax.dot_general(kv_grad, kv_local, contract_last, preferred_element_type=...  4.6 us
    dot_general x1, matrix products, local(): lax.dot_general(query_grad, query_full, contract_last, preferred_element_...  4.37 us
    unnamed x13, local copies, waits for them, and re-layouts  4.22 us
  transfers between devices with their start and end apart: 4, of which 2 were waited for; matrix products, arithmetic and copies ran while one was open for 5% of the time, Pallas kernels for 0%

profile of v7, /device:TPU:1, one launch (start us, length us, event | category | flops | bytes accessed | tf_op | source)
XLA Modules:
  0.0 200.3 jit_solution(9225023407813538137)
XLA Ops:
  1.3 1.0 fusion.29
  2.4 0.9 copy.20
  4.2 1.0 fusion.37
  5.2 1.6 pad_maximum_fusion.pieces_ref
  6.8 1.6 pad_maximum_fusion.1.weights_ref
  8.4 74.1 %shard_map.94 = (bf16[16,2,16,4096]{3,2,1,0:T(8,128)(2,1)}, bf16[32,128,576]{2,1,0:T(8,128)(2,1)}) custom-call(bf16[2,16,4096]{2,1,0:T(8,128)(2,1)} %pad_maximum_fusion.pieces_ref, bf16[128,576]{1,0:T(8,128)(2,1)} %pad_maximum_fusion.1.weights_ref), custom_call_target="tpu_custom_call" | custom-call | bytes 17825792 | tf_op jit(solution)/shard_map/pallas_call | solution.py:220
  82.5 2.9 %fusion.55 = (bf16[16,1,16,4096]{3,2,1,0:T(8,128)(2,1)S(1)}, bf16[16,1,16,4096]{3,2,1,0:T(8,128)(2,1)S(1)}) fusion(bf16[16,2,16,4096]{3,2,1,0:T(8,128)(2,1)} %get-tuple-element.7), kind=kLoop, calls=%fused_computation.78 | loop fusion | bytes 8388608 | tf_op jit(solution)/shard_map/slice | solution.py:314
  87.1 3.1 %collective-permute-start = (bf16[256,64]{0,1:T(8,128)(2,1)S(1)}, bf16[256,64]{0,1:T(8,128)(2,1)S(1)}, u32[]{:S(2)}, u32[]{:S(2)}) collective-permute-start(bf16[256,64]{0,1:T(8,128)(2,1)S(1)} %convolution_convert_fusion.2), channel_id=1, source_target_pairs={{0,1},{1,0},{2,3},{3,2},{4,5},{5,4},{6,7},{7,6},{8,9},{9,8},{10,11... | collective-permute-start | bytes 98312 | tf_op jit(solution)/shard_map/ppermute | solution.py:23
  90.2 1.0 fusion.17
  91.2 1.9 fusion.20
  93.4 2.2 %collective-permute-start.1 = (bf16[256,128]{0,1:T(8,128)(2,1)S(1)}, bf16[256,128]{0,1:T(8,128)(2,1)S(1)}, u32[]{:S(2)}, u32[]{:S(2)}) collective-permute-start(bf16[256,128]{0,1:T(8,128)(2,1)S(1)} %pad_maximum_fusion.2), channel_id=1, source_target_pairs={{0,2},{1,3},{2,0},{3,1},{4,6},{5,7},{6,4},{7,5},{8,10},{9,11},{10,... | collective-permute-start | bytes 196616 | tf_op jit(solution)/shard_map/ppermute | solution.py:23
  95.7 5.7 %collective-permute-done.1 = bf16[256,128]{0,1:T(8,128)(2,1)S(1)} collective-permute-done((bf16[256,128]{0,1:T(8,128)(2,1)S(1)}, bf16[256,128]{0,1:T(8,128)(2,1)S(1)}, u32[]{:S(2)}, u32[]{:S(2)}) %collective-permute-start.1) | collective-permute-done | bytes 65568 | tf_op jit(solution)/shard_map/ppermute | solution.py:23
  103.1 1.6 select_convert_fusion
  104.7 1.9 collective-permute-start.2
  106.6 1.6 convolution_convert_fusion.1
  108.2 3.7 %collective-permute-done.2 = bf16[256,128]{0,1:T(8,128)(2,1)S(1)} collective-permute-done((bf16[256,128]{0,1:T(8,128)(2,1)S(1)}, bf16[256,128]{0,1:T(8,128)(2,1)S(1)}, u32[]{:S(2)}, u32[]{:S(2)}) %collective-permute-start.2) | collective-permute-done | bytes 65568 | tf_op jit(solution)/shard_map/ppermute | solution.py:23
  112.0 1.9 collective-permute-start.3
  113.9 4.4 %fusion.5 = f32[256,4096]{1,0:T(8,128)} fusion(bf16[256,256]{0,1:T(8,128)(2,1)S(1)} %bitcast.69, bf16[4096,576]{1,0:T(8,128)(2,1)} %bitcast.62), kind=kOutput, calls=%fused_computation.9 | convolution fusion | flops 536870912 | bytes 6422528 | tf_op jit(solution)/shard_map/dot_general | solution.py:371
  118.3 2.3 %convolution_convert_fusion.x_ref = bf16[320,4096]{1,0:T(8,128)(2,1)} fusion(bf16[256,4096]{1,0:T(8,128)(2,1)S(1)} %bitcast.60, bf16[256,64]{0,1:T(8,128)(2,1)S(1)} %add_convert_fusion.1, bf16[256,256]{0,1:T(8,128)(2,1)S(1)} %bitcast.70), kind=kOutput, calls=%fused_computation.3 | convolution fusion | flops 672727040 | bytes 4882432 | tf_op jit(solution)/shard_map/dot_general | solution.py:377
  120.6 6.2 %shard_map.95.refs_1_ = bf16[16,320,128]{2,1,0:T(8,128)(2,1)} custom-call(bf16[320,4096]{1,0:T(8,128)(2,1)} %convolution_convert_fusion.x_ref), custom_call_target="tpu_custom_call" | custom-call | flops 655360 | bytes 5242880 | tf_op jit(solution)/shard_map/pallas_call | solution.py:277
  126.8 4.6 %fusion.2 = bf16[256,4096]{1,0:T(8,128)(2,1)} fusion(f32[256,4096]{1,0:T(8,128)} %fusion.5, bf16[256,64]{0,1:T(8,128)(2,1)S(1)} %add_convert_fusion.1, bf16[4096,576]{1,0:T(8,128)(2,1)} %bitcast.63), kind=kOutput, calls=%fused_computation.4 | convolution fusion | flops 136314880 | bytes 7372800 | tf_op jit(solution)/shard_map/dot_general | solution.py:374
  131.4 62.9 %shard_map.96 = (bf16[16,16,4096]{2,1,0:T(8,128)(2,1)}, bf16[16,320,128]{2,1,0:T(8,128)(2,1)}) custom-call(bf16[16,16,4096]{2,1,0:T(8,128)(2,1)} %bitcast.61, bf16[16,320,128]{2,1,0:T(8,128)(2,1)} %shard_map.95.refs_1_), custom_call_target="tpu_custom_call" | custom-call | bytes 6815744 | tf_op jit(solution)/shard_map/pallas_call | solution.py:100
  194.4 1.5 convert_reduce_fusion.1
  197.3 1.9 convert_reduce_fusion
  (35 shorter events, 7.7 us)
Async XLA Ops:
  82.5 3.8 %copy-start = (bf16[32,128,576]{2,1,0:T(8,128)(2,1)S(1)}, bf16[32,128,576]{2,1,0:T(8,128)(2,1)}, u32[]{:S(2)}) copy-start(bf16[32,128,576]{2,1,0:T(8,128)(2,1)} %get-tuple-element.8) | copy-start | bytes 14155780
  87.1 6.3 %collective-permute-start = (bf16[256,64]{0,1:T(8,128)(2,1)S(1)}, bf16[256,64]{0,1:T(8,128)(2,1)S(1)}, u32[]{:S(2)}, u32[]{:S(2)}) collective-permute-start(bf16[256,64]{0,1:T(8,128)(2,1)S(1)} %convolution_convert_fusion.2), channel_id=1, source_target_pairs={{0,1},{1,0},{2,3},{3,2},{4,5},{5,4},{6,7},{7,6},{8,9},{9,8},{10,11... | collective-permute-start | bytes 98312 | tf_op jit(solution)/shard_map/ppermute | solution.py:23
  91.2 1.9 copy-start.3
  93.4 8.1 %collective-permute-start.1 = (bf16[256,128]{0,1:T(8,128)(2,1)S(1)}, bf16[256,128]{0,1:T(8,128)(2,1)S(1)}, u32[]{:S(2)}, u32[]{:S(2)}) collective-permute-start(bf16[256,128]{0,1:T(8,128)(2,1)S(1)} %pad_maximum_fusion.2), channel_id=1, source_target_pairs={{0,2},{1,3},{2,0},{3,1},{4,6},{5,7},{6,4},{7,5},{8,10},{9,11},{10,... | collective-permute-start | bytes 196616 | tf_op jit(solution)/shard_map/ppermute | solution.py:23
  101.8 0.8 copy-start.4
  104.7 7.2 %collective-permute-start.2 = (bf16[256,128]{0,1:T(8,128)(2,1)S(1)}, bf16[256,128]{0,1:T(8,128)(2,1)S(1)}, u32[]{:S(2)}, u32[]{:S(2)}) collective-permute-start(bf16[256,128]{0,1:T(8,128)(2,1)S(1)} %get-tuple-element.23), channel_id=1, source_target_pairs={{0,2},{1,3},{2,0},{3,1},{4,6},{5,7},{6,4},{7,5},{8,10},{9,11},{10,... | collective-permute-start | bytes 196616 | tf_op jit(solution)/shard_map/ppermute | solution.py:23
  112.0 6.3 %collective-permute-start.3 = (bf16[256,64]{0,1:T(8,128)(2,1)S(1)}, bf16[256,64]{0,1:T(8,128)(2,1)S(1)}, u32[]{:S(2)}, u32[]{:S(2)}) collective-permute-start(bf16[256,64]{0,1:T(8,128)(2,1)S(1)} %select_convert_fusion.1), channel_id=1, source_target_pairs={{0,1},{1,0},{2,3},{3,2},{4,5},{5,4},{6,7},{7,6},{8,9},{9,8},{10,11... | collective-permute-start | bytes 98312 | tf_op jit(solution)/shard_map/ppermute | solution.py:23
  194.3 4.9 %copy-start.1 = (bf16[16,4096]{1,0:T(8,128)(2,1)S(1)}, bf16[16,4096]{1,0:T(8,128)(2,1)}, u32[]{:S(2)}) copy-start(bf16[16,4096]{1,0:T(8,128)(2,1)} %param.7) | copy-start | bytes 393220
  195.9 3.6 %copy-start.2 = (bf16[16,4096]{1,0:T(8,128)(2,1)S(1)}, bf16[16,4096]{1,0:T(8,128)(2,1)}, u32[]{:S(2)}) copy-start(bf16[16,4096]{1,0:T(8,128)(2,1)} %param.12) | copy-start | bytes 393220

commit v8 on v7

--- a/solution.py
+++ b/solution.py
@@ -293,6 +293,120 @@
     )(x)
 
 
+def _end_body(ring, x_ref, w_ref, o_ref, w_out, send_buf, recv_buf, cross_buf, cross_in,
+              t_send, t_recv, c_sem, w_send, w_recv, local_sem):
+    n_t = lax.axis_size("tensor")
+    n_d = lax.axis_size("dp")
+    t = lax.axis_index("tensor")
+    r = lax.axis_index("dp")
+    z = lax.rem(t, ring)
+    t_base = t - z
+    t_other = lax.rem(t + ring, n_t) - z
+    t_far = lax.rem(t + ring, n_t)
+    right = t_base + lax.rem(z + 1, ring)
+    left = t_base + lax.rem(z + ring - 1, ring)
+    parity = lax.rem(r, 2)
+    n_w = n_d // 2
+    me_w = r // 2
+    barrier = pltpu.get_barrier_semaphore()
+    for device in ({"tensor": t_far}, {"tensor": right}, {"tensor": left}):
+        pl.semaphore_signal(barrier, inc=1, device_id=device, device_id_type=MESH_ID)
+    for j in range(1, n_w):
+        peer = 2 * lax.rem(me_w + j, n_w) + parity
+        pl.semaphore_signal(barrier, inc=1, device_id={"dp": peer}, device_id_type=MESH_ID)
+    pl.semaphore_wait(barrier, 3 + n_w - 1)
+
+    def remote(src, dst, send, recv, device):
+        copy = pltpu.make_async_remote_copy(
+            src_ref=src, dst_ref=dst, send_sem=send, recv_sem=recv,
+            device_id=device, device_id_type=MESH_ID,
+        )
+        copy.start()
+        return copy
+
+    waits = []
+    for j in range(1, n_w):
+        peer = lax.rem(me_w + j, n_w)
+        waits.append(remote(w_ref.at[peer], w_out.at[me_w], w_send.at[j], w_recv.at[j],
+                            {"dp": 2 * peer + parity}))
+    own_w = pltpu.make_async_copy(w_ref.at[me_w], w_out.at[me_w], local_sem.at[0])
+    own_w.start()
+    steps = (ring // 2, ring - 1 - ring // 2)
+    moving = [None, None]
+    for s in range(max(steps)):
+        for d, (target, sign) in enumerate(((right, -1), (left, 1))):
+            if s >= steps[d]:
+                continue
+            q = lax.rem(z - sign * (steps[d] - s) + 2 * ring, ring)
+            sent = []
+            for h, start in enumerate((t_base, t_other)):
+                slot = start + q
+                if s == 0:
+                    src = x_ref.at[slot]
+                else:
+                    moving[d][h].wait_recv()
+                    send_buf[d, s, h] = (
+                        recv_buf[d, s - 1, h].astype(jnp.float32) + x_ref[slot].astype(jnp.float32)
+                    ).astype(send_buf.dtype)
+                    src = send_buf.at[d, s, h]
+                sent.append(remote(src, recv_buf.at[d, s, h], t_send.at[d, s, h],
+                                   t_recv.at[d, s, h], {"tensor": target}))
+            waits.extend(sent)
+            moving[d] = sent
+    for d in range(2):
+        for copy in moving[d]:
+            copy.wait_recv()
+    plus, minus = steps[0] - 1, steps[1] - 1
+    cross_buf[...] = (
+        x_ref[t_far].astype(jnp.float32)
+        + recv_buf[0, plus, 1].astype(jnp.float32)
+        + recv_buf[1, minus, 1].astype(jnp.float32)
+    ).astype(cross_buf.dtype)
+    crossed = remote(cross_buf, cross_in, c_sem.at[0], c_sem.at[1], {"tensor": t_far})
+    crossed.wait()
+    o_ref[...] = (
+        x_ref[t].astype(jnp.float32)
+        + recv_buf[0, plus, 0].astype(jnp.float32)
+        + recv_buf[1, minus, 0].astype(jnp.float32)
+        + cross_in[...].astype(jnp.float32)
+    )
+    for copy in waits:
+        copy.wait_send()
+    for j in range(1, n_w):
+        pltpu.make_async_copy(w_out.at[0], w_out.at[0], w_recv.at[j]).wait()
+    own_w.wait()
+
+
+def end_exchange(partial, paired, ring):
+    n_t, rows, cols = partial.shape
+    n_w = paired.shape[0]
+    piece = (rows, cols)
+    moved = 2 * (partial.size * partial.dtype.itemsize + paired.size * paired.dtype.itemsize)
+    return pl.pallas_call(
+        functools.partial(_end_body, ring),
+        out_shape=[
+            jax.ShapeDtypeStruct(piece, jnp.float32),
+            jax.ShapeDtypeStruct(paired.shape, paired.dtype),
+        ],
+        in_specs=[pl.BlockSpec(memory_space=pltpu.VMEM), pl.BlockSpec(memory_space=pl.ANY)],
+        out_specs=[pl.BlockSpec(memory_space=pltpu.VMEM), pl.BlockSpec(memory_space=pl.ANY)],
+        scratch_shapes=[
+            pltpu.VMEM((2, ring // 2, 2) + piece, partial.dtype),
+            pltpu.VMEM((2, ring // 2, 2) + piece, partial.dtype),
+            pltpu.VMEM(piece, partial.dtype),
+            pltpu.VMEM(piece, partial.dtype),
+            pltpu.SemaphoreType.DMA((2, ring // 2, 2)),
+            pltpu.SemaphoreType.DMA((2, ring // 2, 2)),
+            pltpu.SemaphoreType.DMA((2,)),
+            pltpu.SemaphoreType.DMA((n_w,)),
+            pltpu.SemaphoreType.DMA((n_w,)),
+            pltpu.SemaphoreType.DMA((1,)),
+        ],
+        compiler_params=pltpu.CompilerParams(collective_id=1, has_side_effects=True),
+        cost_estimate=pl.CostEstimate(flops=4 * partial.size, transcendentals=0, bytes_accessed=moved),
+    )(partial, paired)
+
+
 def local(tokens, norm_gain, query_weight, kv_weight, out_weight, grad_out, doc_lengths):
     tensor_size = lax.axis_size("tensor")
     data_size = lax.axis_size("dp")
@@ -379,14 +493,7 @@
     ).astype(jnp.bfloat16)
     block = weight_partial.shape[1] // data_size
     paired = pair_sum(weight_partial, block)
-    arrived, weight_arrived = push_exchange(
-        [
-            ("tensor", tensor_size, partial, True),
-            ("dp", data_size // 2, paired, True, 2),
-        ],
-        1,
-    )
-    normed_grad = jnp.sum(arrived.astype(jnp.float32), axis=0)
+    normed_grad, weight_arrived = end_exchange(partial, paired, RING)
     scaled = normed_grad * gain32
     correction = unit * jnp.mean(scaled * unit, axis=-1, keepdims=True)
     input_grad = (grad_out.astype(jnp.float32) + (scaled - correction) / root_mean[:, None]).astype(

time: 201 us -> 175 us (0.87)
  Pallas kernels: 143 us -> 119 us
    pallas_call x1, Pallas kernels: 62.9 us -> 38.6 us  [end_exchange(): pl.pallas_call(functools.partial(_end_body, ring), out_shape=[jax.ShapeDt...]
    unnamed x13 -> x15, local copies, waits for them, and re-layouts: 4.22 us -> 4.34 us
where the time goes in v8:
time: 175 us; the launch traced here: 174 us
  Pallas kernels  119 us (68%)
  matrix products  18.9 us (11%)
  waiting for transfers between devices  9.48 us (5%)
  starting transfers between devices  9.17 us (5%)
  other arithmetic  9.06 us (5%)
  local copies, waits for them, and re-layouts  7.72 us (4%)
    pallas_call x1, Pallas kernels, gather_start(): pl.pallas_call(functools.partial(_gather_start_body, ring), out_shape=[ja...  74.1 us
    pallas_call x1, Pallas kernels, end_exchange(): pl.pallas_call(functools.partial(_end_body, ring), out_shape=[jax.ShapeDt...  38.6 us
    ppermute x4, waiting for transfers between devices, partner_2(): return lax.ppermute(value, axis, pairs)  9.48 us
    ppermute x4, starting transfers between devices, partner_2(): return lax.ppermute(value, axis, pairs)  9.17 us
    pallas_call x1, Pallas kernels, pair_sum(): pl.pallas_call(_pair_body, out_shape=jax.ShapeDtypeStruct(shape, x.dtype)...  6.22 us
    dot_general x1, matrix products, local(): lax.dot_general(kv_grad, kv_local, contract_last, preferred_element_type=...  4.6 us
    dot_general x1, matrix products, local(): lax.dot_general(query_grad, query_full, contract_last, preferred_element_...  4.37 us
    unnamed x15, local copies, waits for them, and re-layouts  4.34 us
  transfers between devices with their start and end apart: 4, of which 2 were waited for; matrix products, arithmetic and copies ran while one was open for 5% of the time, Pallas kernels for 0%

profile of v8, /device:TPU:1, one launch (start us, length us, event | category | flops | bytes accessed | tf_op | source)
XLA Modules:
  0.0 174.1 jit_solution(4223644518650091681)
XLA Ops:
  1.3 1.0 fusion.29
  2.4 0.9 copy.20
  4.2 1.0 fusion.37
  5.2 1.6 pad_maximum_fusion.pieces_ref
  6.8 1.6 pad_maximum_fusion.1.weights_ref
  8.4 74.1 %shard_map.94 = (bf16[16,2,16,4096]{3,2,1,0:T(8,128)(2,1)}, bf16[32,128,576]{2,1,0:T(8,128)(2,1)}) custom-call(bf16[2,16,4096]{2,1,0:T(8,128)(2,1)} %pad_maximum_fusion.pieces_ref, bf16[128,576]{1,0:T(8,128)(2,1)} %pad_maximum_fusion.1.weights_ref), custom_call_target="tpu_custom_call" | custom-call | bytes 17825792 | tf_op jit(solution)/shard_map/pallas_call | solution.py:220
  82.5 2.7 %fusion.55 = (bf16[16,1,16,4096]{3,2,1,0:T(8,128)(2,1)S(1)}, bf16[16,1,16,4096]{3,2,1,0:T(8,128)(2,1)S(1)}) fusion(bf16[16,2,16,4096]{3,2,1,0:T(8,128)(2,1)} %get-tuple-element.7), kind=kLoop, calls=%fused_computation.77 | loop fusion | bytes 8388608 | tf_op jit(solution)/shard_map/slice | solution.py:428
  85.3 1.0 copy-done
  87.1 3.1 %collective-permute-start = (bf16[256,64]{0,1:T(8,128)(2,1)S(1)}, bf16[256,64]{0,1:T(8,128)(2,1)S(1)}, u32[]{:S(2)}, u32[]{:S(2)}) collective-permute-start(bf16[256,64]{0,1:T(8,128)(2,1)S(1)} %convolution_convert_fusion.2), channel_id=1, source_target_pairs={{0,1},{1,0},{2,3},{3,2},{4,5},{5,4},{6,7},{7,6},{8,9},{9,8},{10,11... | collective-permute-start | bytes 98312 | tf_op jit(solution)/shard_map/ppermute | solution.py:23
  90.2 1.0 fusion.17
  91.2 1.9 %fusion.20 = bf16[256,256]{0,1:T(8,128)(2,1)S(1)} fusion(bf16[256,4096]{1,0:T(8,128)(2,1)S(1)} %bitcast.67, bf16[4096,576]{1,0:T(8,128)(2,1)S(1)} %bitcast.66), kind=kOutput, calls=%fused_computation.24 | convolution fusion | flops 536936448 | bytes 4325376 | tf_op jit(solution)/shard_map/dot_general | solution.py:449
  93.4 2.2 %collective-permute-start.1 = (bf16[256,128]{0,1:T(8,128)(2,1)S(1)}, bf16[256,128]{0,1:T(8,128)(2,1)S(1)}, u32[]{:S(2)}, u32[]{:S(2)}) collective-permute-start(bf16[256,128]{0,1:T(8,128)(2,1)S(1)} %pad_maximum_fusion.2), channel_id=1, source_target_pairs={{0,2},{1,3},{2,0},{3,1},{4,6},{5,7},{6,4},{7,5},{8,10},{9,11},{10,... | collective-permute-start | bytes 196616 | tf_op jit(solution)/shard_map/ppermute | solution.py:23
  95.7 5.7 %collective-permute-done.1 = bf16[256,128]{0,1:T(8,128)(2,1)S(1)} collective-permute-done((bf16[256,128]{0,1:T(8,128)(2,1)S(1)}, bf16[256,128]{0,1:T(8,128)(2,1)S(1)}, u32[]{:S(2)}, u32[]{:S(2)}) %collective-permute-start.1) | collective-permute-done | bytes 65568 | tf_op jit(solution)/shard_map/ppermute | solution.py:23
  103.1 1.6 select_convert_fusion
  104.7 1.9 %collective-permute-start.2 = (bf16[256,128]{0,1:T(8,128)(2,1)S(1)}, bf16[256,128]{0,1:T(8,128)(2,1)S(1)}, u32[]{:S(2)}, u32[]{:S(2)}) collective-permute-start(bf16[256,128]{0,1:T(8,128)(2,1)S(1)} %get-tuple-element.23), channel_id=1, source_target_pairs={{0,2},{1,3},{2,0},{3,1},{4,6},{5,7},{6,4},{7,5},{8,10},{9,11},{10,... | collective-permute-start | bytes 196616 | tf_op jit(solution)/shard_map/ppermute | solution.py:23
  106.6 1.6 convolution_convert_fusion.1
  108.2 3.7 %collective-permute-done.2 = bf16[256,128]{0,1:T(8,128)(2,1)S(1)} collective-permute-done((bf16[256,128]{0,1:T(8,128)(2,1)S(1)}, bf16[256,128]{0,1:T(8,128)(2,1)S(1)}, u32[]{:S(2)}, u32[]{:S(2)}) %collective-permute-start.2) | collective-permute-done | bytes 65568 | tf_op jit(solution)/shard_map/ppermute | solution.py:23
  112.0 1.9 %collective-permute-start.3 = (bf16[256,64]{0,1:T(8,128)(2,1)S(1)}, bf16[256,64]{0,1:T(8,128)(2,1)S(1)}, u32[]{:S(2)}, u32[]{:S(2)}) collective-permute-start(bf16[256,64]{0,1:T(8,128)(2,1)S(1)} %select_convert_fusion.1), channel_id=1, source_target_pairs={{0,1},{1,0},{2,3},{3,2},{4,5},{5,4},{6,7},{7,6},{8,9},{9,8},{10,11... | collective-permute-start | bytes 98312 | tf_op jit(solution)/shard_map/ppermute | solution.py:23
  113.9 4.4 %fusion.5 = f32[256,4096]{1,0:T(8,128)} fusion(bf16[256,256]{0,1:T(8,128)(2,1)S(1)} %bitcast.69, bf16[4096,576]{1,0:T(8,128)(2,1)} %bitcast.62), kind=kOutput, calls=%fused_computation.8 | convolution fusion | flops 536870912 | bytes 6422528 | tf_op jit(solution)/shard_map/dot_general | solution.py:485
  118.3 2.3 %convolution_convert_fusion.x_ref = bf16[320,4096]{1,0:T(8,128)(2,1)} fusion(bf16[256,4096]{1,0:T(8,128)(2,1)S(1)} %bitcast.60, bf16[256,64]{0,1:T(8,128)(2,1)S(1)} %add_convert_fusion.1, bf16[256,256]{0,1:T(8,128)(2,1)S(1)} %bitcast.70), kind=kOutput, calls=%fused_computation.3 | convolution fusion | flops 672727040 | bytes 4882432 | tf_op jit(solution)/shard_map/dot_general | solution.py:491
  120.6 6.2 %shard_map.95.w_ref = bf16[16,320,128]{2,1,0:T(8,128)(2,1)} custom-call(bf16[320,4096]{1,0:T(8,128)(2,1)} %convolution_convert_fusion.x_ref), custom_call_target="tpu_custom_call" | custom-call | flops 655360 | bytes 5242880 | tf_op jit(solution)/shard_map/pallas_call | solution.py:277
  126.8 4.6 %fusion.2 = bf16[256,4096]{1,0:T(8,128)(2,1)} fusion(f32[256,4096]{1,0:T(8,128)} %fusion.5, bf16[256,64]{0,1:T(8,128)(2,1)S(1)} %add_convert_fusion.1, bf16[4096,576]{1,0:T(8,128)(2,1)} %bitcast.63), kind=kOutput, calls=%fused_computation.4 | convolution fusion | flops 136314880 | bytes 7372800 | tf_op jit(solution)/shard_map/dot_general | solution.py:488
  131.4 38.6 %shard_map.96 = (f32[16,4096]{1,0:T(8,128)}, bf16[16,320,128]{2,1,0:T(8,128)(2,1)}) custom-call(bf16[16,16,4096]{2,1,0:T(8,128)(2,1)} %bitcast.61, bf16[16,320,128]{2,1,0:T(8,128)(2,1)} %shard_map.95.w_ref), custom_call_target="tpu_custom_call" | custom-call | flops 4194304 | bytes 6815744 | tf_op jit(solution)/shard_map/pallas_call | solution.py:385
  170.1 1.5 convert_reduce_fusion
  (36 shorter events, 6.9 us)
Async XLA Ops:
  82.5 3.8 %copy-start = (bf16[32,128,576]{2,1,0:T(8,128)(2,1)S(1)}, bf16[32,128,576]{2,1,0:T(8,128)(2,1)}, u32[]{:S(2)}) copy-start(bf16[32,128,576]{2,1,0:T(8,128)(2,1)} %get-tuple-element.8) | copy-start | bytes 14155780
  87.1 6.3 %collective-permute-start = (bf16[256,64]{0,1:T(8,128)(2,1)S(1)}, bf16[256,64]{0,1:T(8,128)(2,1)S(1)}, u32[]{:S(2)}, u32[]{:S(2)}) collective-permute-start(bf16[256,64]{0,1:T(8,128)(2,1)S(1)} %convolution_convert_fusion.2), channel_id=1, source_target_pairs={{0,1},{1,0},{2,3},{3,2},{4,5},{5,4},{6,7},{7,6},{8,9},{9,8},{10,11... | collective-permute-start | bytes 98312 | tf_op jit(solution)/shard_map/ppermute | solution.py:23
  91.2 1.9 %copy-start.4 = (s32[1,4]{1,0:T(1,128)S(1)}, s32[1,4]{1,0:T(1,128)}, u32[]{:S(2)}) copy-start(s32[1,4]{1,0:T(1,128)} %param.13) | copy-start | bytes 52
  93.4 8.1 %collective-permute-start.1 = (bf16[256,128]{0,1:T(8,128)(2,1)S(1)}, bf16[256,128]{0,1:T(8,128)(2,1)S(1)}, u32[]{:S(2)}, u32[]{:S(2)}) collective-permute-start(bf16[256,128]{0,1:T(8,128)(2,1)S(1)} %pad_maximum_fusion.2), channel_id=1, source_target_pairs={{0,2},{1,3},{2,0},{3,1},{4,6},{5,7},{6,4},{7,5},{8,10},{9,11},{10,... | collective-permute-start | bytes 196616 | tf_op jit(solution)/shard_map/ppermute | solution.py:23
  101.8 0.8 copy-start.5
  104.7 7.2 %collective-permute-start.2 = (bf16[256,128]{0,1:T(8,128)(2,1)S(1)}, bf16[256,128]{0,1:T(8,128)(2,1)S(1)}, u32[]{:S(2)}, u32[]{:S(2)}) collective-permute-start(bf16[256,128]{0,1:T(8,128)(2,1)S(1)} %get-tuple-element.23), channel_id=1, source_target_pairs={{0,2},{1,3},{2,0},{3,1},{4,6},{5,7},{6,4},{7,5},{8,10},{9,11},{10,... | collective-permute-start | bytes 196616 | tf_op jit(solution)/shard_map/ppermute | solution.py:23
  112.0 6.3 %collective-permute-start.3 = (bf16[256,64]{0,1:T(8,128)(2,1)S(1)}, bf16[256,64]{0,1:T(8,128)(2,1)S(1)}, u32[]{:S(2)}, u32[]{:S(2)}) collective-permute-start(bf16[256,64]{0,1:T(8,128)(2,1)S(1)} %select_convert_fusion.1), channel_id=1, source_target_pairs={{0,1},{1,0},{2,3},{3,2},{4,5},{5,4},{6,7},{7,6},{8,9},{9,8},{10,11... | collective-permute-start | bytes 98312 | tf_op jit(solution)/shard_map/ppermute | solution.py:23
  131.4 41.6 %copy-start.1 = (bf16[16,4096]{1,0:T(8,128)(2,1)S(1)}, bf16[16,4096]{1,0:T(8,128)(2,1)}, u32[]{:S(2)}) copy-start(bf16[16,4096]{1,0:T(8,128)(2,1)} %param.7) | copy-start | bytes 393220
  170.1 3.0 %copy-start.2 = (f32[16,4096]{1,0:T(8,128)S(1)}, f32[16,4096]{1,0:T(8,128)}, u32[]{:S(2)}) copy-start(f32[16,4096]{1,0:T(8,128)} %get-tuple-element.9) | copy-start | bytes 786436
  170.1 3.2 %copy-start.3 = (bf16[16,4096]{1,0:T(8,128)(2,1)S(1)}, bf16[16,4096]{1,0:T(8,128)(2,1)}, u32[]{:S(2)}) copy-start(bf16[16,4096]{1,0:T(8,128)(2,1)} %param.12) | copy-start | bytes 393220

commit v9 on v8

--- a/solution.py
+++ b/solution.py
@@ -482,12 +482,11 @@
             handed.dtype
         )
     kv_grad = kv_partial.astype(jnp.bfloat16)
-    from_query = lax.dot_general(
-        query_grad, query_full, contract_last, preferred_element_type=jnp.float32
-    )
-    from_kv = lax.dot_general(kv_grad, kv_local, contract_last, preferred_element_type=jnp.float32)
-    partial = (from_query + from_kv).astype(jnp.bfloat16).reshape(tensor_size, rows, -1)
     combined = jnp.concatenate([query_grad, kv_grad], axis=1)
+    partial = lax.dot_general(
+        combined, weights_full[:, : query_width + kv_width], contract_last,
+        preferred_element_type=jnp.float32,
+    ).astype(jnp.bfloat16).reshape(tensor_size, rows, -1)
     weight_partial = lax.dot_general(
         combined, normed, (((0,), (0,)), ((), ())), preferred_element_type=jnp.float32
     ).astype(jnp.bfloat16)

time: 175 us -> 176 us (level)
  waiting for transfers between devices: 9.48 us -> 12.2 us
  matrix products: 18.9 us -> 16.4 us
    dot_general x2 -> x1, matrix products: 8.96 us -> 4.59 us  [local(): lax.dot_general(combined, weights_full[:, :query_width + kv_width], contr...]
    ppermute x4, waiting for transfers between devices: 9.48 us -> 12.2 us  [partner_2(): return lax.ppermute(value, axis, pairs)]
    unnamed x15 -> x13, local copies, waits for them, and re-layouts: 4.34 us -> 3.53 us
  transfers between devices with their start and end apart: 4 -> 4, of which waited for: 2 -> 3; matrix products, arithmetic and copies ran while one was open for 5% -> 3% of each run, Pallas kernels for 0% -> 0%
where the time goes in v9:
time: 176 us; the launch traced here: 175 us
  Pallas kernels  120 us (68%)
  matrix products  16.4 us (9%)
  waiting for transfers between devices  12.2 us (7%)
  starting transfers between devices  9.17 us (5%)
  other arithmetic  9.06 us (5%)
  local copies, waits for them, and re-layouts  6.91 us (4%)
    pallas_call x1, Pallas kernels, gather_start(): pl.pallas_call(functools.partial(_gather_start_body, ring), out_shape=[ja...  74.1 us
    pallas_call x1, Pallas kernels, end_exchange(): pl.pallas_call(functools.partial(_end_body, ring), out_shape=[jax.ShapeDt...  38.6 us
    ppermute x4, waiting for transfers between devices, partner_2(): return lax.ppermute(value, axis, pairs)  12.2 us
    ppermute x4, starting transfers between devices, partner_2(): return lax.ppermute(value, axis, pairs)  9.17 us
    pallas_call x1, Pallas kernels, pair_sum(): pl.pallas_call(_pair_body, out_shape=jax.ShapeDtypeStruct(shape, x.dtype)...  7.33 us
    dot_general x1, matrix products, local(): lax.dot_general(combined, weights_full[:, :query_width + kv_width], contr...  4.59 us
    unnamed x13, local copies, waits for them, and re-layouts  3.53 us
  transfers between devices with their start and end apart: 4, of which 3 were waited for; matrix products, arithmetic and copies ran while one was open for 3% of the time, Pallas kernels for 0%

profile of v9, /device:TPU:1, one launch (start us, length us, event | category | flops | bytes accessed | tf_op | source)
XLA Modules:
  0.0 174.6 jit_solution(9967928356833923141)
XLA Ops:
  1.3 1.0 fusion.26
  4.2 1.0 fusion.31
  5.2 1.6 pad_maximum_fusion.pieces_ref
  6.8 1.6 pad_maximum_fusion.1.weights_ref
  8.4 74.1 %shard_map.94 = (bf16[16,2,16,4096]{3,2,1,0:T(8,128)(2,1)}, bf16[32,128,576]{2,1,0:T(8,128)(2,1)}) custom-call(bf16[2,16,4096]{2,1,0:T(8,128)(2,1)} %pad_maximum_fusion.pieces_ref, bf16[128,576]{1,0:T(8,128)(2,1)} %pad_maximum_fusion.1.weights_ref), custom_call_target="tpu_custom_call" | custom-call | bytes 17825792 | tf_op jit(solution)/shard_map/pallas_call | solution.py:220
  82.5 2.7 %fusion.50 = (bf16[16,1,16,4096]{3,2,1,0:T(8,128)(2,1)S(1)}, bf16[16,1,16,4096]{3,2,1,0:T(8,128)(2,1)S(1)}) fusion(bf16[16,2,16,4096]{3,2,1,0:T(8,128)(2,1)} %get-tuple-element.7), kind=kLoop, calls=%fused_computation.73 | loop fusion | bytes 8388608 | tf_op jit(solution)/shard_map/slice | solution.py:429
  87.1 3.1 %collective-permute-start = (bf16[256,64]{0,1:T(8,128)(2,1)S(1)}, bf16[256,64]{0,1:T(8,128)(2,1)S(1)}, u32[]{:S(2)}, u32[]{:S(2)}) collective-permute-start(bf16[256,64]{0,1:T(8,128)(2,1)S(1)} %convolution_convert_fusion.3), channel_id=1, source_target_pairs={{0,1},{1,0},{2,3},{3,2},{4,5},{5,4},{6,7},{7,6},{8,9},{9,8},{10,11... | collective-permute-start | bytes 98312 | tf_op jit(solution)/shard_map/ppermute | solution.py:23
  90.2 1.0 fusion.15
  91.2 1.9 %fusion.18 = bf16[256,256]{0,1:T(8,128)(2,1)S(1)} fusion(bf16[256,4096]{1,0:T(8,128)(2,1)S(1)} %bitcast.60, bf16[4096,576]{1,0:T(8,128)(2,1)S(1)} %bitcast.66), kind=kOutput, calls=%fused_computation.22 | convolution fusion | flops 536936448 | bytes 4325376 | tf_op jit(solution)/shard_map/dot_general | solution.py:449
  93.4 2.2 %collective-permute-start.1 = (bf16[256,128]{0,1:T(8,128)(2,1)S(1)}, bf16[256,128]{0,1:T(8,128)(2,1)S(1)}, u32[]{:S(2)}, u32[]{:S(2)}) collective-permute-start(bf16[256,128]{0,1:T(8,128)(2,1)S(1)} %pad_maximum_fusion.5), channel_id=1, source_target_pairs={{0,2},{1,3},{2,0},{3,1},{4,6},{5,7},{6,4},{7,5},{8,10},{9,11},{10,... | collective-permute-start | bytes 196616 | tf_op jit(solution)/shard_map/ppermute | solution.py:23
  95.7 5.7 %collective-permute-done.1 = bf16[256,128]{0,1:T(8,128)(2,1)S(1)} collective-permute-done((bf16[256,128]{0,1:T(8,128)(2,1)S(1)}, bf16[256,128]{0,1:T(8,128)(2,1)S(1)}, u32[]{:S(2)}, u32[]{:S(2)}) %collective-permute-start.1) | collective-permute-done | bytes 65568 | tf_op jit(solution)/shard_map/ppermute | solution.py:23
  101.5 1.1 fusion.51
  102.6 1.3 convolution_bitcast_fusion.2
  104.1 1.6 select_convert_fusion
  105.7 1.9 %collective-permute-start.2 = (bf16[256,128]{0,1:T(8,128)(2,1)S(1)}, bf16[256,128]{0,1:T(8,128)(2,1)S(1)}, u32[]{:S(2)}, u32[]{:S(2)}) collective-permute-start(bf16[256,128]{0,1:T(8,128)(2,1)S(1)} %get-tuple-element.23), channel_id=1, source_target_pairs={{0,2},{1,3},{2,0},{3,1},{4,6},{5,7},{6,4},{7,5},{8,10},{9,11},{10,... | collective-permute-start | bytes 196616 | tf_op jit(solution)/shard_map/ppermute | solution.py:23
  107.6 5.3 %collective-permute-done.2 = bf16[256,128]{0,1:T(8,128)(2,1)S(1)} collective-permute-done((bf16[256,128]{0,1:T(8,128)(2,1)S(1)}, bf16[256,128]{0,1:T(8,128)(2,1)S(1)}, u32[]{:S(2)}, u32[]{:S(2)}) %collective-permute-start.2) | collective-permute-done | bytes 65568 | tf_op jit(solution)/shard_map/ppermute | solution.py:23
  113.0 1.9 %collective-permute-start.3 = (bf16[256,64]{0,1:T(8,128)(2,1)S(1)}, bf16[256,64]{0,1:T(8,128)(2,1)S(1)}, u32[]{:S(2)}, u32[]{:S(2)}) collective-permute-start(bf16[256,64]{0,1:T(8,128)(2,1)S(1)} %select_convert_fusion.1), channel_id=1, source_target_pairs={{0,1},{1,0},{2,3},{3,2},{4,5},{5,4},{6,7},{7,6},{8,9},{9,8},{10,11... | collective-permute-start | bytes 98312 | tf_op jit(solution)/shard_map/ppermute | solution.py:23
  114.9 1.6 convolution_convert_fusion.2
  116.5 1.2 collective-permute-done.3
  117.7 4.6 %convolution_convert_fusion.1 = bf16[256,4096]{1,0:T(8,128)(2,1)} fusion(bf16[4096,576]{1,0:T(8,128)(2,1)} %bitcast.63, bf16[256,64]{0,1:T(8,128)(2,1)S(1)} %add_convert_fusion.1, bf16[256,256]{0,1:T(8,128)(2,1)S(1)} %bitcast.69), kind=kOutput, calls=%fused_computation.3 | convolution fusion | flops 672464896 | bytes 5406720 | tf_op jit(solution)/shard_map/dot_general | solution.py:486
  122.2 2.4 %convolution_convert_fusion.x_ref = bf16[320,4096]{1,0:T(8,128)(2,1)} fusion(bf16[256,4096]{1,0:T(8,128)(2,1)S(1)} %bitcast.58, bf16[256,64]{0,1:T(8,128)(2,1)S(1)} %add_convert_fusion.1, bf16[256,256]{0,1:T(8,128)(2,1)S(1)} %bitcast.70), kind=kOutput, calls=%fused_computation.2 | convolution fusion | flops 672727040 | bytes 4882432 | tf_op jit(solution)/shard_map/dot_general | solution.py:490
  124.6 7.3 %shard_map.95.w_ref = bf16[16,320,128]{2,1,0:T(8,128)(2,1)} custom-call(bf16[320,4096]{1,0:T(8,128)(2,1)} %convolution_convert_fusion.x_ref), custom_call_target="tpu_custom_call" | custom-call | flops 655360 | bytes 5242880 | tf_op jit(solution)/shard_map/pallas_call | solution.py:277
  131.9 38.6 %shard_map.96 = (f32[16,4096]{1,0:T(8,128)}, bf16[16,320,128]{2,1,0:T(8,128)(2,1)}) custom-call(bf16[16,16,4096]{2,1,0:T(8,128)(2,1)} %bitcast.59, bf16[16,320,128]{2,1,0:T(8,128)(2,1)} %shard_map.95.w_ref), custom_call_target="tpu_custom_call" | custom-call | flops 4194304 | bytes 6815744 | tf_op jit(solution)/shard_map/pallas_call | solution.py:385
  170.6 1.5 convert_reduce_fusion
  (33 shorter events, 7.4 us)
Async XLA Ops:
  82.5 3.8 %copy-start.3 = (bf16[32,128,576]{2,1,0:T(8,128)(2,1)S(1)}, bf16[32,128,576]{2,1,0:T(8,128)(2,1)}, u32[]{:S(2)}) copy-start(bf16[32,128,576]{2,1,0:T(8,128)(2,1)} %get-tuple-element.8) | copy-start | bytes 14155780
  87.1 6.3 %collective-permute-start = (bf16[256,64]{0,1:T(8,128)(2,1)S(1)}, bf16[256,64]{0,1:T(8,128)(2,1)S(1)}, u32[]{:S(2)}, u32[]{:S(2)}) collective-permute-start(bf16[256,64]{0,1:T(8,128)(2,1)S(1)} %convolution_convert_fusion.3), channel_id=1, source_target_pairs={{0,1},{1,0},{2,3},{3,2},{4,5},{5,4},{6,7},{7,6},{8,9},{9,8},{10,11... | collective-permute-start | bytes 98312 | tf_op jit(solution)/shard_map/ppermute | solution.py:23
  91.2 1.9 %copy-start.4 = (s32[1,4]{1,0:T(1,128)S(1)}, s32[1,4]{1,0:T(1,128)}, u32[]{:S(2)}) copy-start(s32[1,4]{1,0:T(1,128)} %param.13) | copy-start | bytes 52
  93.4 8.1 %collective-permute-start.1 = (bf16[256,128]{0,1:T(8,128)(2,1)S(1)}, bf16[256,128]{0,1:T(8,128)(2,1)S(1)}, u32[]{:S(2)}, u32[]{:S(2)}) collective-permute-start(bf16[256,128]{0,1:T(8,128)(2,1)S(1)} %pad_maximum_fusion.5), channel_id=1, source_target_pairs={{0,2},{1,3},{2,0},{3,1},{4,6},{5,7},{6,4},{7,5},{8,10},{9,11},{10,... | collective-permute-start | bytes 196616 | tf_op jit(solution)/shard_map/ppermute | solution.py:23
  105.7 7.2 %collective-permute-start.2 = (bf16[256,128]{0,1:T(8,128)(2,1)S(1)}, bf16[256,128]{0,1:T(8,128)(2,1)S(1)}, u32[]{:S(2)}, u32[]{:S(2)}) collective-permute-start(bf16[256,128]{0,1:T(8,128)(2,1)S(1)} %get-tuple-element.23), channel_id=1, source_target_pairs={{0,2},{1,3},{2,0},{3,1},{4,6},{5,7},{6,4},{7,5},{8,10},{9,11},{10,... | collective-permute-start | bytes 196616 | tf_op jit(solution)/shard_map/ppermute | solution.py:23
  113.0 4.7 %collective-permute-start.3 = (bf16[256,64]{0,1:T(8,128)(2,1)S(1)}, bf16[256,64]{0,1:T(8,128)(2,1)S(1)}, u32[]{:S(2)}, u32[]{:S(2)}) collective-permute-start(bf16[256,64]{0,1:T(8,128)(2,1)S(1)} %select_convert_fusion.1), channel_id=1, source_target_pairs={{0,1},{1,0},{2,3},{3,2},{4,5},{5,4},{6,7},{7,6},{8,9},{9,8},{10,11... | collective-permute-start | bytes 98312 | tf_op jit(solution)/shard_map/ppermute | solution.py:23
  131.9 40.9 %copy-start = (bf16[16,4096]{1,0:T(8,128)(2,1)S(1)}, bf16[16,4096]{1,0:T(8,128)(2,1)}, u32[]{:S(2)}) copy-start(bf16[16,4096]{1,0:T(8,128)(2,1)} %param.7) | copy-start | bytes 393220
  170.6 2.2 %copy-start.1 = (f32[16,4096]{1,0:T(8,128)S(1)}, f32[16,4096]{1,0:T(8,128)}, u32[]{:S(2)}) copy-start(f32[16,4096]{1,0:T(8,128)} %get-tuple-element.9) | copy-start | bytes 786436
  170.6 2.5 %copy-start.2 = (bf16[16,4096]{1,0:T(8,128)(2,1)S(1)}, bf16[16,4096]{1,0:T(8,128)(2,1)}, u32[]{:S(2)}) copy-start(bf16[16,4096]{1,0:T(8,128)(2,1)} %param.12) | copy-start | bytes 393220

commit v10 on v8

--- a/solution.py
+++ b/solution.py
@@ -293,8 +293,9 @@
     )(x)
 
 
-def _end_body(ring, x_ref, w_ref, o_ref, w_out, send_buf, recv_buf, cross_buf, cross_in,
-              t_send, t_recv, c_sem, w_send, w_recv, local_sem):
+def _end_body(ring, x_ref, g_ref, o_ref, w_out, send_buf, recv_buf, cross_buf, cross_in,
+              mine, theirs, w_ref, t_send, t_recv, c_sem, w_send, w_recv, p_send, p_recv, p_local,
+              local_sem):
     n_t = lax.axis_size("tensor")
     n_d = lax.axis_size("dp")
     t = lax.axis_index("tensor")
@@ -306,15 +307,17 @@
     right = t_base + lax.rem(z + 1, ring)
     left = t_base + lax.rem(z + ring - 1, ring)
     parity = lax.rem(r, 2)
+    pair = r + 1 - 2 * parity
     n_w = n_d // 2
     me_w = r // 2
+    width = mine.shape[2]
     barrier = pltpu.get_barrier_semaphore()
-    for device in ({"tensor": t_far}, {"tensor": right}, {"tensor": left}):
+    for device in ({"tensor": t_far}, {"tensor": right}, {"tensor": left}, {"dp": pair}):
         pl.semaphore_signal(barrier, inc=1, device_id=device, device_id_type=MESH_ID)
     for j in range(1, n_w):
         peer = 2 * lax.rem(me_w + j, n_w) + parity
         pl.semaphore_signal(barrier, inc=1, device_id={"dp": peer}, device_id_type=MESH_ID)
-    pl.semaphore_wait(barrier, 3 + n_w - 1)
+    pl.semaphore_wait(barrier, 4 + n_w - 1)
 
     def remote(src, dst, send, recv, device):
         copy = pltpu.make_async_remote_copy(
@@ -325,15 +328,34 @@
         return copy
 
     waits = []
-    for j in range(1, n_w):
-        peer = lax.rem(me_w + j, n_w)
-        waits.append(remote(w_ref.at[peer], w_out.at[me_w], w_send.at[j], w_recv.at[j],
-                            {"dp": 2 * peer + parity}))
-    own_w = pltpu.make_async_copy(w_ref.at[me_w], w_out.at[me_w], local_sem.at[0])
-    own_w.start()
+    swapped = []
+    kept = []
+    for i in range(n_w):
+        give = pl.ds(pl.multiple_of((2 * i + 1 - parity) * width, width), width)
+        keep = pl.ds(pl.multiple_of((2 * i + parity) * width, width), width)
+        swapped.append(remote(g_ref.at[:, give], theirs.at[i], p_send.at[i], p_recv.at[i],
+                              {"dp": pair}))
+        own = pltpu.make_async_copy(g_ref.at[:, keep], mine.at[i], p_local.at[i])
+        own.start()
+        kept.append(own)
     steps = (ring // 2, ring - 1 - ring // 2)
     moving = [None, None]
+    own_w = None
     for s in range(max(steps)):
+        if s == 1:
+            for copy in swapped:
+                copy.wait()
+            for copy in kept:
+                copy.wait()
+            w_ref[...] = (
+                mine[...].astype(jnp.float32) + theirs[...].astype(jnp.float32)
+            ).astype(w_ref.dtype)
+            for j in range(1, n_w):
+                peer = lax.rem(me_w + j, n_w)
+                waits.append(remote(w_ref.at[peer], w_out.at[me_w], w_send.at[j], w_recv.at[j],
+                                    {"dp": 2 * peer + parity}))
+            own_w = pltpu.make_async_copy(w_ref.at[me_w], w_out.at[me_w], local_sem.at[0])
+            own_w.start()
         for d, (target, sign) in enumerate(((right, -1), (left, 1))):
             if s >= steps[d]:
                 continue
@@ -377,16 +399,19 @@
     own_w.wait()
 
 
-def end_exchange(partial, paired, ring):
+def end_exchange(partial, g, ring):
     n_t, rows, cols = partial.shape
-    n_w = paired.shape[0]
+    n_w = lax.axis_size("dp") // 2
+    g_rows, g_cols = g.shape
+    width = g_cols // (2 * n_w)
+    slots = (n_w, g_rows, width)
     piece = (rows, cols)
-    moved = 2 * (partial.size * partial.dtype.itemsize + paired.size * paired.dtype.itemsize)
+    moved = 2 * (partial.size * partial.dtype.itemsize + g.size * g.dtype.itemsize)
     return pl.pallas_call(
         functools.partial(_end_body, ring),
         out_shape=[
             jax.ShapeDtypeStruct(piece, jnp.float32),
-            jax.ShapeDtypeStruct(paired.shape, paired.dtype),
+            jax.ShapeDtypeStruct(slots, g.dtype),
         ],
         in_specs=[pl.BlockSpec(memory_space=pltpu.VMEM), pl.BlockSpec(memory_space=pl.ANY)],
         out_specs=[pl.BlockSpec(memory_space=pltpu.VMEM), pl.BlockSpec(memory_space=pl.ANY)],
@@ -395,16 +420,22 @@
             pltpu.VMEM((2, ring // 2, 2) + piece, partial.dtype),
             pltpu.VMEM(piece, partial.dtype),
             pltpu.VMEM(piece, partial.dtype),
+            pltpu.VMEM(slots, g.dtype),
+            pltpu.VMEM(slots, g.dtype),
+            pltpu.VMEM(slots, g.dtype),
             pltpu.SemaphoreType.DMA((2, ring // 2, 2)),
             pltpu.SemaphoreType.DMA((2, ring // 2, 2)),
             pltpu.SemaphoreType.DMA((2,)),
+            pltpu.SemaphoreType.DMA((n_w,)),
+            pltpu.SemaphoreType.DMA((n_w,)),
+            pltpu.SemaphoreType.DMA((n_w,)),
             pltpu.SemaphoreType.DMA((n_w,)),
             pltpu.SemaphoreType.DMA((n_w,)),
             pltpu.SemaphoreType.DMA((1,)),
         ],
         compiler_params=pltpu.CompilerParams(collective_id=1, has_side_effects=True),
         cost_estimate=pl.CostEstimate(flops=4 * partial.size, transcendentals=0, bytes_accessed=moved),
-    )(partial, paired)
+    )(partial, g)
 
 
 def local(tokens, norm_gain, query_weight, kv_weight, out_weight, grad_out, doc_lengths):
@@ -492,8 +523,7 @@
         combined, normed, (((0,), (0,)), ((), ())), preferred_element_type=jnp.float32
     ).astype(jnp.bfloat16)
     block = weight_partial.shape[1] // data_size
-    paired = pair_sum(weight_partial, block)
-    normed_grad, weight_arrived = end_exchange(partial, paired, RING)
+    normed_grad, weight_arrived = end_exchange(partial, weight_partial, RING)
     scaled = normed_grad * gain32
     correction = unit * jnp.mean(scaled * unit, axis=-1, keepdims=True)
     input_grad = (grad_out.astype(jnp.float32) + (scaled - correction) / root_mean[:, None]).astype(

time: 175 us -> 171 us (0.977)
  matrix products: 18.9 us -> 15.7 us
    pallas_call x1 -> x0, Pallas kernels: 6.22 us -> none  [pair_sum(): pl.pallas_call(_pair_body, out_shape=jax.ShapeDtypeStruct(shape, x.dtype)...]
    pallas_call x1, Pallas kernels: 38.6 us -> 44.2 us  [end_exchange(): pl.pallas_call(functools.partial(_end_body, ring), out_shape=[jax.ShapeDt...]
    dot_general x1, matrix products: 4.37 us -> 2.35 us  [local(): lax.dot_general(query_grad, query_full, contract_last, preferred_element_...]
  transfers between devices with their start and end apart: 4 -> 4, of which waited for: 2 -> 3; matrix products, arithmetic and copies ran while one was open for 5% -> 4% of each run, Pallas kernels for 0% -> 0%
where the time goes in v10:
time: 171 us
  Pallas kernels  118 us (69%)
  matrix products  15.7 us (9%)
  waiting for transfers between devices  9.86 us (6%)
  starting transfers between devices  9.17 us (5%)
  other arithmetic  9.06 us (5%)
  local copies, waits for them, and re-layouts  7.72 us (5%)
    pallas_call x1, Pallas kernels, gather_start(): pl.pallas_call(functools.partial(_gather_start_body, ring), out_shape=[ja...  74.1 us
    pallas_call x1, Pallas kernels, end_exchange(): pl.pallas_call(functools.partial(_end_body, ring), out_shape=[jax.ShapeDt...  44.2 us
    ppermute x4, waiting for transfers between devices, partner_2(): return lax.ppermute(value, axis, pairs)  9.86 us
    ppermute x4, starting transfers between devices, partner_2(): return lax.ppermute(value, axis, pairs)  9.17 us
    unnamed x15, local copies, waits for them, and re-layouts  4.34 us
  transfers between devices with their start and end apart: 4, of which 3 were waited for; matrix products, arithmetic and copies ran while one was open for 4% of the time, Pallas kernels for 0%

profile of v10, /device:TPU:1, one launch (start us, length us, event | category | flops | bytes accessed | tf_op | source)
XLA Modules:
  0.0 170.7 jit_solution(7744744464562956812)
XLA Ops:
  1.3 1.0 fusion.29
  2.4 0.9 copy.20
  3.3 0.8 copy.21
  4.2 1.0 fusion.37
  5.2 1.6 pad_maximum_fusion.pieces_ref
  6.8 1.6 pad_maximum_fusion.1.weights_ref
  8.4 74.1 %shard_map.94 = (bf16[16,2,16,4096]{3,2,1,0:T(8,128)(2,1)}, bf16[32,128,576]{2,1,0:T(8,128)(2,1)}) custom-call(bf16[2,16,4096]{2,1,0:T(8,128)(2,1)} %pad_maximum_fusion.pieces_ref, bf16[128,576]{1,0:T(8,128)(2,1)} %pad_maximum_fusion.1.weights_ref), custom_call_target="tpu_custom_call" | custom-call | bytes 17825792 | tf_op jit(solution)/shard_map/pallas_call | solution.py:220
  82.5 2.7 %fusion.55 = (bf16[16,1,16,4096]{3,2,1,0:T(8,128)(2,1)S(1)}, bf16[16,1,16,4096]{3,2,1,0:T(8,128)(2,1)S(1)}) fusion(bf16[16,2,16,4096]{3,2,1,0:T(8,128)(2,1)} %get-tuple-element.7), kind=kLoop, calls=%fused_computation.77 | loop fusion | bytes 8388608 | tf_op jit(solution)/shard_map/slice | solution.py:459
  85.3 1.0 copy-done
  87.1 3.1 %collective-permute-start = (bf16[256,64]{0,1:T(8,128)(2,1)S(1)}, bf16[256,64]{0,1:T(8,128)(2,1)S(1)}, u32[]{:S(2)}, u32[]{:S(2)}) collective-permute-start(bf16[256,64]{0,1:T(8,128)(2,1)S(1)} %convolution_convert_fusion.2), channel_id=1, source_target_pairs={{0,1},{1,0},{2,3},{3,2},{4,5},{5,4},{6,7},{7,6},{8,9},{9,8},{10,11... | collective-permute-start | bytes 98312 | tf_op jit(solution)/shard_map/ppermute | solution.py:23
  90.2 1.0 fusion.17
  91.2 1.9 %fusion.20 = bf16[256,256]{0,1:T(8,128)(2,1)S(1)} fusion(bf16[256,4096]{1,0:T(8,128)(2,1)S(1)} %bitcast.67, bf16[4096,576]{1,0:T(8,128)(2,1)S(1)} %bitcast.66), kind=kOutput, calls=%fused_computation.24 | convolution fusion | flops 536936448 | bytes 4325376 | tf_op jit(solution)/shard_map/dot_general | solution.py:480
  93.4 2.2 %collective-permute-start.1 = (bf16[256,128]{0,1:T(8,128)(2,1)S(1)}, bf16[256,128]{0,1:T(8,128)(2,1)S(1)}, u32[]{:S(2)}, u32[]{:S(2)}) collective-permute-start(bf16[256,128]{0,1:T(8,128)(2,1)S(1)} %pad_maximum_fusion.2), channel_id=1, source_target_pairs={{0,2},{1,3},{2,0},{3,1},{4,6},{5,7},{6,4},{7,5},{8,10},{9,11},{10,... | collective-permute-start | bytes 196616 | tf_op jit(solution)/shard_map/ppermute | solution.py:23
  95.7 5.7 %collective-permute-done.1 = bf16[256,128]{0,1:T(8,128)(2,1)S(1)} collective-permute-done((bf16[256,128]{0,1:T(8,128)(2,1)S(1)}, bf16[256,128]{0,1:T(8,128)(2,1)S(1)}, u32[]{:S(2)}, u32[]{:S(2)}) %collective-permute-start.1) | collective-permute-done | bytes 65568 | tf_op jit(solution)/shard_map/ppermute | solution.py:23
  103.1 1.6 select_convert_fusion
  104.7 1.9 %collective-permute-start.2 = (bf16[256,128]{0,1:T(8,128)(2,1)S(1)}, bf16[256,128]{0,1:T(8,128)(2,1)S(1)}, u32[]{:S(2)}, u32[]{:S(2)}) collective-permute-start(bf16[256,128]{0,1:T(8,128)(2,1)S(1)} %get-tuple-element.23), channel_id=1, source_target_pairs={{0,2},{1,3},{2,0},{3,1},{4,6},{5,7},{6,4},{7,5},{8,10},{9,11},{10,... | collective-permute-start | bytes 196616 | tf_op jit(solution)/shard_map/ppermute | solution.py:23
  106.6 1.6 convolution_convert_fusion.1
  108.2 3.7 %collective-permute-done.2 = bf16[256,128]{0,1:T(8,128)(2,1)S(1)} collective-permute-done((bf16[256,128]{0,1:T(8,128)(2,1)S(1)}, bf16[256,128]{0,1:T(8,128)(2,1)S(1)}, u32[]{:S(2)}, u32[]{:S(2)}) %collective-permute-start.2) | collective-permute-done | bytes 65568 | tf_op jit(solution)/shard_map/ppermute | solution.py:23
  112.0 1.9 %collective-permute-start.3 = (bf16[256,64]{0,1:T(8,128)(2,1)S(1)}, bf16[256,64]{0,1:T(8,128)(2,1)S(1)}, u32[]{:S(2)}, u32[]{:S(2)}) collective-permute-start(bf16[256,64]{0,1:T(8,128)(2,1)S(1)} %select_convert_fusion.1), channel_id=1, source_target_pairs={{0,1},{1,0},{2,3},{3,2},{4,5},{5,4},{6,7},{7,6},{8,9},{9,8},{10,11... | collective-permute-start | bytes 98312 | tf_op jit(solution)/shard_map/ppermute | solution.py:23
  113.9 2.3 %fusion.5 = f32[256,4096]{1,0:T(8,128)S(1)} fusion(bf16[256,256]{0,1:T(8,128)(2,1)S(1)} %bitcast.69, bf16[4096,576]{1,0:T(8,128)(2,1)} %bitcast.62), kind=kOutput, calls=%fused_computation.8 | convolution fusion | flops 536870912 | bytes 6422528 | tf_op jit(solution)/shard_map/dot_general | solution.py:516
  116.6 2.4 %convolution_convert_fusion.g_ref = bf16[320,4096]{1,0:T(8,128)(2,1)} fusion(bf16[256,4096]{1,0:T(8,128)(2,1)S(1)} %bitcast.60, bf16[256,64]{0,1:T(8,128)(2,1)S(1)} %add_convert_fusion.1, bf16[256,256]{0,1:T(8,128)(2,1)S(1)} %bitcast.70), kind=kOutput, calls=%fused_computation.3 | convolution fusion | flops 672727040 | bytes 4882432 | tf_op jit(solution)/shard_map/dot_general | solution.py:522
  119.0 3.4 %fusion.2 = bf16[256,4096]{1,0:T(8,128)(2,1)} fusion(f32[256,4096]{1,0:T(8,128)S(1)} %fusion.5, bf16[256,64]{0,1:T(8,128)(2,1)S(1)} %add_convert_fusion.1, bf16[4096,576]{1,0:T(8,128)(2,1)} %bitcast.63), kind=kOutput, calls=%fused_computation.4 | convolution fusion | flops 136314880 | bytes 7372800 | tf_op jit(solution)/shard_map/dot_general | solution.py:519
  122.4 44.2 %shard_map.95 = (f32[16,4096]{1,0:T(8,128)}, bf16[16,320,128]{2,1,0:T(8,128)(2,1)}) custom-call(bf16[16,16,4096]{2,1,0:T(8,128)(2,1)} %bitcast.61, bf16[320,4096]{1,0:T(8,128)(2,1)} %convolution_convert_fusion.g_ref), custom_call_target="tpu_custom_call" | custom-call | flops 4194304 | bytes 9437184 | tf_op jit(solution)/shard_map/pallas_call | solution.py:410
  166.6 1.6 convert_reduce_fusion
  (35 shorter events, 6.4 us)
Async XLA Ops:
  82.5 3.8 %copy-start = (bf16[32,128,576]{2,1,0:T(8,128)(2,1)S(1)}, bf16[32,128,576]{2,1,0:T(8,128)(2,1)}, u32[]{:S(2)}) copy-start(bf16[32,128,576]{2,1,0:T(8,128)(2,1)} %get-tuple-element.8) | copy-start | bytes 14155780
  87.1 6.3 %collective-permute-start = (bf16[256,64]{0,1:T(8,128)(2,1)S(1)}, bf16[256,64]{0,1:T(8,128)(2,1)S(1)}, u32[]{:S(2)}, u32[]{:S(2)}) collective-permute-start(bf16[256,64]{0,1:T(8,128)(2,1)S(1)} %convolution_convert_fusion.2), channel_id=1, source_target_pairs={{0,1},{1,0},{2,3},{3,2},{4,5},{5,4},{6,7},{7,6},{8,9},{9,8},{10,11... | collective-permute-start | bytes 98312 | tf_op jit(solution)/shard_map/ppermute | solution.py:23
  91.2 1.9 %copy-start.4 = (s32[1,4]{1,0:T(1,128)S(1)}, s32[1,4]{1,0:T(1,128)}, u32[]{:S(2)}) copy-start(s32[1,4]{1,0:T(1,128)} %param.13) | copy-start | bytes 52
  93.4 8.1 %collective-permute-start.1 = (bf16[256,128]{0,1:T(8,128)(2,1)S(1)}, bf16[256,128]{0,1:T(8,128)(2,1)S(1)}, u32[]{:S(2)}, u32[]{:S(2)}) collective-permute-start(bf16[256,128]{0,1:T(8,128)(2,1)S(1)} %pad_maximum_fusion.2), channel_id=1, source_target_pairs={{0,2},{1,3},{2,0},{3,1},{4,6},{5,7},{6,4},{7,5},{8,10},{9,11},{10,... | collective-permute-start | bytes 196616 | tf_op jit(solution)/shard_map/ppermute | solution.py:23
  101.8 0.8 copy-start.5
  104.7 7.2 %collective-permute-start.2 = (bf16[256,128]{0,1:T(8,128)(2,1)S(1)}, bf16[256,128]{0,1:T(8,128)(2,1)S(1)}, u32[]{:S(2)}, u32[]{:S(2)}) collective-permute-start(bf16[256,128]{0,1:T(8,128)(2,1)S(1)} %get-tuple-element.23), channel_id=1, source_target_pairs={{0,2},{1,3},{2,0},{3,1},{4,6},{5,7},{6,4},{7,5},{8,10},{9,11},{10,... | collective-permute-start | bytes 196616 | tf_op jit(solution)/shard_map/ppermute | solution.py:23
  112.0 4.7 %collective-permute-start.3 = (bf16[256,64]{0,1:T(8,128)(2,1)S(1)}, bf16[256,64]{0,1:T(8,128)(2,1)S(1)}, u32[]{:S(2)}, u32[]{:S(2)}) collective-permute-start(bf16[256,64]{0,1:T(8,128)(2,1)S(1)} %select_convert_fusion.1), channel_id=1, source_target_pairs={{0,1},{1,0},{2,3},{3,2},{4,5},{5,4},{6,7},{7,6},{8,9},{9,8},{10,11... | collective-permute-start | bytes 98312 | tf_op jit(solution)/shard_map/ppermute | solution.py:23
  166.6 2.3 %copy-start.1 = (bf16[16,4096]{1,0:T(8,128)(2,1)S(1)}, bf16[16,4096]{1,0:T(8,128)(2,1)}, u32[]{:S(2)}) copy-start(bf16[16,4096]{1,0:T(8,128)(2,1)} %param.7) | copy-start | bytes 393220
  166.6 2.2 %copy-start.2 = (f32[16,4096]{1,0:T(8,128)S(1)}, f32[16,4096]{1,0:T(8,128)}, u32[]{:S(2)}) copy-start(f32[16,4096]{1,0:T(8,128)} %get-tuple-element.9) | copy-start | bytes 786436
  166.6 2.5 %copy-start.3 = (bf16[16,4096]{1,0:T(8,128)(2,1)S(1)}, bf16[16,4096]{1,0:T(8,128)(2,1)}, u32[]{:S(2)}) copy-start(bf16[16,4096]{1,0:T(8,128)(2,1)} %param.12) | copy-start | bytes 393220

commit v11 on v10

--- a/solution.py
+++ b/solution.py
@@ -21,6 +21,10 @@
     mask = 2**bit
     pairs = [(source, source ^ mask) for source in range(lax.axis_size(axis))]
     return lax.ppermute(value, axis, pairs)
+
+
+def group_shift(size, group, k):
+    return [(i, i - i % group + (i % group + k) % group) for i in range(size)]
 
 
 def document_mask(lengths, length_total):
@@ -465,16 +469,13 @@
     out_full_t = weights_full[:, query_width + kv_width :]
     queries = jnp.dot(normed, query_full, preferred_element_type=jnp.float32).astype(jnp.bfloat16)
     keyvals = jnp.dot(normed, kv_local, preferred_element_type=jnp.float32).astype(jnp.bfloat16)
-    for bit_index in range(levels):
-        partner = partner_2(keyvals, "tensor", bit_index)
-        joined_upper_half = tensor_index >> bit_index & 1 == 1
-        keyvals = jnp.concatenate(
-            [
-                jnp.where(joined_upper_half, partner, keyvals),
-                jnp.where(joined_upper_half, keyvals, partner),
-            ],
-            axis=1,
-        )
+    slot = lax.rem(lax.axis_index("tensor"), sharers)
+    shifted = [keyvals]
+    for k in range(1, sharers):
+        shifted.append(lax.ppermute(keyvals, "tensor", group_shift(tensor_size, sharers, k)))
+    shifted = jnp.stack(shifted)
+    order = lax.rem(slot - jnp.arange(sharers) + sharers, sharers)
+    keyvals = jnp.moveaxis(jnp.take(shifted, order, axis=0), 0, 1).reshape(seq_length, -1)
     key_rows = keyvals[:, :HD]
     value_rows = keyvals[:, HD:]
     out_grad = jnp.dot(grad_full, out_full_t, preferred_element_type=jnp.float32).astype(
@@ -502,16 +503,14 @@
     )
     value_part = jnp.einsum("hqt,qhd->td", probs_low, out_heads, preferred_element_type=jnp.float32)
     kv_partial = jnp.concatenate([key_part, value_part], axis=1)
-    for bit_index in reversed(range(levels)):
-        half_cols = kv_partial.shape[1] // 2
-        upper_half = tensor_index >> bit_index & 1 == 1
-        lower_cols = kv_partial[:, :half_cols]
-        higher_cols = kv_partial[:, half_cols:]
-        kept = jnp.where(upper_half, higher_cols, lower_cols)
-        handed = jnp.where(upper_half, lower_cols, higher_cols)
-        kv_partial = kept + partner_2(handed.astype(jnp.bfloat16), "tensor", bit_index).astype(
-            handed.dtype
+    blocks = jnp.moveaxis(kv_partial.reshape(seq_length, sharers, -1), 1, 0)
+    kv_sum = jnp.take(blocks, slot, axis=0)
+    for k in range(1, sharers):
+        handed = jnp.take(blocks, lax.rem(slot + k, sharers), axis=0).astype(jnp.bfloat16)
+        kv_sum = kv_sum + lax.ppermute(handed, "tensor", group_shift(tensor_size, sharers, k)).astype(
+            jnp.float32
         )
+    kv_partial = kv_sum
     kv_grad = kv_partial.astype(jnp.bfloat16)
     from_query = lax.dot_general(
         query_grad, query_full, contract_last, preferred_element_type=jnp.float32

time: 171 us -> 174 us (1.018)
  starting transfers between devices: 9.17 us -> 16.9 us
  waiting for transfers between devices: 9.86 us -> 2.43 us
  matrix products: 15.7 us -> 17.5 us
    ppermute x4 -> x6, starting transfers between devices: 9.17 us -> 16.9 us  [the longest x3 8.69 us: local(): lax.ppermute(keyvals, 'tensor', group_shift(tensor_size, sharers, k))]
    ppermute x4 -> x6, waiting for transfers between devices: 9.86 us -> 2.43 us  [the longest x3 1.89 us: local(): lax.ppermute(handed, 'tensor', group_shift(tensor_size, sharers, k))]
    unnamed x15 -> x13, local copies, waits for them, and re-layouts: 4.34 us -> 3.42 us
  transfers between devices with their start and end apart: 4 -> 6, of which waited for: 3 -> 2; matrix products, arithmetic and copies ran while one was open for 4% -> 3% of each run, Pallas kernels for 0% -> 0%
where the time goes in v11:
time: 174 us; the launch traced here: 173 us
  Pallas kernels  119 us (68%)
  matrix products  17.5 us (10%)
  starting transfers between devices  16.9 us (10%)
  other arithmetic  9.19 us (5%)
  local copies, waits for them, and re-layouts  7.47 us (4%)
  waiting for transfers between devices  2.43 us (1%)
    pallas_call x1, Pallas kernels, gather_start(): pl.pallas_call(functools.partial(_gather_start_body, ring), out_shape=[ja...  74.1 us
    pallas_call x1, Pallas kernels, end_exchange(): pl.pallas_call(functools.partial(_end_body, ring), out_shape=[jax.ShapeDt...  44.8 us
    ppermute x3, starting transfers between devices, local(): lax.ppermute(keyvals, 'tensor', group_shift(tensor_size, sharers, k))  8.69 us
    ppermute x3, starting transfers between devices, local(): lax.ppermute(handed, 'tensor', group_shift(tensor_size, sharers, k))  8.17 us
  transfers between devices with their start and end apart: 6, of which 2 were waited for; matrix products, arithmetic and copies ran while one was open for 3% of the time, Pallas kernels for 0%

profile of v11, /device:TPU:1, one launch (start us, length us, event | category | flops | bytes accessed | tf_op | source)
XLA Modules:
  0.0 173.3 jit_solution(16638274891017141099)
XLA Ops:
  1.3 1.0 fusion.29
  4.2 1.0 fusion.37
  5.2 1.6 pad_maximum_fusion.pieces_ref
  6.8 1.6 pad_maximum_fusion.2.weights_ref
  8.4 74.1 %shard_map.94 = (bf16[16,2,16,4096]{3,2,1,0:T(8,128)(2,1)}, bf16[32,128,576]{2,1,0:T(8,128)(2,1)}) custom-call(bf16[2,16,4096]{2,1,0:T(8,128)(2,1)} %pad_maximum_fusion.pieces_ref, bf16[128,576]{1,0:T(8,128)(2,1)} %pad_maximum_fusion.2.weights_ref), custom_call_target="tpu_custom_call" | custom-call | bytes 17825792 | tf_op jit(solution)/shard_map/pallas_call | solution.py:224
  82.5 2.9 %fusion.52 = (bf16[16,1,16,4096]{3,2,1,0:T(8,128)(2,1)S(1)}, bf16[16,1,16,4096]{3,2,1,0:T(8,128)(2,1)S(1)}) fusion(bf16[16,2,16,4096]{3,2,1,0:T(8,128)(2,1)} %get-tuple-element.8), kind=kLoop, calls=%fused_computation.88 | loop fusion | bytes 8388608 | tf_op jit(solution)/shard_map/slice | solution.py:463
  87.1 2.5 %collective-permute-start.2 = (bf16[256,64]{0,1:T(8,128)(2,1)S(1)}, bf16[256,64]{0,1:T(8,128)(2,1)S(1)}, u32[]{:S(2)}, u32[]{:S(2)}) collective-permute-start(bf16[256,64]{0,1:T(8,128)(2,1)S(1)} %convolution_convert_fusion.2), channel_id=1, source_target_pairs={{0,3},{1,0},{2,1},{3,2},{4,7},{5,4},{6,5},{7,6},{8,11},{9,8},{10,9... | collective-permute-start | bytes 98312 | tf_op jit(solution)/shard_map/ppermute | solution.py:475
  89.6 3.7 %collective-permute-start.1 = (bf16[256,64]{0,1:T(8,128)(2,1)S(1)}, bf16[256,64]{0,1:T(8,128)(2,1)S(1)}, u32[]{:S(2)}, u32[]{:S(2)}) collective-permute-start(bf16[256,64]{0,1:T(8,128)(2,1)S(1)} %convolution_convert_fusion.2), channel_id=1, source_target_pairs={{0,2},{1,3},{2,0},{3,1},{4,6},{5,7},{6,4},{7,5},{8,10},{9,11},{10,... | collective-permute-start | bytes 98312 | tf_op jit(solution)/shard_map/ppermute | solution.py:475
  93.3 2.5 %collective-permute-start = (bf16[256,64]{0,1:T(8,128)(2,1)S(1)}, bf16[256,64]{0,1:T(8,128)(2,1)S(1)}, u32[]{:S(2)}, u32[]{:S(2)}) collective-permute-start(bf16[256,64]{0,1:T(8,128)(2,1)S(1)} %convolution_convert_fusion.2), channel_id=1, source_target_pairs={{0,1},{1,2},{2,3},{3,0},{4,5},{5,6},{6,7},{7,4},{8,9},{9,10},{10,1... | collective-permute-start | bytes 98312 | tf_op jit(solution)/shard_map/ppermute | solution.py:475
  95.8 1.0 fusion.17
  96.8 1.9 %fusion.20 = bf16[256,256]{0,1:T(8,128)(2,1)S(1)} fusion(bf16[256,4096]{1,0:T(8,128)(2,1)S(1)} %bitcast.95, bf16[4096,576]{1,0:T(8,128)(2,1)S(1)} %bitcast.94), kind=kOutput, calls=%fused_computation.25 | convolution fusion | flops 536936448 | bytes 4325376 | tf_op jit(solution)/shard_map/dot_general | solution.py:481
  100.6 1.1 fusion.53
  101.8 1.3 convolution_bitcast_fusion.1
  103.1 1.6 convolution_convert_fusion.1
  104.6 1.5 convolution_bitcast_fusion.2
  106.2 4.1 %collective-permute-start.5 = (bf16[256,64]{0,1:T(8,128)(2,1)S(1)}, bf16[256,64]{0,1:T(8,128)(2,1)S(1)}, u32[]{:S(2)}, u32[]{:S(2)}) collective-permute-start(bf16[256,64]{0,1:T(8,128)(2,1)S(1)} %get-tuple-element.32), channel_id=1, source_target_pairs={{0,3},{1,0},{2,1},{3,2},{4,7},{5,4},{6,5},{7,6},{8,11},{9,8},{10,9... | collective-permute-start | bytes 98312 | tf_op jit(solution)/shard_map/ppermute | solution.py:510
  110.3 1.9 %collective-permute-start.4 = (bf16[256,64]{0,1:T(8,128)(2,1)S(1)}, bf16[256,64]{0,1:T(8,128)(2,1)S(1)}, u32[]{:S(2)}, u32[]{:S(2)}) collective-permute-start(bf16[256,64]{0,1:T(8,128)(2,1)S(1)} %get-tuple-element.33), channel_id=1, source_target_pairs={{0,2},{1,3},{2,0},{3,1},{4,6},{5,7},{6,4},{7,5},{8,10},{9,11},{10,... | collective-permute-start | bytes 98312 | tf_op jit(solution)/shard_map/ppermute | solution.py:510
  112.2 2.2 %collective-permute-start.3 = (bf16[256,64]{0,1:T(8,128)(2,1)S(1)}, bf16[256,64]{0,1:T(8,128)(2,1)S(1)}, u32[]{:S(2)}, u32[]{:S(2)}) collective-permute-start(bf16[256,64]{0,1:T(8,128)(2,1)S(1)} %get-tuple-element.31), channel_id=1, source_target_pairs={{0,1},{1,2},{2,3},{3,0},{4,5},{5,6},{6,7},{7,4},{8,9},{9,10},{10,1... | collective-permute-start | bytes 98312 | tf_op jit(solution)/shard_map/ppermute | solution.py:510
  114.4 2.4 %fusion.5 = f32[256,4096]{1,0:T(8,128)S(1)} fusion(bf16[256,256]{0,1:T(8,128)(2,1)S(1)} %bitcast.99, bf16[4096,576]{1,0:T(8,128)(2,1)} %bitcast.90), kind=kOutput, calls=%fused_computation.9 | convolution fusion | flops 536870912 | bytes 6422528 | tf_op jit(solution)/shard_map/dot_general | solution.py:515
  116.8 1.9 %collective-permute-done.3 = bf16[256,64]{0,1:T(8,128)(2,1)S(1)} collective-permute-done((bf16[256,64]{0,1:T(8,128)(2,1)S(1)}, bf16[256,64]{0,1:T(8,128)(2,1)S(1)}, u32[]{:S(2)}, u32[]{:S(2)}) %collective-permute-start.3) | collective-permute-done | bytes 32800 | tf_op jit(solution)/shard_map/ppermute | solution.py:510
  118.7 2.4 %convolution_convert_fusion.g_ref = bf16[320,4096]{1,0:T(8,128)(2,1)} fusion(bf16[256,4096]{1,0:T(8,128)(2,1)S(1)} %bitcast.88, bf16[256,64]{0,1:T(8,128)(2,1)S(1)} %fusion.40, bf16[256,256]{0,1:T(8,128)(2,1)S(1)} %bitcast.100), kind=kOutput, calls=%fused_computation.4 | convolution fusion | flops 672727040 | bytes 4882432 | tf_op jit(solution)/shard_map/dot_general | solution.py:521
  121.1 3.4 %fusion.2 = bf16[256,4096]{1,0:T(8,128)(2,1)} fusion(f32[256,4096]{1,0:T(8,128)S(1)} %fusion.5, bf16[256,64]{0,1:T(8,128)(2,1)S(1)} %fusion.40, bf16[4096,576]{1,0:T(8,128)(2,1)} %bitcast.91), kind=kOutput, calls=%fused_computation.5 | convolution fusion | flops 136314880 | bytes 7372800 | tf_op jit(solution)/shard_map/dot_general | solution.py:518
  124.5 44.8 %shard_map.95 = (f32[16,4096]{1,0:T(8,128)}, bf16[16,320,128]{2,1,0:T(8,128)(2,1)}) custom-call(bf16[16,16,4096]{2,1,0:T(8,128)(2,1)} %bitcast.89, bf16[320,4096]{1,0:T(8,128)(2,1)} %convolution_convert_fusion.g_ref), custom_call_target="tpu_custom_call" | custom-call | flops 4194304 | bytes 9437184 | tf_op jit(solution)/shard_map/pallas_call | solution.py:414
  169.3 1.6 convert_reduce_fusion
  (40 shorter events, 8.5 us)
Async XLA Ops:
  82.5 3.8 %copy-start = (bf16[32,128,576]{2,1,0:T(8,128)(2,1)S(1)}, bf16[32,128,576]{2,1,0:T(8,128)(2,1)}, u32[]{:S(2)}) copy-start(bf16[32,128,576]{2,1,0:T(8,128)(2,1)} %get-tuple-element.9) | copy-start | bytes 14155780
  87.1 12.1 %collective-permute-start.2 = (bf16[256,64]{0,1:T(8,128)(2,1)S(1)}, bf16[256,64]{0,1:T(8,128)(2,1)S(1)}, u32[]{:S(2)}, u32[]{:S(2)}) collective-permute-start(bf16[256,64]{0,1:T(8,128)(2,1)S(1)} %convolution_convert_fusion.2), channel_id=1, source_target_pairs={{0,3},{1,0},{2,1},{3,2},{4,7},{5,4},{6,5},{7,6},{8,11},{9,8},{10,9... | collective-permute-start | bytes 98312 | tf_op jit(solution)/shard_map/ppermute | solution.py:475
  89.6 9.6 %collective-permute-start.1 = (bf16[256,64]{0,1:T(8,128)(2,1)S(1)}, bf16[256,64]{0,1:T(8,128)(2,1)S(1)}, u32[]{:S(2)}, u32[]{:S(2)}) collective-permute-start(bf16[256,64]{0,1:T(8,128)(2,1)S(1)} %convolution_convert_fusion.2), channel_id=1, source_target_pairs={{0,2},{1,3},{2,0},{3,1},{4,6},{5,7},{6,4},{7,5},{8,10},{9,11},{10,... | collective-permute-start | bytes 98312 | tf_op jit(solution)/shard_map/ppermute | solution.py:475
  93.3 6.5 %collective-permute-start = (bf16[256,64]{0,1:T(8,128)(2,1)S(1)}, bf16[256,64]{0,1:T(8,128)(2,1)S(1)}, u32[]{:S(2)}, u32[]{:S(2)}) collective-permute-start(bf16[256,64]{0,1:T(8,128)(2,1)S(1)} %convolution_convert_fusion.2), channel_id=1, source_target_pairs={{0,1},{1,2},{2,3},{3,0},{4,5},{5,6},{6,7},{7,4},{8,9},{9,10},{10,1... | collective-permute-start | bytes 98312 | tf_op jit(solution)/shard_map/ppermute | solution.py:475
  96.8 1.9 %copy-start.4 = (s32[1,4]{1,0:T(1,128)S(1)}, s32[1,4]{1,0:T(1,128)}, u32[]{:S(2)}) copy-start(s32[1,4]{1,0:T(1,128)} %param.15) | copy-start | bytes 52
  106.2 10.6 %collective-permute-start.5 = (bf16[256,64]{0,1:T(8,128)(2,1)S(1)}, bf16[256,64]{0,1:T(8,128)(2,1)S(1)}, u32[]{:S(2)}, u32[]{:S(2)}) collective-permute-start(bf16[256,64]{0,1:T(8,128)(2,1)S(1)} %get-tuple-element.32), channel_id=1, source_target_pairs={{0,3},{1,0},{2,1},{3,2},{4,7},{5,4},{6,5},{7,6},{8,11},{9,8},{10,9... | collective-permute-start | bytes 98312 | tf_op jit(solution)/shard_map/ppermute | solution.py:510
  110.3 6.5 %collective-permute-start.4 = (bf16[256,64]{0,1:T(8,128)(2,1)S(1)}, bf16[256,64]{0,1:T(8,128)(2,1)S(1)}, u32[]{:S(2)}, u32[]{:S(2)}) collective-permute-start(bf16[256,64]{0,1:T(8,128)(2,1)S(1)} %get-tuple-element.33), channel_id=1, source_target_pairs={{0,2},{1,3},{2,0},{3,1},{4,6},{5,7},{6,4},{7,5},{8,10},{9,11},{10,... | collective-permute-start | bytes 98312 | tf_op jit(solution)/shard_map/ppermute | solution.py:510
  112.2 6.5 %collective-permute-start.3 = (bf16[256,64]{0,1:T(8,128)(2,1)S(1)}, bf16[256,64]{0,1:T(8,128)(2,1)S(1)}, u32[]{:S(2)}, u32[]{:S(2)}) collective-permute-start(bf16[256,64]{0,1:T(8,128)(2,1)S(1)} %get-tuple-element.31), channel_id=1, source_target_pairs={{0,1},{1,2},{2,3},{3,0},{4,5},{5,6},{6,7},{7,4},{8,9},{9,10},{10,1... | collective-permute-start | bytes 98312 | tf_op jit(solution)/shard_map/ppermute | solution.py:510
  169.2 2.3 %copy-start.1 = (bf16[16,4096]{1,0:T(8,128)(2,1)S(1)}, bf16[16,4096]{1,0:T(8,128)(2,1)}, u32[]{:S(2)}) copy-start(bf16[16,4096]{1,0:T(8,128)(2,1)} %param.9) | copy-start | bytes 393220
  169.3 2.2 %copy-start.2 = (f32[16,4096]{1,0:T(8,128)S(1)}, f32[16,4096]{1,0:T(8,128)}, u32[]{:S(2)}) copy-start(f32[16,4096]{1,0:T(8,128)} %get-tuple-element.10) | copy-start | bytes 786436
  169.3 2.5 %copy-start.3 = (bf16[16,4096]{1,0:T(8,128)(2,1)S(1)}, bf16[16,4096]{1,0:T(8,128)(2,1)}, u32[]{:S(2)}) copy-start(bf16[16,4096]{1,0:T(8,128)(2,1)} %param.14) | copy-start | bytes 393220

commit v12 on v10

--- a/solution.py
+++ b/solution.py
@@ -167,10 +167,16 @@
     own_t.start()
     own_d = pltpu.make_async_copy(weights_ref, dp_out.at[r], local_sem.at[1])
     own_d.start()
+    moving = {}
+    for k, (axis, out, own, pos, bases, stride, n, send, recv) in enumerate(rings):
+        for d, target in enumerate(neighbours(pos, bases, stride, n)):
+            first = remote(own, out.at[bases[0] + pos * stride], send.at[d, 0, 0], recv.at[d, 0, 0],
+                           {axis: target})
+            waits.append(first)
+            moving[k, d] = [first]
     t_crossed.wait()
     d_crossed.wait()
     forward(dp_out.at[d_far], d_far)
-    moving = {}
     for s in range(max(ring, d_ring) // 2):
         for k, (axis, out, own, pos, bases, stride, n, send, recv) in enumerate(rings):
             right, left = neighbours(pos, bases, stride, n)
@@ -186,13 +192,14 @@
                         for start in bases:
                             slot = start + origin * stride
                             forward(out.at[slot], slot)
-                sent = []
+                sent = list(moving[k, d]) if s == 0 else []
                 for h, start in enumerate(bases):
+                    if s == 0 and h == 0:
+                        continue
                     slot = start + origin * stride
-                    src = own if (s == 0 and h == 0) else out.at[slot]
-                    sent.append(remote(src, out.at[slot], send.at[d, s, h], recv.at[d, s, h],
-                                       {axis: target}))
-                waits.extend(sent)
+                    sent.append(remote(out.at[slot], out.at[slot], send.at[d, s, h],
+                                       recv.at[d, s, h], {axis: target}))
+                    waits.append(sent[-1])
                 moving[k, d] = sent
     for k, (axis, out, own, pos, bases, stride, n, send, recv) in enumerate(rings):
         steps = (n // 2, n - 1 - n // 2)

time: 171 us -> 166 us (0.971)
  Pallas kernels: 118 us -> 113 us
    pallas_call x1, Pallas kernels: 74.1 us -> 68.5 us  [gather_start(): pl.pallas_call(functools.partial(_gather_start_body, ring), out_shape=[ja...]
where the time goes in v12:
time: 166 us; the launch traced here: 165 us
  Pallas kernels  113 us (68%)
  matrix products  15.7 us (9%)
  waiting for transfers between devices  9.86 us (6%)
  starting transfers between devices  9.17 us (6%)
  other arithmetic  9.06 us (5%)
  local copies, waits for them, and re-layouts  7.72 us (5%)
    pallas_call x1, Pallas kernels, gather_start(): pl.pallas_call(functools.partial(_gather_start_body, ring), out_shape=[ja...  68.5 us
    pallas_call x1, Pallas kernels, end_exchange(): pl.pallas_call(functools.partial(_end_body, ring), out_shape=[jax.ShapeDt...  44.2 us
    ppermute x4, waiting for transfers between devices, partner_2(): return lax.ppermute(value, axis, pairs)  9.86 us
    ppermute x4, starting transfers between devices, partner_2(): return lax.ppermute(value, axis, pairs)  9.17 us
    unnamed x15, local copies, waits for them, and re-layouts  4.34 us
    dot_general x1, matrix products, local(): lax.dot_general(kv_grad, kv_local, contract_last, preferred_element_type=...  3.37 us
  transfers between devices with their start and end apart: 4, of which 3 were waited for; matrix products, arithmetic and copies ran while one was open for 4% of the time, Pallas kernels for 0%

profile of v12, /device:TPU:1, one launch (start us, length us, event | category | flops | bytes accessed | tf_op | source)
XLA Modules:
  0.0 165.0 jit_solution(3810080772238037757)
XLA Ops:
  1.3 1.0 fusion.29
  2.4 0.9 copy.20
  3.3 0.8 copy.21
  4.2 1.0 fusion.37
  5.2 1.6 pad_maximum_fusion.pieces_ref
  6.8 1.6 pad_maximum_fusion.1.weights_ref
  8.4 68.5 %shard_map.94 = (bf16[16,2,16,4096]{3,2,1,0:T(8,128)(2,1)}, bf16[32,128,576]{2,1,0:T(8,128)(2,1)}) custom-call(bf16[2,16,4096]{2,1,0:T(8,128)(2,1)} %pad_maximum_fusion.pieces_ref, bf16[128,576]{1,0:T(8,128)(2,1)} %pad_maximum_fusion.1.weights_ref), custom_call_target="tpu_custom_call" | custom-call | bytes 17825792 | tf_op jit(solution)/shard_map/pallas_call | solution.py:227
  76.9 2.7 %fusion.55 = (bf16[16,1,16,4096]{3,2,1,0:T(8,128)(2,1)S(1)}, bf16[16,1,16,4096]{3,2,1,0:T(8,128)(2,1)S(1)}) fusion(bf16[16,2,16,4096]{3,2,1,0:T(8,128)(2,1)} %get-tuple-element.7), kind=kLoop, calls=%fused_computation.77 | loop fusion | bytes 8388608 | tf_op jit(solution)/shard_map/slice | solution.py:466
  79.7 1.0 copy-done
  81.4 3.1 %collective-permute-start = (bf16[256,64]{0,1:T(8,128)(2,1)S(1)}, bf16[256,64]{0,1:T(8,128)(2,1)S(1)}, u32[]{:S(2)}, u32[]{:S(2)}) collective-permute-start(bf16[256,64]{0,1:T(8,128)(2,1)S(1)} %convolution_convert_fusion.2), channel_id=1, source_target_pairs={{0,1},{1,0},{2,3},{3,2},{4,5},{5,4},{6,7},{7,6},{8,9},{9,8},{10,11... | collective-permute-start | bytes 98312 | tf_op jit(solution)/shard_map/ppermute | solution.py:23
  84.5 1.0 fusion.17
  85.6 1.9 %fusion.20 = bf16[256,256]{0,1:T(8,128)(2,1)S(1)} fusion(bf16[256,4096]{1,0:T(8,128)(2,1)S(1)} %bitcast.67, bf16[4096,576]{1,0:T(8,128)(2,1)S(1)} %bitcast.66), kind=kOutput, calls=%fused_computation.24 | convolution fusion | flops 536936448 | bytes 4325376 | tf_op jit(solution)/shard_map/dot_general | solution.py:487
  87.7 2.2 %collective-permute-start.1 = (bf16[256,128]{0,1:T(8,128)(2,1)S(1)}, bf16[256,128]{0,1:T(8,128)(2,1)S(1)}, u32[]{:S(2)}, u32[]{:S(2)}) collective-permute-start(bf16[256,128]{0,1:T(8,128)(2,1)S(1)} %pad_maximum_fusion.2), channel_id=1, source_target_pairs={{0,2},{1,3},{2,0},{3,1},{4,6},{5,7},{6,4},{7,5},{8,10},{9,11},{10,... | collective-permute-start | bytes 196616 | tf_op jit(solution)/shard_map/ppermute | solution.py:23
  90.1 5.7 %collective-permute-done.1 = bf16[256,128]{0,1:T(8,128)(2,1)S(1)} collective-permute-done((bf16[256,128]{0,1:T(8,128)(2,1)S(1)}, bf16[256,128]{0,1:T(8,128)(2,1)S(1)}, u32[]{:S(2)}, u32[]{:S(2)}) %collective-permute-start.1) | collective-permute-done | bytes 65568 | tf_op jit(solution)/shard_map/ppermute | solution.py:23
  97.5 1.6 select_convert_fusion
  99.1 1.9 %collective-permute-start.2 = (bf16[256,128]{0,1:T(8,128)(2,1)S(1)}, bf16[256,128]{0,1:T(8,128)(2,1)S(1)}, u32[]{:S(2)}, u32[]{:S(2)}) collective-permute-start(bf16[256,128]{0,1:T(8,128)(2,1)S(1)} %get-tuple-element.23), channel_id=1, source_target_pairs={{0,2},{1,3},{2,0},{3,1},{4,6},{5,7},{6,4},{7,5},{8,10},{9,11},{10,... | collective-permute-start | bytes 196616 | tf_op jit(solution)/shard_map/ppermute | solution.py:23
  101.0 1.6 convolution_convert_fusion.1
  102.6 3.7 %collective-permute-done.2 = bf16[256,128]{0,1:T(8,128)(2,1)S(1)} collective-permute-done((bf16[256,128]{0,1:T(8,128)(2,1)S(1)}, bf16[256,128]{0,1:T(8,128)(2,1)S(1)}, u32[]{:S(2)}, u32[]{:S(2)}) %collective-permute-start.2) | collective-permute-done | bytes 65568 | tf_op jit(solution)/shard_map/ppermute | solution.py:23
  106.3 1.9 %collective-permute-start.3 = (bf16[256,64]{0,1:T(8,128)(2,1)S(1)}, bf16[256,64]{0,1:T(8,128)(2,1)S(1)}, u32[]{:S(2)}, u32[]{:S(2)}) collective-permute-start(bf16[256,64]{0,1:T(8,128)(2,1)S(1)} %select_convert_fusion.1), channel_id=1, source_target_pairs={{0,1},{1,0},{2,3},{3,2},{4,5},{5,4},{6,7},{7,6},{8,9},{9,8},{10,11... | collective-permute-start | bytes 98312 | tf_op jit(solution)/shard_map/ppermute | solution.py:23
  108.3 2.3 %fusion.5 = f32[256,4096]{1,0:T(8,128)S(1)} fusion(bf16[256,256]{0,1:T(8,128)(2,1)S(1)} %bitcast.69, bf16[4096,576]{1,0:T(8,128)(2,1)} %bitcast.62), kind=kOutput, calls=%fused_computation.8 | convolution fusion | flops 536870912 | bytes 6422528 | tf_op jit(solution)/shard_map/dot_general | solution.py:523
  111.0 2.4 %convolution_convert_fusion.g_ref = bf16[320,4096]{1,0:T(8,128)(2,1)} fusion(bf16[256,4096]{1,0:T(8,128)(2,1)S(1)} %bitcast.60, bf16[256,64]{0,1:T(8,128)(2,1)S(1)} %add_convert_fusion.1, bf16[256,256]{0,1:T(8,128)(2,1)S(1)} %bitcast.70), kind=kOutput, calls=%fused_computation.3 | convolution fusion | flops 672727040 | bytes 4882432 | tf_op jit(solution)/shard_map/dot_general | solution.py:529
  113.4 3.4 %fusion.2 = bf16[256,4096]{1,0:T(8,128)(2,1)} fusion(f32[256,4096]{1,0:T(8,128)S(1)} %fusion.5, bf16[256,64]{0,1:T(8,128)(2,1)S(1)} %add_convert_fusion.1, bf16[4096,576]{1,0:T(8,128)(2,1)} %bitcast.63), kind=kOutput, calls=%fused_computation.4 | convolution fusion | flops 136314880 | bytes 7372800 | tf_op jit(solution)/shard_map/dot_general | solution.py:526
  116.8 44.2 %shard_map.95 = (f32[16,4096]{1,0:T(8,128)}, bf16[16,320,128]{2,1,0:T(8,128)(2,1)}) custom-call(bf16[16,16,4096]{2,1,0:T(8,128)(2,1)} %bitcast.61, bf16[320,4096]{1,0:T(8,128)(2,1)} %convolution_convert_fusion.g_ref), custom_call_target="tpu_custom_call" | custom-call | flops 4194304 | bytes 9437184 | tf_op jit(solution)/shard_map/pallas_call | solution.py:417
  161.0 1.6 convert_reduce_fusion
  (35 shorter events, 6.4 us)
Async XLA Ops:
  76.9 3.8 %copy-start = (bf16[32,128,576]{2,1,0:T(8,128)(2,1)S(1)}, bf16[32,128,576]{2,1,0:T(8,128)(2,1)}, u32[]{:S(2)}) copy-start(bf16[32,128,576]{2,1,0:T(8,128)(2,1)} %get-tuple-element.8) | copy-start | bytes 14155780
  81.4 6.3 %collective-permute-start = (bf16[256,64]{0,1:T(8,128)(2,1)S(1)}, bf16[256,64]{0,1:T(8,128)(2,1)S(1)}, u32[]{:S(2)}, u32[]{:S(2)}) collective-permute-start(bf16[256,64]{0,1:T(8,128)(2,1)S(1)} %convolution_convert_fusion.2), channel_id=1, source_target_pairs={{0,1},{1,0},{2,3},{3,2},{4,5},{5,4},{6,7},{7,6},{8,9},{9,8},{10,11... | collective-permute-start | bytes 98312 | tf_op jit(solution)/shard_map/ppermute | solution.py:23
  85.6 1.9 %copy-start.4 = (s32[1,4]{1,0:T(1,128)S(1)}, s32[1,4]{1,0:T(1,128)}, u32[]{:S(2)}) copy-start(s32[1,4]{1,0:T(1,128)} %param.13) | copy-start | bytes 52
  87.7 8.1 %collective-permute-start.1 = (bf16[256,128]{0,1:T(8,128)(2,1)S(1)}, bf16[256,128]{0,1:T(8,128)(2,1)S(1)}, u32[]{:S(2)}, u32[]{:S(2)}) collective-permute-start(bf16[256,128]{0,1:T(8,128)(2,1)S(1)} %pad_maximum_fusion.2), channel_id=1, source_target_pairs={{0,2},{1,3},{2,0},{3,1},{4,6},{5,7},{6,4},{7,5},{8,10},{9,11},{10,... | collective-permute-start | bytes 196616 | tf_op jit(solution)/shard_map/ppermute | solution.py:23
  96.2 0.8 copy-start.5
  99.1 7.2 %collective-permute-start.2 = (bf16[256,128]{0,1:T(8,128)(2,1)S(1)}, bf16[256,128]{0,1:T(8,128)(2,1)S(1)}, u32[]{:S(2)}, u32[]{:S(2)}) collective-permute-start(bf16[256,128]{0,1:T(8,128)(2,1)S(1)} %get-tuple-element.23), channel_id=1, source_target_pairs={{0,2},{1,3},{2,0},{3,1},{4,6},{5,7},{6,4},{7,5},{8,10},{9,11},{10,... | collective-permute-start | bytes 196616 | tf_op jit(solution)/shard_map/ppermute | solution.py:23
  106.3 4.7 %collective-permute-start.3 = (bf16[256,64]{0,1:T(8,128)(2,1)S(1)}, bf16[256,64]{0,1:T(8,128)(2,1)S(1)}, u32[]{:S(2)}, u32[]{:S(2)}) collective-permute-start(bf16[256,64]{0,1:T(8,128)(2,1)S(1)} %select_convert_fusion.1), channel_id=1, source_target_pairs={{0,1},{1,0},{2,3},{3,2},{4,5},{5,4},{6,7},{7,6},{8,9},{9,8},{10,11... | collective-permute-start | bytes 98312 | tf_op jit(solution)/shard_map/ppermute | solution.py:23
  161.0 2.3 %copy-start.1 = (bf16[16,4096]{1,0:T(8,128)(2,1)S(1)}, bf16[16,4096]{1,0:T(8,128)(2,1)}, u32[]{:S(2)}) copy-start(bf16[16,4096]{1,0:T(8,128)(2,1)} %param.7) | copy-start | bytes 393220
  161.0 2.2 %copy-start.2 = (f32[16,4096]{1,0:T(8,128)S(1)}, f32[16,4096]{1,0:T(8,128)}, u32[]{:S(2)}) copy-start(f32[16,4096]{1,0:T(8,128)} %get-tuple-element.9) | copy-start | bytes 786436
  161.0 2.5 %copy-start.3 = (bf16[16,4096]{1,0:T(8,128)(2,1)S(1)}, bf16[16,4096]{1,0:T(8,128)(2,1)}, u32[]{:S(2)}) copy-start(bf16[16,4096]{1,0:T(8,128)(2,1)} %param.12) | copy-start | bytes 393220

commit v13 on v12

--- a/solution.py
+++ b/solution.py
@@ -155,9 +155,13 @@
     waits = []
     forwarded = [0]
 
-    def forward(src, slot):
+    halves = []
+
+    def forward(src, slot, dst=None):
         f = forwarded[0]
-        waits.append(remote(src, dp_out.at[slot], pair_send.at[f], pair_recv.at[f], {"dp": pair}))
+        waits.append(remote(src, dst if dst is not None else dp_out.at[slot], pair_send.at[f],
+                            pair_recv.at[f], {"dp": pair}))
+        halves.append(dst is not None)
         forwarded[0] = f + 1
 
     forward(weights_ref, r)
@@ -177,12 +181,20 @@
     t_crossed.wait()
     d_crossed.wait()
     forward(dp_out.at[d_far], d_far)
+    sizes = [None] * 2
+
+    def part(ref, d, last):
+        if not last:
+            return ref
+        rows = ref.shape[0] // 2
+        return ref.at[pl.ds(d * rows, rows)]
+
     for s in range(max(ring, d_ring) // 2):
         for k, (axis, out, own, pos, bases, stride, n, send, recv) in enumerate(rings):
             right, left = neighbours(pos, bases, stride, n)
-            steps = (n // 2, n - 1 - n // 2)
+            steps = n // 2
             for d, (target, sign) in enumerate(((right, -1), (left, 1))):
-                if s >= steps[d]:
+                if s >= steps:
                     continue
                 origin = lax.rem(pos + sign * s + n, n)
                 if s > 0:
@@ -192,29 +204,35 @@
                         for start in bases:
                             slot = start + origin * stride
                             forward(out.at[slot], slot)
+                last = s == steps - 1
                 sent = list(moving[k, d]) if s == 0 else []
                 for h, start in enumerate(bases):
                     if s == 0 and h == 0:
                         continue
                     slot = start + origin * stride
-                    sent.append(remote(out.at[slot], out.at[slot], send.at[d, s, h],
-                                       recv.at[d, s, h], {axis: target}))
+                    piece = part(out.at[slot], d, last)
+                    sent.append(remote(piece, piece, send.at[d, s, h], recv.at[d, s, h],
+                                       {axis: target}))
                     waits.append(sent[-1])
                 moving[k, d] = sent
     for k, (axis, out, own, pos, bases, stride, n, send, recv) in enumerate(rings):
-        steps = (n // 2, n - 1 - n // 2)
+        steps = n // 2
         for d, sign in enumerate((-1, 1)):
             for copy in moving[k, d]:
                 copy.wait_recv()
             if k == 1:
-                origin = lax.rem(pos + sign * steps[d] + n, n)
+                origin = lax.rem(pos + sign * steps + n, n)
                 for start in bases:
                     slot = start + origin * stride
-                    forward(out.at[slot], slot)
+                    piece = part(out.at[slot], d, True)
+                    forward(piece, slot, piece)
     for copy in waits:
         copy.wait_send()
     for f in range(forwarded[0]):
-        pltpu.make_async_copy(dp_out.at[0], dp_out.at[0], pair_recv.at[f]).wait()
+        probe = dp_out.at[0]
+        if halves[f]:
+            probe = probe.at[pl.ds(0, probe.shape[0] // 2)]
+        pltpu.make_async_copy(probe, probe, pair_recv.at[f]).wait()
     own_t.wait()
     own_d.wait()
 
@@ -239,8 +257,8 @@
             pltpu.SemaphoreType.DMA((2, d_ring // 2, 2)),
             pltpu.SemaphoreType.DMA((2, d_ring // 2, 2)),
             pltpu.SemaphoreType.DMA((2,)),
-            pltpu.SemaphoreType.DMA((2 * d_ring,)),
-            pltpu.SemaphoreType.DMA((2 * d_ring,)),
+            pltpu.SemaphoreType.DMA((2 * d_ring + 2,)),
+            pltpu.SemaphoreType.DMA((2 * d_ring + 2,)),
             pltpu.SemaphoreType.DMA((2,)),
         ],
         compiler_params=pltpu.CompilerParams(collective_id=0, has_side_effects=True),

time: 166 us -> 162 us (0.976)
  waiting for transfers between devices: 9.86 us -> 4.05 us
  starting transfers between devices: 9.17 us -> 11.8 us
    ppermute x4, waiting for transfers between devices: 9.86 us -> 4.05 us  [partner_2(): return lax.ppermute(value, axis, pairs)]
    pallas_call x1, Pallas kernels: 68.5 us -> 64.8 us  [gather_start(): pl.pallas_call(functools.partial(_gather_start_body, ring), out_shape=[ja...]
    pallas_call x1, Pallas kernels: 44.2 us -> 47 us  [end_exchange(): pl.pallas_call(functools.partial(_end_body, ring), out_shape=[jax.ShapeDt...]
    ppermute x4, starting transfers between devices: 9.17 us -> 11.8 us  [partner_2(): return lax.ppermute(value, axis, pairs)]
  transfers between devices with their start and end apart: 4 -> 4, of which waited for: 3 -> 2; matrix products, arithmetic and copies ran while one was open for 4% -> 4% of each run, Pallas kernels for 0% -> 0%
where the time goes in v13:
time: 162 us; the launch traced here: 161 us
  Pallas kernels  112 us (69%)
  matrix products  15.7 us (10%)
  starting transfers between devices  11.8 us (7%)
  other arithmetic  9.07 us (6%)
  local copies, waits for them, and re-layouts  7.72 us (5%)
  waiting for transfers between devices  4.05 us (2%)
    pallas_call x1, Pallas kernels, gather_start(): pl.pallas_call(functools.partial(_gather_start_body, ring), out_shape=[ja...  64.8 us
    pallas_call x1, Pallas kernels, end_exchange(): pl.pallas_call(functools.partial(_end_body, ring), out_shape=[jax.ShapeDt...  47 us
    ppermute x4, starting transfers between devices, partner_2(): return lax.ppermute(value, axis, pairs)  11.8 us
    unnamed x15, local copies, waits for them, and re-layouts  4.34 us
    ppermute x4, waiting for transfers between devices, partner_2(): return lax.ppermute(value, axis, pairs)  4.05 us
    dot_general x1, matrix products, local(): lax.dot_general(kv_grad, kv_local, contract_last, preferred_element_type=...  3.37 us
  transfers between devices with their start and end apart: 4, of which 2 were waited for; matrix products, arithmetic and copies ran while one was open for 4% of the time, Pallas kernels for 0%

profile of v13, /device:TPU:1, one launch (start us, length us, event | category | flops | bytes accessed | tf_op | source)
XLA Modules:
  0.0 161.0 jit_solution(1615186958481278799)
XLA Ops:
  1.3 1.0 fusion.29
  2.4 0.9 copy.20
  3.3 0.8 copy.21
  4.2 1.0 fusion.37
  5.2 1.6 %pad_maximum_fusion.pieces_ref = bf16[2,16,4096]{2,1,0:T(8,128)(2,1)} fusion(bf16[1,16,4096]{2,1,0:T(8,128)(2,1)} %bitcast.68, bf16[1,16,4096]{2,1,0:T(8,128)(2,1)S(1)} %fusion.37), kind=kLoop, calls=%fused_computation.36 | loop fusion | flops 131072 | bytes 524288 | tf_op jit(solution)/shard_map/stack | solution.py:481
  6.8 1.6 pad_maximum_fusion.1.weights_ref
  8.4 64.8 %shard_map.94 = (bf16[16,2,16,4096]{3,2,1,0:T(8,128)(2,1)}, bf16[32,128,576]{2,1,0:T(8,128)(2,1)}) custom-call(bf16[2,16,4096]{2,1,0:T(8,128)(2,1)} %pad_maximum_fusion.pieces_ref, bf16[128,576]{1,0:T(8,128)(2,1)} %pad_maximum_fusion.1.weights_ref), custom_call_target="tpu_custom_call" | custom-call | bytes 17825792 | tf_op jit(solution)/shard_map/pallas_call | solution.py:245
  73.2 2.7 %fusion.55 = (bf16[16,1,16,4096]{3,2,1,0:T(8,128)(2,1)S(1)}, bf16[16,1,16,4096]{3,2,1,0:T(8,128)(2,1)S(1)}) fusion(bf16[16,2,16,4096]{3,2,1,0:T(8,128)(2,1)} %get-tuple-element.7), kind=kLoop, calls=%fused_computation.77 | loop fusion | bytes 8388608 | tf_op jit(solution)/shard_map/slice | solution.py:484
  76.0 1.0 copy-done
  77.8 1.9 %collective-permute-start = (bf16[256,64]{0,1:T(8,128)(2,1)S(1)}, bf16[256,64]{0,1:T(8,128)(2,1)S(1)}, u32[]{:S(2)}, u32[]{:S(2)}) collective-permute-start(bf16[256,64]{0,1:T(8,128)(2,1)S(1)} %convolution_convert_fusion.2), channel_id=1, source_target_pairs={{0,1},{1,0},{2,3},{3,2},{4,5},{5,4},{6,7},{7,6},{8,9},{9,8},{10,11... | collective-permute-start | bytes 98312 | tf_op jit(solution)/shard_map/ppermute | solution.py:23
  79.7 1.0 fusion.17
  80.7 1.9 %fusion.20 = bf16[256,256]{0,1:T(8,128)(2,1)S(1)} fusion(bf16[256,4096]{1,0:T(8,128)(2,1)S(1)} %bitcast.67, bf16[4096,576]{1,0:T(8,128)(2,1)S(1)} %bitcast.66), kind=kOutput, calls=%fused_computation.24 | convolution fusion | flops 536936448 | bytes 4325376 | tf_op jit(solution)/shard_map/dot_general | solution.py:505
  82.9 3.0 %collective-permute-start.1 = (bf16[256,128]{0,1:T(8,128)(2,1)S(1)}, bf16[256,128]{0,1:T(8,128)(2,1)S(1)}, u32[]{:S(2)}, u32[]{:S(2)}) collective-permute-start(bf16[256,128]{0,1:T(8,128)(2,1)S(1)} %pad_maximum_fusion.2), channel_id=1, source_target_pairs={{0,2},{1,3},{2,0},{3,1},{4,6},{5,7},{6,4},{7,5},{8,10},{9,11},{10,... | collective-permute-start | bytes 196616 | tf_op jit(solution)/shard_map/ppermute | solution.py:23
  86.0 2.8 %collective-permute-done.1 = bf16[256,128]{0,1:T(8,128)(2,1)S(1)} collective-permute-done((bf16[256,128]{0,1:T(8,128)(2,1)S(1)}, bf16[256,128]{0,1:T(8,128)(2,1)S(1)}, u32[]{:S(2)}, u32[]{:S(2)}) %collective-permute-start.1) | collective-permute-done | bytes 65568 | tf_op jit(solution)/shard_map/ppermute | solution.py:23
  90.5 1.5 select_convert_fusion
  92.1 3.1 %collective-permute-start.2 = (bf16[256,128]{0,1:T(8,128)(2,1)S(1)}, bf16[256,128]{0,1:T(8,128)(2,1)S(1)}, u32[]{:S(2)}, u32[]{:S(2)}) collective-permute-start(bf16[256,128]{0,1:T(8,128)(2,1)S(1)} %get-tuple-element.23), channel_id=1, source_target_pairs={{0,2},{1,3},{2,0},{3,1},{4,6},{5,7},{6,4},{7,5},{8,10},{9,11},{10,... | collective-permute-start | bytes 196616 | tf_op jit(solution)/shard_map/ppermute | solution.py:23
  95.1 1.6 convolution_convert_fusion.1
  96.7 1.3 collective-permute-done.2
  98.0 3.8 %collective-permute-start.3 = (bf16[256,64]{0,1:T(8,128)(2,1)S(1)}, bf16[256,64]{0,1:T(8,128)(2,1)S(1)}, u32[]{:S(2)}, u32[]{:S(2)}) collective-permute-start(bf16[256,64]{0,1:T(8,128)(2,1)S(1)} %select_convert_fusion.1), channel_id=1, source_target_pairs={{0,1},{1,0},{2,3},{3,2},{4,5},{5,4},{6,7},{7,6},{8,9},{9,8},{10,11... | collective-permute-start | bytes 98312 | tf_op jit(solution)/shard_map/ppermute | solution.py:23
  101.8 2.4 %fusion.5 = f32[256,4096]{1,0:T(8,128)S(1)} fusion(bf16[256,256]{0,1:T(8,128)(2,1)S(1)} %bitcast.69, bf16[4096,576]{1,0:T(8,128)(2,1)} %bitcast.62), kind=kOutput, calls=%fused_computation.8 | convolution fusion | flops 536870912 | bytes 6422528 | tf_op jit(solution)/shard_map/dot_general | solution.py:541
  104.2 2.4 %convolution_convert_fusion.g_ref = bf16[320,4096]{1,0:T(8,128)(2,1)} fusion(bf16[256,4096]{1,0:T(8,128)(2,1)S(1)} %bitcast.60, bf16[256,64]{0,1:T(8,128)(2,1)S(1)} %add_convert_fusion.1, bf16[256,256]{0,1:T(8,128)(2,1)S(1)} %bitcast.70), kind=kOutput, calls=%fused_computation.3 | convolution fusion | flops 672727040 | bytes 4882432 | tf_op jit(solution)/shard_map/dot_general | solution.py:547
  106.6 3.4 %fusion.2 = bf16[256,4096]{1,0:T(8,128)(2,1)} fusion(f32[256,4096]{1,0:T(8,128)S(1)} %fusion.5, bf16[256,64]{0,1:T(8,128)(2,1)S(1)} %add_convert_fusion.1, bf16[4096,576]{1,0:T(8,128)(2,1)} %bitcast.63), kind=kOutput, calls=%fused_computation.4 | convolution fusion | flops 136314880 | bytes 7372800 | tf_op jit(solution)/shard_map/dot_general | solution.py:544
  109.9 47.0 %shard_map.95 = (f32[16,4096]{1,0:T(8,128)}, bf16[16,320,128]{2,1,0:T(8,128)(2,1)}) custom-call(bf16[16,16,4096]{2,1,0:T(8,128)(2,1)} %bitcast.61, bf16[320,4096]{1,0:T(8,128)(2,1)} %convolution_convert_fusion.g_ref), custom_call_target="tpu_custom_call" | custom-call | flops 4194304 | bytes 9437184 | tf_op jit(solution)/shard_map/pallas_call | solution.py:435
  156.9 1.6 convert_reduce_fusion
  (35 shorter events, 6.1 us)
Async XLA Ops:
  73.2 3.8 %copy-start = (bf16[32,128,576]{2,1,0:T(8,128)(2,1)S(1)}, bf16[32,128,576]{2,1,0:T(8,128)(2,1)}, u32[]{:S(2)}) copy-start(bf16[32,128,576]{2,1,0:T(8,128)(2,1)} %get-tuple-element.8) | copy-start | bytes 14155780
  77.8 5.1 %collective-permute-start = (bf16[256,64]{0,1:T(8,128)(2,1)S(1)}, bf16[256,64]{0,1:T(8,128)(2,1)S(1)}, u32[]{:S(2)}, u32[]{:S(2)}) collective-permute-start(bf16[256,64]{0,1:T(8,128)(2,1)S(1)} %convolution_convert_fusion.2), channel_id=1, source_target_pairs={{0,1},{1,0},{2,3},{3,2},{4,5},{5,4},{6,7},{7,6},{8,9},{9,8},{10,11... | collective-permute-start | bytes 98312 | tf_op jit(solution)/shard_map/ppermute | solution.py:23
  80.7 1.9 %copy-start.4 = (s32[1,4]{1,0:T(1,128)S(1)}, s32[1,4]{1,0:T(1,128)}, u32[]{:S(2)}) copy-start(s32[1,4]{1,0:T(1,128)} %param.13) | copy-start | bytes 52
  82.9 5.9 %collective-permute-start.1 = (bf16[256,128]{0,1:T(8,128)(2,1)S(1)}, bf16[256,128]{0,1:T(8,128)(2,1)S(1)}, u32[]{:S(2)}, u32[]{:S(2)}) collective-permute-start(bf16[256,128]{0,1:T(8,128)(2,1)S(1)} %pad_maximum_fusion.2), channel_id=1, source_target_pairs={{0,2},{1,3},{2,0},{3,1},{4,6},{5,7},{6,4},{7,5},{8,10},{9,11},{10,... | collective-permute-start | bytes 196616 | tf_op jit(solution)/shard_map/ppermute | solution.py:23
  89.2 0.8 copy-start.5
  92.1 5.9 %collective-permute-start.2 = (bf16[256,128]{0,1:T(8,128)(2,1)S(1)}, bf16[256,128]{0,1:T(8,128)(2,1)S(1)}, u32[]{:S(2)}, u32[]{:S(2)}) collective-permute-start(bf16[256,128]{0,1:T(8,128)(2,1)S(1)} %get-tuple-element.23), channel_id=1, source_target_pairs={{0,2},{1,3},{2,0},{3,1},{4,6},{5,7},{6,4},{7,5},{8,10},{9,11},{10,... | collective-permute-start | bytes 196616 | tf_op jit(solution)/shard_map/ppermute | solution.py:23
  98.0 6.2 %collective-permute-start.3 = (bf16[256,64]{0,1:T(8,128)(2,1)S(1)}, bf16[256,64]{0,1:T(8,128)(2,1)S(1)}, u32[]{:S(2)}, u32[]{:S(2)}) collective-permute-start(bf16[256,64]{0,1:T(8,128)(2,1)S(1)} %select_convert_fusion.1), channel_id=1, source_target_pairs={{0,1},{1,0},{2,3},{3,2},{4,5},{5,4},{6,7},{7,6},{8,9},{9,8},{10,11... | collective-permute-start | bytes 98312 | tf_op jit(solution)/shard_map/ppermute | solution.py:23
  156.9 2.3 %copy-start.1 = (bf16[16,4096]{1,0:T(8,128)(2,1)S(1)}, bf16[16,4096]{1,0:T(8,128)(2,1)}, u32[]{:S(2)}) copy-start(bf16[16,4096]{1,0:T(8,128)(2,1)} %param.7) | copy-start | bytes 393220
  156.9 2.2 %copy-start.2 = (f32[16,4096]{1,0:T(8,128)S(1)}, f32[16,4096]{1,0:T(8,128)}, u32[]{:S(2)}) copy-start(f32[16,4096]{1,0:T(8,128)} %get-tuple-element.9) | copy-start | bytes 786436
  156.9 2.5 %copy-start.3 = (bf16[16,4096]{1,0:T(8,128)(2,1)S(1)}, bf16[16,4096]{1,0:T(8,128)(2,1)}, u32[]{:S(2)}) copy-start(bf16[16,4096]{1,0:T(8,128)(2,1)} %param.12) | copy-start | bytes 393220

commit v14 on v13

--- a/solution.py
+++ b/solution.py
@@ -164,6 +164,13 @@
         halves.append(dst is not None)
         forwarded[0] = f + 1
 
+    moving = {}
+    for k, (axis, out, own, pos, bases, stride, n, send, recv) in enumerate(rings):
+        for d, target in enumerate(neighbours(pos, bases, stride, n)):
+            first = remote(own, out.at[bases[0] + pos * stride], send.at[d, 0, 0], recv.at[d, 0, 0],
+                           {axis: target})
+            waits.append(first)
+            moving[k, d] = [first]
     forward(weights_ref, r)
     t_crossed = remote(pieces_ref, tens_out.at[t], t_cross.at[0], t_cross.at[1], {"tensor": t_far})
     d_crossed = remote(weights_ref, dp_out.at[r], d_cross.at[0], d_cross.at[1], {"dp": d_far})
@@ -171,13 +178,6 @@
     own_t.start()
     own_d = pltpu.make_async_copy(weights_ref, dp_out.at[r], local_sem.at[1])
     own_d.start()
-    moving = {}
-    for k, (axis, out, own, pos, bases, stride, n, send, recv) in enumerate(rings):
-        for d, target in enumerate(neighbours(pos, bases, stride, n)):
-            first = remote(own, out.at[bases[0] + pos * stride], send.at[d, 0, 0], recv.at[d, 0, 0],
-                           {axis: target})
-            waits.append(first)
-            moving[k, d] = [first]
     t_crossed.wait()
     d_crossed.wait()
     forward(dp_out.at[d_far], d_far)
@@ -355,14 +355,6 @@
     waits = []
     swapped = []
     kept = []
-    for i in range(n_w):
-        give = pl.ds(pl.multiple_of((2 * i + 1 - parity) * width, width), width)
-        keep = pl.ds(pl.multiple_of((2 * i + parity) * width, width), width)
-        swapped.append(remote(g_ref.at[:, give], theirs.at[i], p_send.at[i], p_recv.at[i],
-                              {"dp": pair}))
-        own = pltpu.make_async_copy(g_ref.at[:, keep], mine.at[i], p_local.at[i])
-        own.start()
-        kept.append(own)
     steps = (ring // 2, ring - 1 - ring // 2)
     moving = [None, None]
     own_w = None
@@ -400,6 +392,15 @@
                                    t_recv.at[d, s, h], {"tensor": target}))
             waits.extend(sent)
             moving[d] = sent
+        if s == 0:
+            for i in range(n_w):
+                give = pl.ds(pl.multiple_of((2 * i + 1 - parity) * width, width), width)
+                keep = pl.ds(pl.multiple_of((2 * i + parity) * width, width), width)
+                swapped.append(remote(g_ref.at[:, give], theirs.at[i], p_send.at[i], p_recv.at[i],
+                                      {"dp": pair}))
+                own = pltpu.make_async_copy(g_ref.at[:, keep], mine.at[i], p_local.at[i])
+                own.start()
+                kept.append(own)
     for d in range(2):
         for copy in moving[d]:
             copy.wait_recv()

time: 162 us -> 162 us (level)
  no operation moved by 1% of the time
where the time goes in v14:
time: 162 us; the launch traced here: 161 us
  Pallas kernels  112 us (69%)
  matrix products  15.7 us (10%)
  starting transfers between devices  11.8 us (7%)
  other arithmetic  9.07 us (6%)
  local copies, waits for them, and re-layouts  7.72 us (5%)
  waiting for transfers between devices  4.05 us (2%)
    pallas_call x1, Pallas kernels, gather_start(): pl.pallas_call(functools.partial(_gather_start_body, ring), out_shape=[ja...  64.9 us
    pallas_call x1, Pallas kernels, end_exchange(): pl.pallas_call(functools.partial(_end_body, ring), out_shape=[jax.ShapeDt...  47 us
    ppermute x4, starting transfers between devices, partner_2(): return lax.ppermute(value, axis, pairs)  11.8 us
    unnamed x15, local copies, waits for them, and re-layouts  4.34 us
    ppermute x4, waiting for transfers between devices, partner_2(): return lax.ppermute(value, axis, pairs)  4.05 us
    dot_general x1, matrix products, local(): lax.dot_general(kv_grad, kv_local, contract_last, preferred_element_type=...  3.37 us
  transfers between devices with their start and end apart: 4, of which 2 were waited for; matrix products, arithmetic and copies ran while one was open for 4% of the time, Pallas kernels for 0%

profile of v14, /device:TPU:1, one launch (start us, length us, event | category | flops | bytes accessed | tf_op | source)
XLA Modules:
  0.0 161.0 jit_solution(8374453720518670431)
XLA Ops:
  1.3 1.0 fusion.29
  2.4 0.9 copy.20
  3.3 0.8 copy.21
  4.2 1.0 fusion.37
  5.2 1.6 %pad_maximum_fusion.pieces_ref = bf16[2,16,4096]{2,1,0:T(8,128)(2,1)} fusion(bf16[1,16,4096]{2,1,0:T(8,128)(2,1)} %bitcast.68, bf16[1,16,4096]{2,1,0:T(8,128)(2,1)S(1)} %fusion.37), kind=kLoop, calls=%fused_computation.36 | loop fusion | flops 131072 | bytes 524288 | tf_op jit(solution)/shard_map/stack | solution.py:482
  6.8 1.6 pad_maximum_fusion.1.weights_ref
  8.4 64.9 %shard_map.94 = (bf16[16,2,16,4096]{3,2,1,0:T(8,128)(2,1)}, bf16[32,128,576]{2,1,0:T(8,128)(2,1)}) custom-call(bf16[2,16,4096]{2,1,0:T(8,128)(2,1)} %pad_maximum_fusion.pieces_ref, bf16[128,576]{1,0:T(8,128)(2,1)} %pad_maximum_fusion.1.weights_ref), custom_call_target="tpu_custom_call" | custom-call | bytes 17825792 | tf_op jit(solution)/shard_map/pallas_call | solution.py:245
  73.3 2.7 %fusion.55 = (bf16[16,1,16,4096]{3,2,1,0:T(8,128)(2,1)S(1)}, bf16[16,1,16,4096]{3,2,1,0:T(8,128)(2,1)S(1)}) fusion(bf16[16,2,16,4096]{3,2,1,0:T(8,128)(2,1)} %get-tuple-element.7), kind=kLoop, calls=%fused_computation.77 | loop fusion | bytes 8388608 | tf_op jit(solution)/shard_map/slice | solution.py:485
  76.1 1.0 copy-done
  77.8 1.9 %collective-permute-start = (bf16[256,64]{0,1:T(8,128)(2,1)S(1)}, bf16[256,64]{0,1:T(8,128)(2,1)S(1)}, u32[]{:S(2)}, u32[]{:S(2)}) collective-permute-start(bf16[256,64]{0,1:T(8,128)(2,1)S(1)} %convolution_convert_fusion.2), channel_id=1, source_target_pairs={{0,1},{1,0},{2,3},{3,2},{4,5},{5,4},{6,7},{7,6},{8,9},{9,8},{10,11... | collective-permute-start | bytes 98312 | tf_op jit(solution)/shard_map/ppermute | solution.py:23
  79.8 1.0 fusion.17
  80.8 1.9 %fusion.20 = bf16[256,256]{0,1:T(8,128)(2,1)S(1)} fusion(bf16[256,4096]{1,0:T(8,128)(2,1)S(1)} %bitcast.67, bf16[4096,576]{1,0:T(8,128)(2,1)S(1)} %bitcast.66), kind=kOutput, calls=%fused_computation.24 | convolution fusion | flops 536936448 | bytes 4325376 | tf_op jit(solution)/shard_map/dot_general | solution.py:506
  83.0 3.0 %collective-permute-start.1 = (bf16[256,128]{0,1:T(8,128)(2,1)S(1)}, bf16[256,128]{0,1:T(8,128)(2,1)S(1)}, u32[]{:S(2)}, u32[]{:S(2)}) collective-permute-start(bf16[256,128]{0,1:T(8,128)(2,1)S(1)} %pad_maximum_fusion.2), channel_id=1, source_target_pairs={{0,2},{1,3},{2,0},{3,1},{4,6},{5,7},{6,4},{7,5},{8,10},{9,11},{10,... | collective-permute-start | bytes 196616 | tf_op jit(solution)/shard_map/ppermute | solution.py:23
  86.1 2.8 %collective-permute-done.1 = bf16[256,128]{0,1:T(8,128)(2,1)S(1)} collective-permute-done((bf16[256,128]{0,1:T(8,128)(2,1)S(1)}, bf16[256,128]{0,1:T(8,128)(2,1)S(1)}, u32[]{:S(2)}, u32[]{:S(2)}) %collective-permute-start.1) | collective-permute-done | bytes 65568 | tf_op jit(solution)/shard_map/ppermute | solution.py:23
  90.6 1.6 select_convert_fusion
  92.1 3.1 %collective-permute-start.2 = (bf16[256,128]{0,1:T(8,128)(2,1)S(1)}, bf16[256,128]{0,1:T(8,128)(2,1)S(1)}, u32[]{:S(2)}, u32[]{:S(2)}) collective-permute-start(bf16[256,128]{0,1:T(8,128)(2,1)S(1)} %get-tuple-element.23), channel_id=1, source_target_pairs={{0,2},{1,3},{2,0},{3,1},{4,6},{5,7},{6,4},{7,5},{8,10},{9,11},{10,... | collective-permute-start | bytes 196616 | tf_op jit(solution)/shard_map/ppermute | solution.py:23
  95.2 1.6 convolution_convert_fusion.1
  96.8 1.3 collective-permute-done.2
  98.1 3.8 %collective-permute-start.3 = (bf16[256,64]{0,1:T(8,128)(2,1)S(1)}, bf16[256,64]{0,1:T(8,128)(2,1)S(1)}, u32[]{:S(2)}, u32[]{:S(2)}) collective-permute-start(bf16[256,64]{0,1:T(8,128)(2,1)S(1)} %select_convert_fusion.1), channel_id=1, source_target_pairs={{0,1},{1,0},{2,3},{3,2},{4,5},{5,4},{6,7},{7,6},{8,9},{9,8},{10,11... | collective-permute-start | bytes 98312 | tf_op jit(solution)/shard_map/ppermute | solution.py:23
  101.9 2.4 %fusion.5 = f32[256,4096]{1,0:T(8,128)S(1)} fusion(bf16[256,256]{0,1:T(8,128)(2,1)S(1)} %bitcast.69, bf16[4096,576]{1,0:T(8,128)(2,1)} %bitcast.62), kind=kOutput, calls=%fused_computation.8 | convolution fusion | flops 536870912 | bytes 6422528 | tf_op jit(solution)/shard_map/dot_general | solution.py:542
  104.3 2.4 %convolution_convert_fusion.g_ref = bf16[320,4096]{1,0:T(8,128)(2,1)} fusion(bf16[256,4096]{1,0:T(8,128)(2,1)S(1)} %bitcast.60, bf16[256,64]{0,1:T(8,128)(2,1)S(1)} %add_convert_fusion.1, bf16[256,256]{0,1:T(8,128)(2,1)S(1)} %bitcast.70), kind=kOutput, calls=%fused_computation.3 | convolution fusion | flops 672727040 | bytes 4882432 | tf_op jit(solution)/shard_map/dot_general | solution.py:548
  106.6 3.4 %fusion.2 = bf16[256,4096]{1,0:T(8,128)(2,1)} fusion(f32[256,4096]{1,0:T(8,128)S(1)} %fusion.5, bf16[256,64]{0,1:T(8,128)(2,1)S(1)} %add_convert_fusion.1, bf16[4096,576]{1,0:T(8,128)(2,1)} %bitcast.63), kind=kOutput, calls=%fused_computation.4 | convolution fusion | flops 136314880 | bytes 7372800 | tf_op jit(solution)/shard_map/dot_general | solution.py:545
  110.0 47.0 %shard_map.95 = (f32[16,4096]{1,0:T(8,128)}, bf16[16,320,128]{2,1,0:T(8,128)(2,1)}) custom-call(bf16[16,16,4096]{2,1,0:T(8,128)(2,1)} %bitcast.61, bf16[320,4096]{1,0:T(8,128)(2,1)} %convolution_convert_fusion.g_ref), custom_call_target="tpu_custom_call" | custom-call | flops 4194304 | bytes 9437184 | tf_op jit(solution)/shard_map/pallas_call | solution.py:436
  157.0 1.6 convert_reduce_fusion
  (35 shorter events, 6.1 us)
Async XLA Ops:
  73.3 3.8 %copy-start = (bf16[32,128,576]{2,1,0:T(8,128)(2,1)S(1)}, bf16[32,128,576]{2,1,0:T(8,128)(2,1)}, u32[]{:S(2)}) copy-start(bf16[32,128,576]{2,1,0:T(8,128)(2,1)} %get-tuple-element.8) | copy-start | bytes 14155780
  77.8 5.1 %collective-permute-start = (bf16[256,64]{0,1:T(8,128)(2,1)S(1)}, bf16[256,64]{0,1:T(8,128)(2,1)S(1)}, u32[]{:S(2)}, u32[]{:S(2)}) collective-permute-start(bf16[256,64]{0,1:T(8,128)(2,1)S(1)} %convolution_convert_fusion.2), channel_id=1, source_target_pairs={{0,1},{1,0},{2,3},{3,2},{4,5},{5,4},{6,7},{7,6},{8,9},{9,8},{10,11... | collective-permute-start | bytes 98312 | tf_op jit(solution)/shard_map/ppermute | solution.py:23
  80.8 1.9 %copy-start.4 = (s32[1,4]{1,0:T(1,128)S(1)}, s32[1,4]{1,0:T(1,128)}, u32[]{:S(2)}) copy-start(s32[1,4]{1,0:T(1,128)} %param.13) | copy-start | bytes 52
  83.0 5.9 %collective-permute-start.1 = (bf16[256,128]{0,1:T(8,128)(2,1)S(1)}, bf16[256,128]{0,1:T(8,128)(2,1)S(1)}, u32[]{:S(2)}, u32[]{:S(2)}) collective-permute-start(bf16[256,128]{0,1:T(8,128)(2,1)S(1)} %pad_maximum_fusion.2), channel_id=1, source_target_pairs={{0,2},{1,3},{2,0},{3,1},{4,6},{5,7},{6,4},{7,5},{8,10},{9,11},{10,... | collective-permute-start | bytes 196616 | tf_op jit(solution)/shard_map/ppermute | solution.py:23
  89.3 0.8 copy-start.5
  92.1 5.9 %collective-permute-start.2 = (bf16[256,128]{0,1:T(8,128)(2,1)S(1)}, bf16[256,128]{0,1:T(8,128)(2,1)S(1)}, u32[]{:S(2)}, u32[]{:S(2)}) collective-permute-start(bf16[256,128]{0,1:T(8,128)(2,1)S(1)} %get-tuple-element.23), channel_id=1, source_target_pairs={{0,2},{1,3},{2,0},{3,1},{4,6},{5,7},{6,4},{7,5},{8,10},{9,11},{10,... | collective-permute-start | bytes 196616 | tf_op jit(solution)/shard_map/ppermute | solution.py:23
  98.1 6.2 %collective-permute-start.3 = (bf16[256,64]{0,1:T(8,128)(2,1)S(1)}, bf16[256,64]{0,1:T(8,128)(2,1)S(1)}, u32[]{:S(2)}, u32[]{:S(2)}) collective-permute-start(bf16[256,64]{0,1:T(8,128)(2,1)S(1)} %select_convert_fusion.1), channel_id=1, source_target_pairs={{0,1},{1,0},{2,3},{3,2},{4,5},{5,4},{6,7},{7,6},{8,9},{9,8},{10,11... | collective-permute-start | bytes 98312 | tf_op jit(solution)/shard_map/ppermute | solution.py:23
  157.0 2.3 %copy-start.1 = (bf16[16,4096]{1,0:T(8,128)(2,1)S(1)}, bf16[16,4096]{1,0:T(8,128)(2,1)}, u32[]{:S(2)}) copy-start(bf16[16,4096]{1,0:T(8,128)(2,1)} %param.7) | copy-start | bytes 393220
  157.0 2.2 %copy-start.2 = (f32[16,4096]{1,0:T(8,128)S(1)}, f32[16,4096]{1,0:T(8,128)}, u32[]{:S(2)}) copy-start(f32[16,4096]{1,0:T(8,128)} %get-tuple-element.9) | copy-start | bytes 786436
  157.0 2.5 %copy-start.3 = (bf16[16,4096]{1,0:T(8,128)(2,1)S(1)}, bf16[16,4096]{1,0:T(8,128)(2,1)}, u32[]{:S(2)}) copy-start(bf16[16,4096]{1,0:T(8,128)(2,1)} %param.12) | copy-start | bytes 393220
